TPU v7x, 32 devices: a whole 2x2x4 slice. The times are simulated.
32 devices in a mesh: dev: 32 (over z, y, x, core).
Axes of the slice: x: 2, y: 2, z: 4, core: 2. Of those that a mesh axis runs over, the one named last changes fastest.
Arguments:
- positions: float32 [3, 131072], P(None, 'dev'), may hold values from 0 to 1
- velocities: float32 [3, 131072], P(None, 'dev'), may hold values from -3 to 3
- masses: float32 [131072], P('dev'), may hold values from 0.25 to 4
- samples: float32 [3, 1048576], P(None, 'dev'), may hold values from 0 to 1
- sample_mass: float32 [1048576], P('dev'), may hold values from 0.5 to 2
- start_potential: float32 [1048576], P('dev'), may hold values from -0.1 to 2.9
- route_owner: int32 [1024, 4], P('dev'), may hold values from 0 to 31, all different within a row; in each aligned block of 32 rows (0 to 31, 32 to 63, ...) at most 8 rows name the same one
- route_tile: int32 [1024, 4], P('dev'), may hold values from 0 to 63
- live_count: int32 [1024], P('dev'), may hold values from 3 to 4
Outputs:
- new_position: float32 [3, 131072], P(None, 'dev')
- new_velocity: float32 [3, 131072], P(None, 'dev')
Inputs may be any that keep to these rules, and one draw needn't show every extreme that they name: `route_owner`: each row names 4 different devices; among the 32 rows of one device no device is named more than 8 times, and some device is named exactly 8 times.
All inputs are finite; a program needn't handle non-finite values.
Results may differ from a plain program's by a relative error of at most 0.0003.
Values sent between devices are 32-bit elements; how exact they have to be, the bound alone decides.
No kernel may reach another device: no remote copies, remote signals or barrier semaphores. Data moves between devices by JAX's collectives and lax.ppermute only.
A program may use at most 64 MiB of HBM per device.

v0:
```python
import jax
import jax.numpy as jnp
from jax import lax
from jax.sharding import PartitionSpec as P

BLK = 128
TILE = 512
K = 4
ITERS = 2


EPSILON = 0.01
STIFFNESS = 150.0
TIMESTEP = 0.05
NEGATIVE = -1e30
HIGHEST = lax.Precision.HIGHEST


def pair_costs(block_coordinates, tile_coordinates):
    first = block_coordinates[0][None, :, None] - tile_coordinates[:, 0][:, None, :]
    second = block_coordinates[1][None, :, None] - tile_coordinates[:, 1][:, None, :]
    third = block_coordinates[2][None, :, None] - tile_coordinates[:, 2][:, None, :]
    return 0.5 * (first * first + second * second + third * third)


def row_lse(score, active_mask):
    masked = jnp.where(active_mask[:, None, None], score, NEGATIVE)
    top = jnp.max(masked, axis=(0, 2))
    total = jnp.sum(jnp.exp(masked - top[None, :, None]), axis=(0, 2))
    return top + jnp.log(total)


def transport_block_update(
    block_coordinates, logarithm_masses, tile_coordinates, tile_dual_values, active_mask
):
    cost = pair_costs(block_coordinates, tile_coordinates)
    row_dual_values = EPSILON * logarithm_masses - EPSILON * row_lse(
        (tile_dual_values[:, None, :] - cost) / EPSILON, active_mask
    )
    score = (row_dual_values[None, :, None] - cost) / EPSILON
    column_peak = jnp.max(score, axis=1)
    column_total_sum = jnp.sum(jnp.exp(score - column_peak[:, None, :]), axis=1)
    return (
        row_dual_values,
        jnp.where(active_mask[:, None], column_peak, NEGATIVE),
        jnp.where(active_mask[:, None], column_total_sum, 0.0),
    )


def centre_block(block_coordinates, tile_coordinates, tile_dual_values, active_mask):
    cost = pair_costs(block_coordinates, tile_coordinates)
    masked = jnp.where(
        active_mask[:, None, None], (tile_dual_values[:, None, :] - cost) / EPSILON, NEGATIVE
    )
    top = jnp.max(masked, axis=(0, 2))
    weight = jnp.exp(masked - top[None, :, None])
    total = jnp.sum(weight, axis=(0, 2))
    numer = jnp.einsum("kij,kdj->di", weight, tile_coordinates, precision=HIGHEST)
    return numer / total[None, :]


def by_turns(func, inputs, width):
    count = inputs[0].shape[0]
    folded = tuple((item.reshape((count // width, width) + item.shape[1:]) for item in inputs))
    result = lax.map(lambda group: jax.vmap(func)(*group), folded)
    return jax.tree.map(lambda item: item.reshape((count,) + item.shape[2:]), result)


def merge_tiles(dual_variable, log_sample, asked_tile, part_top, part_sum):
    tiles_here = dual_variable.shape[0]
    top = jnp.full(dual_variable.shape, NEGATIVE, jnp.float32).at[asked_tile].max(part_top)
    scaled = part_sum * jnp.exp(part_top - top[asked_tile])
    member = (jnp.arange(tiles_here, dtype=jnp.int32)[:, None] == asked_tile[None, :]).astype(
        jnp.float32
    )
    total = jnp.dot(member, scaled, precision=HIGHEST, preferred_element_type=jnp.float32)
    covered = total > 0
    updated = EPSILON * log_sample - EPSILON * (top + jnp.log(jnp.where(covered, total, 1.0)))
    return jnp.where(covered, updated, dual_variable)


def local(
    positions,
    velocities,
    masses,
    samples,
    sample_mass,
    start_potential,
    route_owner,
    route_tile,
    live_count,
):
    devices = lax.axis_size("dev")
    blocks = route_owner.shape[0]
    tiles_here = start_potential.shape[0] // TILE
    capacity = 2 * blocks * K // devices
    buffer_len = devices * capacity
    flat_owner = route_owner.reshape(-1)
    onehot = (flat_owner[:, None] == jnp.arange(devices, dtype=jnp.int32)[None, :]).astype(
        jnp.int32
    )
    rank = jnp.sum((jnp.cumsum(onehot, axis=0) - onehot) * onehot, axis=1)
    slot_pos = flat_owner * capacity + rank
    active_mask = jnp.arange(K, dtype=jnp.int32)[None, :] < live_count[:, None]
    wanted = jnp.where(active_mask.reshape(-1), route_tile.reshape(-1), -1)
    request = jnp.full((buffer_len,), -1, jnp.int32).at[slot_pos].set(wanted)
    asked = lax.all_to_all(
        request.reshape(devices, capacity), "dev", split_axis=0, concat_axis=0, tiled=True
    ).reshape(buffer_len)
    asked_tile = jnp.maximum(asked, 0)
    block_coordinates = positions.reshape(3, blocks, BLK).transpose(1, 0, 2)
    logarithm_masses = jnp.log(masses).reshape(blocks, BLK)
    tile_coordinates = samples.reshape(3, tiles_here, TILE).transpose(1, 0, 2)
    log_sample = jnp.log(sample_mass).reshape(tiles_here, TILE)
    dual_variable = start_potential.reshape(tiles_here, TILE)

    def to_slots(values):
        inner = values.shape[2:]
        return values.reshape((buffer_len,) + inner)[slot_pos].reshape((blocks, K) + inner)

    def to_buffer(values, filler):
        inner = values.shape[2:]
        flat = values.reshape((blocks * K,) + inner)
        empty = jnp.full((buffer_len,) + inner, filler, jnp.float32)
        return empty.at[slot_pos].set(flat).reshape((devices, capacity) + inner)

    got_tiles = lax.all_to_all(
        tile_coordinates[asked_tile].reshape(devices, capacity, 3, TILE),
        "dev",
        split_axis=0,
        concat_axis=0,
        tiled=True,
    )
    distant_coordinates = to_slots(got_tiles)
    for step in range(ITERS + 1):
        got_pot = lax.all_to_all(
            dual_variable[asked_tile].reshape(devices, capacity, TILE),
            "dev",
            split_axis=0,
            concat_axis=0,
            tiled=True,
        )
        distant_dual = to_slots(got_pot)
        if step < ITERS:
            row_dual_values, column_peak, column_total_sum = by_turns(
                transport_block_update,
                (
                    block_coordinates,
                    logarithm_masses,
                    distant_coordinates,
                    distant_dual,
                    active_mask,
                ),
                2,
            )
            back_top, back_sum = (
                lax.all_to_all(
                    to_buffer(column_peak, NEGATIVE), "dev", split_axis=0, concat_axis=0, tiled=True
                ),
                lax.all_to_all(
                    to_buffer(column_total_sum, 0.0), "dev", split_axis=0, concat_axis=0, tiled=True
                ),
            )
            dual_variable = merge_tiles(
                dual_variable,
                log_sample,
                asked_tile,
                back_top.reshape(buffer_len, TILE),
                back_sum.reshape(buffer_len, TILE),
            )
        else:
            centre_rows = by_turns(
                centre_block, (block_coordinates, distant_coordinates, distant_dual, active_mask), 2
            )
    centre = centre_rows.transpose(1, 0, 2).reshape(3, blocks * BLK)
    new_velocity = velocities + STIFFNESS * (centre - positions)
    new_position = positions + TIMESTEP * new_velocity
    return (new_position, new_velocity)


def solution(mesh):
    placed = (
        P(None, "dev"),
        P(None, "dev"),
        P("dev"),
        P(None, "dev"),
        P("dev"),
        P("dev"),
        P("dev", None),
        P("dev", None),
        P("dev"),
    )
    return jax.shard_map(
        local,
        mesh=mesh,
        in_specs=placed,
        out_specs=(P(None, "dev"), P(None, "dev")),
        check_vma=False,
    )
```

profile of v0, /device:TPU:0, one launch (start us, length us, event | category | flops | bytes accessed | tf_op | source)
XLA Modules:
  0.0 505.3 jit_solution(13376837194865821703)
XLA Ops:
  5.5 7.3 %all-to-all-start = ((s32[32,1,8]{2,1,0:T(1,128)}), s32[32,1,8]{2,1,0:T(1,128)S(1)}, u32[]{:S(2)}, u32[]{:S(2)}) async-start(s32[32,1,8]{2,1,0:T(1,128)} %bitcast.40), calls=%async_computation | async-start | bytes 32768 | tf_op jit(solution)/shard_map/all_to_all | solution.py:107
  13.8 6.2 %all-to-all-done = s32[32,1,8]{2,1,0:T(1,128)S(1)} async-done(((s32[32,1,8]{2,1,0:T(1,128)}), s32[32,1,8]{2,1,0:T(1,128)S(1)}, u32[]{:S(2)}, u32[]{:S(2)}) %all-to-all-start) | async-done | bytes 1056 | tf_op jit(solution)/shard_map/all_to_all | solution.py:107
  28.2 11.9 %all-to-all-done.2 = f32[32,8,512]{2,1,0:T(8,128)S(1)} async-done(((f32[32,8,512]{2,1,0:T(8,128)}), f32[32,8,512]{2,1,0:T(8,128)S(1)}, u32[]{:S(2)}, u32[]{:S(2)}) %all-to-all-start.2) | async-done | bytes 524320 | tf_op jit(solution)/shard_map/all_to_all | solution.py:136
  40.1 3.1 all-to-all-start.1
  44.3 36.4 %all-to-all-done.1 = f32[32,8,3,512]{3,1,2,0:T(8,128)S(1)} async-done(((f32[32,8,3,512]{3,1,2,0:T(8,128)}), f32[32,8,3,512]{3,1,2,0:T(8,128)S(1)}, u32[]{:S(2)}, u32[]{:S(2)}) %all-to-all-start.1) | async-done | bytes 1572896 | tf_op jit(solution)/shard_map/all_to_all | solution.py:127
  83.3 2.8 gather_fusion.1
  86.5 76.7 %while.34 = (s32[]{:T(128)}, f32[16,2,4,512]{3,2,1,0:T(4,128)S(1)}, f32[16,2,4,512]{3,2,1,0:T(4,128)S(1)}, pred[16,2,4]{2,1,0:T(4,128)(4,1)S(1)}, f32[16,2,128]{...) while((s32[]{:T(128)}, f32[16,2,4,512]{3,2,1,0:T(4,128)S(1)}, ...), condition=%wide.region_8.9_spmd, body=%wide.region_3.8_spmd.sunk | while | flops 27263488 | bytes 607893 | solution.py:65
  165.2 3.7 all-to-all-start.4
  170.9 13.7 %all-to-all-done.4 = f32[32,8,512]{2,1,0:T(8,128)S(1)} async-done(((f32[32,8,512]{2,1,0:T(8,128)}), f32[32,8,512]{2,1,0:T(8,128)S(1)}, u32[]{:S(2)}, u32[]{:S(2)}) %all-to-all-start.4) | async-done | bytes 524320 | tf_op jit(solution)/shard_map/all_to_all | solution.py:157
  184.6 3.3 all-to-all-start.3
  192.3 11.3 %all-to-all-done.3 = f32[32,8,512]{2,1,0:T(8,128)} async-done(((f32[32,8,512]{2,1,0:T(8,128)}), f32[32,8,512]{2,1,0:T(8,128)}, u32[]{:S(2)}, u32[]{:S(2)}) %all-to-all-start.3) | async-done | bytes 524320 | tf_op jit(solution)/shard_map/all_to_all | solution.py:160
  206.8 2.9 all-to-all-start.5
  209.7 15.6 %all-to-all-done.5 = f32[32,8,512]{2,1,0:T(8,128)S(1)} async-done(((f32[32,8,512]{2,1,0:T(8,128)}), f32[32,8,512]{2,1,0:T(8,128)S(1)}, u32[]{:S(2)}, u32[]{:S(2)}) %all-to-all-start.5) | async-done | bytes 524320 | tf_op jit(solution)/shard_map/all_to_all | solution.py:136
  226.4 109.7 %while.35 = (s32[]{:T(128)}, f32[16,2,4,512]{3,2,1,0:T(4,128)S(1)}, f32[16,2,4,512]{3,2,1,0:T(4,128)S(1)}, pred[16,2,4]{2,1,0:T(4,128)(4,1)}, f32[16,2,128]{2,1,...) while((s32[]{:T(128)}, f32[16,2,4,512]{3,2,1,0:T(4,128)S(1)}, ...), condition=%wide.region_17.18_spmd, body=%wide.region_12.17_spmd.sunk | while | flops 27263488 | bytes 607893 | solution.py:65
  338.1 3.0 all-to-all-start.7
  343.1 13.6 %all-to-all-done.7 = f32[32,8,512]{2,1,0:T(8,128)S(1)} async-done(((f32[32,8,512]{2,1,0:T(8,128)}), f32[32,8,512]{2,1,0:T(8,128)S(1)}, u32[]{:S(2)}, u32[]{:S(2)}) %all-to-all-start.7) | async-done | bytes 524320 | tf_op jit(solution)/shard_map/all_to_all | solution.py:157
  356.7 3.3 all-to-all-start.6
  363.2 12.4 %all-to-all-done.6 = f32[32,8,512]{2,1,0:T(8,128)} async-done(((f32[32,8,512]{2,1,0:T(8,128)}), f32[32,8,512]{2,1,0:T(8,128)}, u32[]{:S(2)}, u32[]{:S(2)}) %all-to-all-start.6) | async-done | bytes 524320 | tf_op jit(solution)/shard_map/all_to_all | solution.py:160
  378.9 3.1 all-to-all-start.8
  382.1 15.3 %all-to-all-done.8 = f32[32,8,512]{2,1,0:T(8,128)S(1)} async-done(((f32[32,8,512]{2,1,0:T(8,128)}), f32[32,8,512]{2,1,0:T(8,128)S(1)}, u32[]{:S(2)}, u32[]{:S(2)}) %all-to-all-start.8) | async-done | bytes 524320 | tf_op jit(solution)/shard_map/all_to_all | solution.py:136
  398.4 106.2 %while.36 = (s32[]{:T(128)}, f32[16,2,3,128]{3,2,1,0:T(4,128)S(1)}, f32[16,2,4,3,512]{4,3,2,1,0:T(4,128)S(1)}, pred[16,2,4]{2,1,0:T(4,128)(4,1)}, f32[16,2,4,512...) while((s32[]{:T(128)}, f32[16,2,3,128]{3,2,1,0:T(4,128)S(1)}, ...), condition=%wide.region_24.25_spmd, body=%wide.region_21.24_spmd.sunk | while | flops 39846144 | bytes 622205 | solution.py:65
  402.3 2.8 fusion.112
  408.9 2.8 fusion.112
  415.5 2.8 fusion.112
  422.2 2.8 fusion.112
  428.8 2.8 fusion.112
  435.4 2.8 fusion.112
  442.1 2.8 fusion.112
  448.7 2.8 fusion.112
  455.3 2.8 fusion.112
  475.2 2.8 fusion.112
  481.9 2.8 fusion.112
  (644 shorter events, 302.4 us)
Async XLA Ops:
  0.6 23.9 %copy-start = (f32[3,32768]{1,0:T(4,128)S(1)}, f32[3,32768]{1,0:T(4,128)}, u32[]{:S(2)}) copy-start(f32[3,32768]{1,0:T(4,128)} %param.18) | copy-start | bytes 1179652
  3.8 165.3 %copy-start.16 = (s32[128]{0:T(128)}, s32[128]{0:T(128)S(1)}, u32[]{:S(2)}) copy-start(s32[128]{0:T(128)S(1)} %fusion.80) | copy-start | bytes 1540
  5.5 14.4 %all-to-all-start = ((s32[32,1,8]{2,1,0:T(1,128)}), s32[32,1,8]{2,1,0:T(1,128)S(1)}, u32[]{:S(2)}, u32[]{:S(2)}) async-start(s32[32,1,8]{2,1,0:T(1,128)} %bitcast.40), calls=%async_computation | async-start | bytes 32768 | tf_op jit(solution)/shard_map/all_to_all | solution.py:107
  20.1 1.8 copy-start.9
  20.1 4.4 copy-start.6
  21.9 18.2 %all-to-all-start.2 = ((f32[32,8,512]{2,1,0:T(8,128)}), f32[32,8,512]{2,1,0:T(8,128)S(1)}, u32[]{:S(2)}, u32[]{:S(2)}) async-start(f32[32,8,512]{2,1,0:T(8,128)} %bitcast.45), calls=%async_computation.2 | async-start | bytes 1048576 | tf_op jit(solution)/shard_map/all_to_all | solution.py:136
  28.2 15.0 %copy-start.15 = (s32[32]{0:T(128)S(1)}, s32[32]{0:T(128)}, u32[]{:S(2)}) copy-start(s32[32]{0:T(128)} %param.23) | copy-start | bytes 388
  28.2 15.1 %copy-start.2 = (f32[3,4096]{1,0:T(4,128)S(1)}, f32[3,4096]{1,0:T(4,128)}, u32[]{:S(2)}) copy-start(f32[3,4096]{1,0:T(4,128)} %param.15) | copy-start | bytes 147460
  28.2 15.1 %copy-start.12 = (f32[4096]{0:T(1024)S(1)}, f32[4096]{0:T(1024)}, u32[]{:S(2)}) copy-start(f32[4096]{0:T(1024)} %param.17) | copy-start | bytes 49156
  40.1 40.6 %all-to-all-start.1 = ((f32[32,8,3,512]{3,1,2,0:T(8,128)}), f32[32,8,3,512]{3,1,2,0:T(8,128)S(1)}, u32[]{:S(2)}, u32[]{:S(2)}) async-start(f32[32,8,3,512]{3,1,2,0:T(8,128)} %copy.38), calls=%async_computation.1 | async-start | bytes 3145728 | tf_op jit(solution)/shard_map/all_to_all | solution.py:127
  43.4 40.0 %copy-start.13 = (s32[1024]{0:T(1024)}, s32[1024]{0:T(1024)S(1)}, u32[]{:S(2)}) copy-start(s32[1024]{0:T(1024)S(1)} %pad_clamp_fusion) | copy-start | bytes 12292
  163.3 2.0 copy-start.1
  163.3 21.3 %copy-start.4 = (f32[16,2,3,128]{3,1,2,0:T(2,128)}, f32[16,2,3,128]{3,1,2,0:T(2,128)S(1)}, u32[]{:S(2)}) copy-start(f32[16,2,3,128]{3,1,2,0:T(2,128)S(1)} %get-tuple-element.544) | copy-start | bytes 147460
  163.3 21.3 %copy-start.14 = (pred[16,2,4]{2,1,0:T(4,128)(4,1)}, pred[16,2,4]{2,1,0:T(4,128)(4,1)S(1)}, u32[]{:S(2)}) copy-start(pred[16,2,4]{2,1,0:T(4,128)(4,1)S(1)} %get-tuple-element.548) | copy-start | bytes 388
  163.4 25.5 %copy-start.10 = (s32[256]{0:T(256)S(1)}, s32[256]{0:T(256)}, u32[]{:S(2)}) copy-start(s32[256]{0:T(256)} %copy-done.9) | copy-start | bytes 3076
  165.2 26.1 %copy-start.7 = (s32[1024]{0:T(1024)S(1)}, s32[1024]{0:T(1024)}, u32[]{:S(2)}) copy-start(s32[1024]{0:T(1024)} %copy-done.6) | copy-start | bytes 12292
  165.2 19.4 %all-to-all-start.4 = ((f32[32,8,512]{2,1,0:T(8,128)}), f32[32,8,512]{2,1,0:T(8,128)S(1)}, u32[]{:S(2)}, u32[]{:S(2)}) async-start(f32[32,8,512]{2,1,0:T(8,128)} %bitcast.51), calls=%async_computation.4 | async-start | bytes 1048576 | tf_op jit(solution)/shard_map/all_to_all | solution.py:157
  184.6 18.9 %all-to-all-start.3 = ((f32[32,8,512]{2,1,0:T(8,128)}), f32[32,8,512]{2,1,0:T(8,128)}, u32[]{:S(2)}, u32[]{:S(2)}) async-start(f32[32,8,512]{2,1,0:T(8,128)} %bitcast.49), calls=%async_computation.3 | async-start | bytes 1048576 | tf_op jit(solution)/shard_map/all_to_all | solution.py:160
  206.8 18.5 %all-to-all-start.5 = ((f32[32,8,512]{2,1,0:T(8,128)}), f32[32,8,512]{2,1,0:T(8,128)S(1)}, u32[]{:S(2)}, u32[]{:S(2)}) async-start(f32[32,8,512]{2,1,0:T(8,128)} %bitcast.53), calls=%async_computation.5 | async-start | bytes 1048576 | tf_op jit(solution)/shard_map/all_to_all | solution.py:136
  336.1 24.0 %copy-start.11 = (s32[256]{0:T(256)S(1)}, s32[256]{0:T(256)}, u32[]{:S(2)}) copy-start(s32[256]{0:T(256)} %copy-done.9) | copy-start | bytes 3076
  336.2 26.0 %copy-start.8 = (s32[1024]{0:T(1024)S(1)}, s32[1024]{0:T(1024)}, u32[]{:S(2)}) copy-start(s32[1024]{0:T(1024)} %copy-done.6) | copy-start | bytes 12292
  338.1 18.6 %all-to-all-start.7 = ((f32[32,8,512]{2,1,0:T(8,128)}), f32[32,8,512]{2,1,0:T(8,128)S(1)}, u32[]{:S(2)}, u32[]{:S(2)}) async-start(f32[32,8,512]{2,1,0:T(8,128)} %bitcast.58), calls=%async_computation.7 | async-start | bytes 1048576 | tf_op jit(solution)/shard_map/all_to_all | solution.py:157
  356.7 18.9 %all-to-all-start.6 = ((f32[32,8,512]{2,1,0:T(8,128)}), f32[32,8,512]{2,1,0:T(8,128)}, u32[]{:S(2)}, u32[]{:S(2)}) async-start(f32[32,8,512]{2,1,0:T(8,128)} %bitcast.56), calls=%async_computation.6 | async-start | bytes 1048576 | tf_op jit(solution)/shard_map/all_to_all | solution.py:160
  378.9 18.5 %all-to-all-start.8 = ((f32[32,8,512]{2,1,0:T(8,128)}), f32[32,8,512]{2,1,0:T(8,128)S(1)}, u32[]{:S(2)}, u32[]{:S(2)}) async-start(f32[32,8,512]{2,1,0:T(8,128)} %bitcast.60), calls=%async_computation.8 | async-start | bytes 1048576 | tf_op jit(solution)/shard_map/all_to_all | solution.py:136
  398.4 106.2 %copy-start.3 = (f32[3,4096]{1,0:T(4,128)S(1)}, f32[3,4096]{1,0:T(4,128)}, u32[]{:S(2)}) copy-start(f32[3,4096]{1,0:T(4,128)} %param.15) | copy-start | bytes 147460
  398.4 106.2 %copy-start.5 = (f32[3,4096]{1,0:T(4,128)S(1)}, f32[3,4096]{1,0:T(4,128)}, u32[]{:S(2)}) copy-start(f32[3,4096]{1,0:T(4,128)} %param.16) | copy-start | bytes 147460
where the time goes:
time: 508 us; the launch traced here: 505 us
  other arithmetic  196 us (39%)
  waiting for transfers between devices  136 us (27%)
  local copies, waits for them, and re-layouts  90 us (18%)
  matrix products  47.1 us (9%)
  starting transfers between devices  32.4 us (6%)
    dot_general x16, matrix products, centre_block(): jnp.einsum('kij,kdj->di', weight, tile_coordinates, precision=HIGHEST)  44.1 us
    all_to_all x3, waiting for transfers between devices, local(): lax.all_to_all(dual_variable[asked_tile].reshape(devices, capacity, TILE)...  42.9 us
    reduce_sum x32, other arithmetic, row_lse(): total = jnp.sum(jnp.exp(masked - top[None, :, None]), axis=(0, 2))  40.1 us
    reduce_sum x32, other arithmetic, transport_block_update(): column_total_sum = jnp.sum(jnp.exp(score - column_peak[:, None, :]), axis=1)  38.3 us
    reduce_max x32, other arithmetic, row_lse(): top = jnp.max(masked, axis=(0, 2))  36.7 us
    all_to_all x1, waiting for transfers between devices, local(): lax.all_to_all(tile_coordinates[asked_tile].reshape(devices, capacity, 3,...  36.4 us
    squeeze x96, local copies, waits for them, and re-layouts, by_turns(): result = lax.map(lambda group: jax.vmap(func)(*group), folded)  35.8 us
    reduce_max x32, other arithmetic, transport_block_update(): column_peak = jnp.max(score, axis=1)  30.9 us
  transfers between devices with their start and end apart: 9, of which 9 were waited for; matrix products, arithmetic and copies ran while one was open for 3% of the time, Pallas kernels for 0%

commit v1 on v0

v1 whole, which is shorter than its diff:
```python
import functools
import jax
import jax.numpy as jnp
from jax import lax
from jax.experimental import pallas as pl
from jax.experimental.pallas import tpu as pltpu
from jax.sharding import PartitionSpec as P

BLK = 128
TILE = 512
K = 4
CHUNKS = TILE // BLK
EPSILON = 0.01
STIFFNESS = 150.0
TIMESTEP = 0.05
LOG2E = 1.4426950408889634
SCALE = LOG2E / EPSILON
NEGATIVE = -1e30
ROW_SHIFT = 115.0
COL_SHIFT = 110.0
G = 8
ROWS = 4
DEPTH = 32

f32 = jnp.float32
bf16 = jnp.bfloat16
VMEM = pl.BlockSpec(memory_space=pltpu.VMEM)
SMEM = pl.BlockSpec(memory_space=pltpu.SMEM)


def call(kernel, out_shape, in_specs, out_specs, scratch, flops, args):
    size = sum(a.size * a.dtype.itemsize for a in args)
    return pl.pallas_call(
        kernel,
        out_shape=out_shape,
        in_specs=in_specs,
        out_specs=out_specs,
        scratch_shapes=scratch,
        compiler_params=pltpu.CompilerParams(vmem_limit_bytes=56 * 2**20),
        cost_estimate=pl.CostEstimate(flops=flops, bytes_accessed=size, transcendentals=0),
    )(*args)


def split3(value):
    high = value.astype(bf16).astype(f32)
    rest = value - high
    middle = rest.astype(bf16).astype(f32)
    return high, middle, rest - middle


def setup_kernel(capacity, owner_ref, tile_ref, live_ref, pos_ref, send_ref, slot_ref, count_ref):
    blocks = owner_ref.shape[0]

    def clear(i, carry):
        count_ref[i] = 0
        return carry

    lax.fori_loop(0, count_ref.shape[0], clear, 0)
    send_ref[...] = jnp.full(send_ref.shape, -1.0, f32)
    for b in range(blocks):
        rows = [pos_ref[d : d + 1, b * BLK : (b + 1) * BLK] for d in range(3)]
        for k in range(K):
            owner = owner_ref[b, k]
            rank = count_ref[owner]
            count_ref[owner] = rank + 1
            slot = owner * capacity + rank
            slot_ref[b * K + k] = slot
            tile = jnp.where(k < live_ref[b], tile_ref[b, k], -1).astype(f32)
            for d in range(3):
                send_ref[pl.ds(slot * ROWS + d, 1), :] = rows[d]
            send_ref[pl.ds(slot * ROWS + 3, 1), :] = jnp.full((1, BLK), tile, f32)


def home_gather(slot_ref, live_ref, recv_ref, parts_ref, filler):
    blocks = live_ref.shape[0]
    for b in range(blocks):
        live = live_ref[b]
        for k in range(K):
            row = recv_ref[pl.ds(slot_ref[b * K + k], 1), :]
            parts_ref[k, b : b + 1, :] = jnp.where(k < live, row, filler)


def home_scatter(slot_ref, rows_ref, send_ref):
    for b in range(rows_ref.shape[0]):
        row = rows_ref[b : b + 1, :]
        for k in range(K):
            send_ref[pl.ds(slot_ref[b * K + k], 1), :] = row


def home_first_kernel(slot_ref, live_ref, recv_ref, mass_ref, send_ref, row_ref, parts_ref):
    home_gather(slot_ref, live_ref, recv_ref, parts_ref, NEGATIVE)
    parts = parts_ref[...]
    top = jnp.max(parts, axis=0)
    total = jnp.sum(jnp.exp2(parts - top[None]), axis=0)
    row_ref[...] = jnp.log2(mass_ref[...]) - (top + jnp.log2(total))
    home_scatter(slot_ref, row_ref, send_ref)


def home_next_kernel(slot_ref, live_ref, recv_ref, mass_ref, old_ref, send_ref, row_ref, parts_ref):
    home_gather(slot_ref, live_ref, recv_ref, parts_ref, 0.0)
    total = jnp.sum(parts_ref[...], axis=0)
    row_ref[...] = old_ref[...] + jnp.log2(mass_ref[...]) - jnp.log2(total)
    home_scatter(slot_ref, row_ref, send_ref)


def home_last_kernel(slot_ref, live_ref, recv_ref, pos_ref, vel_ref, new_pos_ref, new_vel_ref):
    blocks = live_ref.shape[0]
    for b in range(blocks):
        live = live_ref[b]
        parts = jnp.zeros((ROWS, BLK), f32)
        for k in range(K):
            rows = recv_ref[pl.ds(slot_ref[b * K + k] * ROWS, ROWS), :]
            parts = parts + jnp.where(k < live, rows, 0.0)
        where = slice(b * BLK, (b + 1) * BLK)
        centre = parts[0:3] / parts[3:4] + 0.5
        here = pos_ref[:, where]
        velocity = vel_ref[:, where] + STIFFNESS * (centre - here)
        new_vel_ref[:, where] = velocity
        new_pos_ref[:, where] = here + TIMESTEP * velocity


def sample_kernel(sample_ref, tiles_ref):
    tiles = tiles_ref.shape[0]
    row = lax.broadcasted_iota(jnp.int32, (8, TILE), 0)

    def body(t, carry):
        where = pl.ds(pl.multiple_of(t * TILE, TILE), TILE)
        parts = [jnp.broadcast_to(sample_ref[d : d + 1, where], (8, TILE)) - 0.5 for d in range(3)]
        square = parts[0] * parts[0] + parts[1] * parts[1] + parts[2] * parts[2]
        value = (-0.5 * SCALE) * square
        for d in range(3):
            value = jnp.where((row == d) | (row == d + 5), parts[d], value)
        high, middle, low = split3(value)
        one = row == 3
        first = jnp.where(one, 1.0, jnp.where(row > 4, middle, high))
        second = jnp.where(one, 1.0, jnp.where(row > 4, low, middle))
        third = jnp.where(one, 1.0, jnp.where(row == 4, low, high))
        zero = jnp.zeros_like(first)
        tiles_ref[t] = jnp.concatenate([first, second, third, zero], 0).astype(bf16)
        return carry

    lax.fori_loop(0, tiles, body, 0, unroll=4)


def lanes_of(ref):
    tiles = ref.shape[0] // CHUNKS
    return jnp.concatenate([ref[pl.ds(c, tiles, stride=CHUNKS), :] for c in range(CHUNKS)], 1)


def particle_rows(recv_ref, slot, extra, row):
    parts = [
        (jnp.broadcast_to(recv_ref[pl.ds(slot * ROWS + d, 1), :], (8, BLK)) - 0.5) for d in range(3)
    ]
    square = parts[0] * parts[0] + parts[1] * parts[1] + parts[2] * parts[2]
    value = (-0.5 * SCALE) * square + extra
    for d in range(3):
        value = jnp.where((row == d) | (row == d + 5), SCALE * parts[d], value)
    high, middle, low = split3(value)
    one = row == 4
    first = jnp.where(one, 1.0, jnp.where(row > 4, middle, high))
    second = jnp.where(one, 1.0, jnp.where(row == 3, middle, high))
    third = jnp.where(one, 1.0, jnp.where(row < 3, middle, low))
    zero = jnp.zeros_like(first)
    return jnp.concatenate([first, second, third, zero], 0).T.astype(bf16)


def fold_lanes(value):
    out = value[:, :BLK]
    for c in range(1, CHUNKS):
        out = out + value[:, c * BLK : (c + 1) * BLK]
    return out


def product(left, right):
    return jnp.dot(left, right, preferred_element_type=f32)


def row_first_kernel(tile_ref, recv_ref, tiles_ref, pot_ref, part_ref, list_ref, size_ref, beta_ref, top_ref):
    slots = tile_ref.shape[0]
    tiles = tiles_ref.shape[0]

    def compact(g, count):
        for k in range(G):
            slot = g * G + k
            tile = tile_ref[slot]
            list_ref[0, count] = slot
            list_ref[1, count] = tile
            list_ref[2, count] = tile
            count = count + jnp.where(tile >= 0, 1, 0)
        return count

    count = lax.fori_loop(0, slots // G, compact, 0)
    size_ref[0] = (count + G - 1) // G
    for k in range(G):
        list_ref[0, count + k] = list_ref[0, 0]
        list_ref[1, count + k] = list_ref[1, 0]
        list_ref[2, count + k] = tiles

    pot = lanes_of(pot_ref) * SCALE
    top = jnp.max(pot, axis=1, keepdims=True)
    beta_ref[...] = pot - top
    top_ref[...] = jnp.broadcast_to(top - ROW_SHIFT, top_ref.shape)
    row = lax.broadcasted_iota(jnp.int32, (8, BLK), 0)

    def body(g, carry):
        slot = [list_ref[0, g * G + k] for k in range(G)]
        tile = [list_ref[1, g * G + k] for k in range(G)]
        left = [particle_rows(recv_ref, s, ROW_SHIFT, row) for s in slot]
        raised = [product(a, tiles_ref[t]) for a, t in zip(left, tile)]
        power = [jnp.exp2(a + beta_ref[pl.ds(t, 1), :]) for a, t in zip(raised, tile)]
        total = [jnp.sum(fold_lanes(a).T, axis=0, keepdims=True) for a in power]
        for k in range(G):
            part_ref[pl.ds(slot[k], 1), :] = jnp.log2(total[k]) + top_ref[pl.ds(tile[k], 1), :]
        return carry

    lax.fori_loop(0, size_ref[0], body, 0)


def column_pass(list_ref, groups, recv_ref, rows_ref, tiles_ref, mass_ref, left_ref, sums_ref, peak_ref, pot_ref):
    tiles = tiles_ref.shape[0]
    peak_ref[...] = jnp.full(peak_ref.shape, NEGATIVE, f32)

    def find(g, carry):
        for k in range(G):
            at = pl.ds(list_ref[2, g * G + k], 1)
            peak_ref[at, :] = jnp.maximum(peak_ref[at, :], rows_ref[pl.ds(list_ref[0, g * G + k], 1), :])
        return carry

    lax.fori_loop(0, groups, find, 0)
    peak = jnp.max(peak_ref[0:tiles, :], axis=1, keepdims=True)
    peak_ref[0:tiles, :] = jnp.broadcast_to(COL_SHIFT - peak, (tiles, BLK))
    sums_ref[...] = jnp.zeros(sums_ref.shape, f32)
    row = lax.broadcasted_iota(jnp.int32, (8, BLK), 0)

    def body(g, carry):
        slot = [list_ref[0, g * G + k] for k in range(G)]
        tile = [list_ref[1, g * G + k] for k in range(G)]
        into = [list_ref[2, g * G + k] for k in range(G)]
        extra = [
            jnp.broadcast_to(rows_ref[pl.ds(s, 1), :] + peak_ref[pl.ds(t, 1), :], (8, BLK))
            for s, t in zip(slot, tile)
        ]
        left = [particle_rows(recv_ref, s, e, row) for s, e in zip(slot, extra)]
        for k in range(G):
            left_ref[g * G + k] = left[k]
        raised = [product(a, tiles_ref[t]) for a, t in zip(left, tile)]
        total = [jnp.sum(jnp.exp2(a).reshape(BLK // 8, 8, TILE), axis=0) for a in raised]
        for k in range(G):
            sums_ref[into[k]] += total[k]
        return carry

    lax.fori_loop(0, groups, body, 0)
    total = jnp.sum(sums_ref[0:tiles], axis=1)
    pot_ref[...] = jnp.log2(lanes_of(mass_ref)) - jnp.log2(total)


def middle_kernel(list_ref, size_ref, recv_ref, rows_ref, tiles_ref, mass_ref, part_ref, left_ref, sums_ref, peak_ref, pot_ref):
    groups = size_ref[0]
    column_pass(list_ref, groups, recv_ref, rows_ref, tiles_ref, mass_ref, left_ref, sums_ref, peak_ref, pot_ref)

    def body(g, carry):
        slot = [list_ref[0, g * G + k] for k in range(G)]
        tile = [list_ref[1, g * G + k] for k in range(G)]
        raised = [product(left_ref[g * G + k], tiles_ref[tile[k]]) for k in range(G)]
        power = [jnp.exp2(a + pot_ref[pl.ds(t, 1), :]) for a, t in zip(raised, tile)]
        total = [jnp.sum(fold_lanes(a).T, axis=0, keepdims=True) for a in power]
        for k in range(G):
            part_ref[pl.ds(slot[k], 1), :] = total[k]
        return carry

    lax.fori_loop(0, groups, body, 0)


def last_kernel(list_ref, size_ref, recv_ref, rows_ref, tiles_ref, mass_ref, sample_ref, part_ref, left_ref, sums_ref, peak_ref, pot_ref):
    groups = size_ref[0]
    column_pass(list_ref, groups, recv_ref, rows_ref, tiles_ref, mass_ref, left_ref, sums_ref, peak_ref, pot_ref)
    pieces = 2

    def body(h, carry):
        for j in range(G // pieces):
            at = [h * G + j * pieces + k for k in range(pieces)]
            slot = [list_ref[0, i] for i in at]
            tile = [list_ref[1, i] for i in at]
            raised = [product(left_ref[i], tiles_ref[t]) for i, t in zip(at, tile)]
            power = [jnp.exp2(a + pot_ref[pl.ds(t, 1), :]) for a, t in zip(raised, tile)]
            for k in range(pieces):
                where = pl.ds(pl.multiple_of(tile[k] * TILE, TILE), TILE)
                for d in range(3):
                    place = sample_ref[d : d + 1, where] - 0.5
                    part_ref[pl.ds(slot[k] * ROWS + d, 1), :] = jnp.sum(
                        fold_lanes(power[k] * place).T, axis=0, keepdims=True
                    )
                part_ref[pl.ds(slot[k] * ROWS + 3, 1), :] = jnp.sum(
                    fold_lanes(power[k]).T, axis=0, keepdims=True
                )
        return carry

    lax.fori_loop(0, groups, body, 0)


def local(
    positions,
    velocities,
    masses,
    samples,
    sample_mass,
    start_potential,
    route_owner,
    route_tile,
    live_count,
):
    devices = lax.axis_size("dev")
    blocks = route_owner.shape[0]
    tiles = start_potential.shape[0] // TILE
    capacity = 2 * blocks * K // devices
    slots = devices * capacity
    struct = jax.ShapeDtypeStruct

    def exchange(values):
        rows = values.shape[0] // devices
        got = lax.all_to_all(
            values.reshape(devices, rows, BLK), "dev", split_axis=0, concat_axis=0, tiled=True
        )
        return got.reshape(values.shape)

    send, slot = call(
        functools.partial(setup_kernel, capacity),
        (struct((slots * ROWS, BLK), f32), struct((blocks * K,), jnp.int32)),
        [SMEM, SMEM, SMEM, VMEM],
        (VMEM, SMEM),
        [pltpu.SMEM((devices,), jnp.int32)],
        10**6,
        (route_owner, route_tile, live_count, positions),
    )
    recv = exchange(send)
    split_tiles = call(
        sample_kernel,
        struct((tiles, DEPTH, TILE), bf16),
        [VMEM],
        VMEM,
        [],
        10**7,
        (samples,),
    )
    mass_rows = masses.reshape(blocks, BLK)
    sample_rows = sample_mass.reshape(tiles * CHUNKS, BLK)
    pot_rows = start_potential.reshape(tiles * CHUNKS, BLK)
    asked = recv.reshape(slots, ROWS, BLK)[:, 3, 0].astype(jnp.int32)

    part, listed, size = call(
        row_first_kernel,
        (struct((slots, BLK), f32), struct((3, slots + 2 * G), jnp.int32), struct((1,), jnp.int32)),
        [SMEM, VMEM, VMEM, VMEM],
        (VMEM, SMEM, SMEM),
        [pltpu.VMEM((tiles, TILE), f32), pltpu.VMEM((tiles, BLK), f32)],
        10**9,
        (asked, recv, split_tiles, pot_rows),
    )
    part = exchange(part)
    row_scratch = [pltpu.VMEM((K, blocks, BLK), f32)]
    row_out = (struct((slots, BLK), f32), struct((blocks, BLK), f32))
    send, row = call(
        home_first_kernel,
        row_out,
        [SMEM, SMEM, VMEM, VMEM],
        (VMEM, VMEM),
        row_scratch,
        10**6,
        (slot, live_count, part, mass_rows),
    )
    rows = exchange(send)
    scratch = [
        pltpu.VMEM((slots + G, BLK, DEPTH), bf16),
        pltpu.VMEM((tiles + 1, 8, TILE), f32),
        pltpu.VMEM((tiles + 8, BLK), f32),
        pltpu.VMEM((tiles, TILE), f32),
    ]
    part = call(
        middle_kernel,
        struct((slots, BLK), f32),
        [SMEM, SMEM] + [VMEM] * 4,
        VMEM,
        scratch,
        10**9,
        (listed, size, recv, rows, split_tiles, sample_rows),
    )
    part = exchange(part)
    send, row = call(
        home_next_kernel,
        row_out,
        [SMEM, SMEM, VMEM, VMEM, VMEM],
        (VMEM, VMEM),
        row_scratch,
        10**6,
        (slot, live_count, part, mass_rows, row),
    )
    rows = exchange(send)
    part = call(
        last_kernel,
        struct((slots * ROWS, BLK), f32),
        [SMEM, SMEM] + [VMEM] * 5,
        VMEM,
        scratch,
        10**9,
        (listed, size, recv, rows, split_tiles, sample_rows, samples),
    )
    part = exchange(part)
    return call(
        home_last_kernel,
        (struct(positions.shape, f32), struct(positions.shape, f32)),
        [SMEM, SMEM, VMEM, VMEM, VMEM],
        (VMEM, VMEM),
        [],
        10**6,
        (slot, live_count, part, positions, velocities),
    )


def solution(mesh):
    placed = (
        P(None, "dev"),
        P(None, "dev"),
        P("dev"),
        P(None, "dev"),
        P("dev"),
        P("dev"),
        P("dev", None),
        P("dev", None),
        P("dev"),
    )
    return jax.shard_map(
        local,
        mesh=mesh,
        in_specs=placed,
        out_specs=(P(None, "dev"), P(None, "dev")),
        check_vma=False,
    )
```

time: 508 us -> 201 us (0.40)
  other arithmetic: 196 us -> 5.19 us
  waiting for transfers between devices: 136 us -> 12.2 us
  blocking collectives: 0 us -> 113 us
  local copies, waits for them, and re-layouts: 90 us -> 2.74 us
  Pallas kernels: 0 us -> 58.6 us
  matrix products: 47.1 us -> 0 us
  starting transfers between devices: 32.4 us -> 7.33 us
    all_to_all x9 -> x1, waiting for transfers between devices: 136 us -> 12.2 us  [exchange(): lax.all_to_all(values.reshape(devices, rows, BLK), 'dev', split_axis=0, c...]
    all_to_all x0 -> x5, blocking collectives: none -> 113 us  [exchange(): lax.all_to_all(values.reshape(devices, rows, BLK), 'dev', split_axis=0, c...]
    reduce_sum x81 -> x0, other arithmetic: 98.6 us -> none  [the longest x32 40.1 us: row_lse(): total = jnp.sum(jnp.exp(masked - top[None, :, None]), axis=(0, 2))]
    reduce_max x80 -> x0, other arithmetic: 86 us -> none  [the longest x32 36.7 us: row_lse(): top = jnp.max(masked, axis=(0, 2))]
    pallas_call x0 -> x8, Pallas kernels: none -> 58.6 us  [call(): pl.pallas_call(kernel, out_shape=out_shape, in_specs=in_specs, out_specs=...]
    dot_general x18 -> x0, matrix products: 47.1 us -> none  [the longest x16 44.1 us: centre_block(): jnp.einsum('kij,kdj->di', weight, tile_coordinates, precision=HIGHEST)]
    squeeze x96 -> x0, local copies, waits for them, and re-layouts: 35.8 us -> none  [by_turns(): result = lax.map(lambda group: jax.vmap(func)(*group), folded)]
    all_to_all x9 -> x1, starting transfers between devices: 32.4 us -> 7.33 us  [exchange(): lax.all_to_all(values.reshape(devices, rows, BLK), 'dev', split_axis=0, c...]
  transfers between devices with their start and end apart: 9 -> 1, of which waited for: 9 -> 1; matrix products, arithmetic and copies ran while one was open for 3% -> 0% of each run, Pallas kernels for 0% -> 2%
where the time goes in v1:
time: 201 us; the launch traced here: 200 us
  blocking collectives  113 us (56%)
  Pallas kernels  58.6 us (29%)
  waiting for transfers between devices  12.2 us (6%)
  starting transfers between devices  7.33 us (4%)
  other arithmetic  5.19 us (3%)
  local copies, waits for them, and re-layouts  2.74 us (1%)
    all_to_all x5, blocking collectives, exchange(): lax.all_to_all(values.reshape(devices, rows, BLK), 'dev', split_axis=0, c...  113 us
    pallas_call x8, Pallas kernels, call(): pl.pallas_call(kernel, out_shape=out_shape, in_specs=in_specs, out_specs=...  58.6 us
    all_to_all x1, waiting for transfers between devices, exchange(): lax.all_to_all(values.reshape(devices, rows, BLK), 'dev', split_axis=0, c...  12.2 us
    all_to_all x1, starting transfers between devices, exchange(): lax.all_to_all(values.reshape(devices, rows, BLK), 'dev', split_axis=0, c...  7.33 us
    convert_element_type x1, other arithmetic, local(): asked = recv.reshape(slots, ROWS, BLK)[:, 3, 0].astype(jnp.int32)  5.19 us
  transfers between devices with their start and end apart: 1, of which 1 were waited for; matrix products, arithmetic and copies ran while one was open for 0% of the time, Pallas kernels for 2%

profile of v1, /device:TPU:0, one launch (start us, length us, event | category | flops | bytes accessed | tf_op | source)
XLA Modules:
  0.0 200.0 jit_solution(12220389363070063911)
XLA Ops:
  0.6 1.4 copy.15.owner_ref
  2.0 1.4 copy.16.tile_ref
  3.4 2.8 %shard_map.104 = (f32[1024,128]{1,0:T(8,128)}, s32[128]{0:T(128)}) custom-call(s32[32,4]{1,0:T(8,128)} %copy.15.owner_ref, s32[32,4]{1,0:T(8,128)} %copy.16.tile_ref, s32[32]{0:T(128)} %live_ref.7, f32[3,4096]{1,0:T(4,128)} %pos_ref.3), custom_call_target="tpu_custom_call" | custom-call | flops 1000000 | bytes 50304 | tf_op jit(solution)/shard_map/pallas_call | solution.py:33
  6.2 7.3 %all-to-all-start = ((f32[32,32,128]{2,1,0:T(8,128)}), f32[32,32,128]{2,1,0:T(8,128)S(1)}, u32[]{:S(2)}, u32[]{:S(2)}) async-start(f32[32,32,128]{2,1,0:T(8,128)} %bitcast.24), calls=%async_computation | async-start | bytes 1048576 | tf_op jit(solution)/shard_map/all_to_all | solution.py:321
  13.5 3.4 %shard_map.105.tiles_ref = bf16[64,32,512]{2,1,0:T(8,128)(2,1)} custom-call(f32[3,32768]{1,0:T(4,128)} %sample_ref.3), custom_call_target="tpu_custom_call" | custom-call | flops 10000000 | bytes 393216 | tf_op jit(solution)/shard_map/pallas_call | solution.py:33
  16.9 12.2 %all-to-all-done = f32[32,32,128]{2,1,0:T(8,128)S(1)} async-done(((f32[32,32,128]{2,1,0:T(8,128)}), f32[32,32,128]{2,1,0:T(8,128)S(1)}, u32[]{:S(2)}, u32[]{:S(2)}) %all-to-all-start) | async-done | bytes 524320 | tf_op jit(solution)/shard_map/all_to_all | solution.py:321
  29.2 0.0 copy-start
  29.2 5.2 %fusion.tile_ref = s32[256]{0:T(256)} fusion(f32[256,4,128]{2,1,0:T(4,128)S(1)} %bitcast.16), kind=kLoop, calls=%fused_computation.1 | loop fusion | flops 256 | bytes 2048 | tf_op jit(solution)/shard_map/convert_element_type | solution.py:348
  34.4 0.0 copy-done
  34.4 10.6 %shard_map.106 = (f32[256,128]{1,0:T(8,128)}, s32[3,272]{1,0:T(4,128)}, s32[1]{0:T(128)}) custom-call(s32[256]{0:T(256)} %fusion.tile_ref, f32[1024,128]{1,0:T(8,128)} %bitcast.17, bf16[64,32,512]{2,1,0:T(8,128)(2,1)} %shard_map.105.tiles_ref, f32[256,128]{1,0:T(8,128)} %bitcast.35), custom_call_target="tpu_custom_call" | custom-call | flops 1000000000 | bytes 2753536 | tf_op jit(solution)/shard_map/pallas_call | solution.py:33
  44.9 20.4 %all_to_all.30 = f32[32,8,128]{2,1,0:T(8,128)} all-to-all(f32[32,8,128]{2,1,0:T(8,128)} %bitcast.28), channel_id=1, replica_groups=mesh['dev'=32] {'dev'}, dimensions={0} | all-to-all | bytes 262144 | tf_op jit(solution)/shard_map/all_to_all | solution.py:321
  65.3 1.8 shard_map.107
  67.1 11.5 %all_to_all.31 = f32[32,8,128]{2,1,0:T(8,128)} all-to-all(f32[32,8,128]{2,1,0:T(8,128)} %bitcast.30), channel_id=1, replica_groups=mesh['dev'=32] {'dev'}, dimensions={0} | all-to-all | bytes 262144 | tf_op jit(solution)/shard_map/all_to_all | solution.py:321
  78.6 15.5 %shard_map.108 = f32[256,128]{1,0:T(8,128)} custom-call(s32[3,272]{1,0:T(4,128)} %get-tuple-element.12.list_ref, s32[1]{0:T(128)} %get-tuple-element.13.size_ref, f32[1024,128]{1,0:T(8,128)} %bitcast.18, f32[256,128]{1,0:T(8,128)} %bitcast.31, bf16[64,32,512]{2,1,0:T(8,128)(2,1)} %shard_map.105.tiles_ref, f32[256,128]{1,0:T(8,128)} %bitcast.26), custom_call_target="tpu_custom_call" | custom-call | flops 1000000000 | bytes 2886852 | tf_op jit(solution)/shard_map/pallas_call | solution.py:33
  94.1 27.4 %all_to_all.32 = f32[32,8,128]{2,1,0:T(8,128)} all-to-all(f32[32,8,128]{2,1,0:T(8,128)} %bitcast.32), channel_id=1, replica_groups=mesh['dev'=32] {'dev'}, dimensions={0} | all-to-all | bytes 262144 | tf_op jit(solution)/shard_map/all_to_all | solution.py:321
  121.5 1.8 shard_map.109
  123.3 11.4 %all_to_all.33 = f32[32,8,128]{2,1,0:T(8,128)} all-to-all(f32[32,8,128]{2,1,0:T(8,128)} %bitcast.29), channel_id=1, replica_groups=mesh['dev'=32] {'dev'}, dimensions={0} | all-to-all | bytes 262144 | tf_op jit(solution)/shard_map/all_to_all | solution.py:321
  134.8 20.7 %shard_map.110 = f32[1024,128]{1,0:T(8,128)} custom-call(s32[3,272]{1,0:T(4,128)} %get-tuple-element.12.list_ref, s32[1]{0:T(128)} %get-tuple-element.13.size_ref, f32[1024,128]{1,0:T(8,128)} %bitcast.19, f32[256,128]{1,0:T(8,128)} %bitcast.22, bf16[64,32,512]{2,1,0:T(8,128)(2,1)} %shard_map.105.tiles_ref, f32[256,128]{1,0:T(8,128)} %bitcast.27, ...), custom_call_target="tpu_custom_call" | custom-call | flops 1000000000 | bytes 3280068 | tf_op jit(solution)/shard_map/pallas_call | solution.py:33
  155.5 42.5 %all_to_all.34 = f32[32,32,128]{2,1,0:T(8,128)} all-to-all(f32[32,32,128]{2,1,0:T(8,128)} %bitcast.20), channel_id=1, replica_groups=mesh['dev'=32] {'dev'}, dimensions={0} | all-to-all | bytes 1048576 | tf_op jit(solution)/shard_map/all_to_all | solution.py:321
  198.0 2.0 shard_map.111
Async XLA Ops:
  6.2 23.0 %all-to-all-start = ((f32[32,32,128]{2,1,0:T(8,128)}), f32[32,32,128]{2,1,0:T(8,128)S(1)}, u32[]{:S(2)}, u32[]{:S(2)}) async-start(f32[32,32,128]{2,1,0:T(8,128)} %bitcast.24), calls=%async_computation | async-start | bytes 1048576 | tf_op jit(solution)/shard_map/all_to_all | solution.py:321
  29.2 5.2 %copy-start = (f32[32,32,128]{2,1,0:T(8,128)}, f32[32,32,128]{2,1,0:T(8,128)S(1)}, u32[]{:S(2)}) copy-start(f32[32,32,128]{2,1,0:T(8,128)S(1)} %all-to-all-done) | copy-start | bytes 1572868

commit v2 on v1

--- a/solution.py
+++ b/solution.py
@@ -18,7 +18,8 @@
 NEGATIVE = -1e30
 ROW_SHIFT = 115.0
 COL_SHIFT = 110.0
-G = 8
+G = 16
+KEPT = 208
 ROWS = 4
 DEPTH = 32
 
@@ -36,7 +37,7 @@
         in_specs=in_specs,
         out_specs=out_specs,
         scratch_shapes=scratch,
-        compiler_params=pltpu.CompilerParams(vmem_limit_bytes=56 * 2**20),
+        compiler_params=pltpu.CompilerParams(vmem_limit_bytes=67_000_000),
         cost_estimate=pl.CostEstimate(flops=flops, bytes_accessed=size, transcendentals=0),
     )(*args)
 
@@ -49,7 +50,8 @@
 
 
 def setup_kernel(capacity, owner_ref, tile_ref, live_ref, pos_ref, send_ref, slot_ref, count_ref):
-    blocks = owner_ref.shape[0]
+    blocks = live_ref.shape[0]
+    stride = capacity * ROWS
 
     def clear(i, carry):
         count_ref[i] = 0
@@ -60,15 +62,15 @@
     for b in range(blocks):
         rows = [pos_ref[d : d + 1, b * BLK : (b + 1) * BLK] for d in range(3)]
         for k in range(K):
-            owner = owner_ref[b, k]
+            owner = owner_ref[k, b]
             rank = count_ref[owner]
             count_ref[owner] = rank + 1
-            slot = owner * capacity + rank
-            slot_ref[b * K + k] = slot
-            tile = jnp.where(k < live_ref[b], tile_ref[b, k], -1).astype(f32)
+            slot_ref[b * K + k] = owner * capacity + rank
+            tile = jnp.where(k < live_ref[b], tile_ref[k, b], -1).astype(f32)
+            base = owner * stride + rank
             for d in range(3):
-                send_ref[pl.ds(slot * ROWS + d, 1), :] = rows[d]
-            send_ref[pl.ds(slot * ROWS + 3, 1), :] = jnp.full((1, BLK), tile, f32)
+                send_ref[pl.ds(base + d * capacity, 1), :] = rows[d]
+            send_ref[pl.ds(base + 3 * capacity, 1), :] = jnp.full((1, BLK), tile, f32)
 
 
 def home_gather(slot_ref, live_ref, recv_ref, parts_ref, filler):
@@ -147,9 +149,11 @@
     return jnp.concatenate([ref[pl.ds(c, tiles, stride=CHUNKS), :] for c in range(CHUNKS)], 1)
 
 
-def particle_rows(recv_ref, slot, extra, row):
+def particle_rows(recv_ref, place, extra, row):
+    base, capacity = place
     parts = [
-        (jnp.broadcast_to(recv_ref[pl.ds(slot * ROWS + d, 1), :], (8, BLK)) - 0.5) for d in range(3)
+        (jnp.broadcast_to(recv_ref[pl.ds(base + d * capacity, 1), :], (8, BLK)) - 0.5)
+        for d in range(3)
     ]
     square = parts[0] * parts[0] + parts[1] * parts[1] + parts[2] * parts[2]
     value = (-0.5 * SCALE) * square + extra
@@ -175,37 +179,56 @@
     return jnp.dot(left, right, preferred_element_type=f32)
 
 
-def row_first_kernel(tile_ref, recv_ref, tiles_ref, pot_ref, part_ref, list_ref, size_ref, beta_ref, top_ref):
-    slots = tile_ref.shape[0]
-    tiles = tiles_ref.shape[0]
-
-    def compact(g, count):
-        for k in range(G):
-            slot = g * G + k
-            tile = tile_ref[slot]
-            list_ref[0, count] = slot
-            list_ref[1, count] = tile
-            list_ref[2, count] = tile
-            count = count + jnp.where(tile >= 0, 1, 0)
-        return count
-
-    count = lax.fori_loop(0, slots // G, compact, 0)
-    size_ref[0] = (count + G - 1) // G
-    for k in range(G):
-        list_ref[0, count + k] = list_ref[0, 0]
-        list_ref[1, count + k] = list_ref[1, 0]
-        list_ref[2, count + k] = tiles
+def row_first_kernel(
+    capacity,
+    recv_ref,
+    tiles_ref,
+    pot_ref,
+    part_ref,
+    list_ref,
+    size_ref,
+    beta_ref,
+    top_ref,
+    asked_ref,
+    tile_ref,
+    sem,
+):
+    devices = asked_ref.shape[0]
+    lane = lax.broadcasted_iota(jnp.int32, (devices, capacity, BLK), 2)
+    rank = lax.broadcasted_iota(jnp.int32, (devices, capacity, BLK), 1)
+    asked = recv_ref[...].reshape(devices, ROWS * capacity, BLK)[:, 3 * capacity :, :]
+    asked_ref[...] = jnp.sum(jnp.where(lane == rank, asked, 0.0), axis=1).astype(jnp.int32)
+    copy = pltpu.make_async_copy(asked_ref, tile_ref, sem)
+    copy.start()
 
     pot = lanes_of(pot_ref) * SCALE
     top = jnp.max(pot, axis=1, keepdims=True)
     beta_ref[...] = pot - top
     top_ref[...] = jnp.broadcast_to(top - ROW_SHIFT, top_ref.shape)
     row = lax.broadcasted_iota(jnp.int32, (8, BLK), 0)
+    copy.wait()
+
+    def compact(device, count):
+        for k in range(capacity):
+            tile = tile_ref[device, k]
+            list_ref[0, count] = device * capacity + k
+            list_ref[1, count] = tile
+            list_ref[2, count] = device * (capacity * ROWS) + k
+            count = count + jnp.where(tile >= 0, 1, 0)
+        return count
+
+    count = lax.fori_loop(0, devices, compact, 0)
+    size_ref[0] = (count + G - 1) // G
+    size_ref[1] = count
+    for k in range(G):
+        for i in range(3):
+            list_ref[i, count + k] = list_ref[i, 0]
 
     def body(g, carry):
         slot = [list_ref[0, g * G + k] for k in range(G)]
         tile = [list_ref[1, g * G + k] for k in range(G)]
-        left = [particle_rows(recv_ref, s, ROW_SHIFT, row) for s in slot]
+        base = [list_ref[2, g * G + k] for k in range(G)]
+        left = [particle_rows(recv_ref, (i, capacity), ROW_SHIFT, row) for i in base]
         raised = [product(a, tiles_ref[t]) for a, t in zip(left, tile)]
         power = [jnp.exp2(a + beta_ref[pl.ds(t, 1), :]) for a, t in zip(raised, tile)]
         total = [jnp.sum(fold_lanes(a).T, axis=0, keepdims=True) for a in power]
@@ -216,86 +239,168 @@
     lax.fori_loop(0, size_ref[0], body, 0)
 
 
-def column_pass(list_ref, groups, recv_ref, rows_ref, tiles_ref, mass_ref, left_ref, sums_ref, peak_ref, pot_ref):
+def iterate(
+    capacity,
+    weights,
+    store,
+    list_ref,
+    size_ref,
+    recv_ref,
+    rows_ref,
+    tiles_ref,
+    mass_ref,
+    kept_ref,
+    sums_ref,
+    peak_ref,
+    weight_ref,
+):
     tiles = tiles_ref.shape[0]
+    groups, count = size_ref[0], size_ref[1]
+    limit = jnp.minimum(groups, KEPT // G)
+    row = lax.broadcasted_iota(jnp.int32, (8, BLK), 0)
     peak_ref[...] = jnp.full(peak_ref.shape, NEGATIVE, f32)
 
     def find(g, carry):
         for k in range(G):
-            at = pl.ds(list_ref[2, g * G + k], 1)
-            peak_ref[at, :] = jnp.maximum(peak_ref[at, :], rows_ref[pl.ds(list_ref[0, g * G + k], 1), :])
+            at = pl.ds(list_ref[1, g * G + k], 1)
+            peak_ref[at, :] = jnp.maximum(
+                peak_ref[at, :], rows_ref[pl.ds(list_ref[0, g * G + k], 1), :]
+            )
         return carry
 
     lax.fori_loop(0, groups, find, 0)
-    peak = jnp.max(peak_ref[0:tiles, :], axis=1, keepdims=True)
-    peak_ref[0:tiles, :] = jnp.broadcast_to(COL_SHIFT - peak, (tiles, BLK))
+    peak = jnp.max(peak_ref[...], axis=1, keepdims=True)
+    peak_ref[...] = jnp.broadcast_to(COL_SHIFT - peak, peak_ref.shape)
     sums_ref[...] = jnp.zeros(sums_ref.shape, f32)
-    row = lax.broadcasted_iota(jnp.int32, (8, BLK), 0)
-
-    def body(g, carry):
+
+    def powers(g):
         slot = [list_ref[0, g * G + k] for k in range(G)]
         tile = [list_ref[1, g * G + k] for k in range(G)]
-        into = [list_ref[2, g * G + k] for k in range(G)]
+        base = [list_ref[2, g * G + k] for k in range(G)]
         extra = [
             jnp.broadcast_to(rows_ref[pl.ds(s, 1), :] + peak_ref[pl.ds(t, 1), :], (8, BLK))
             for s, t in zip(slot, tile)
         ]
-        left = [particle_rows(recv_ref, s, e, row) for s, e in zip(slot, extra)]
+        left = [particle_rows(recv_ref, (i, capacity), e, row) for i, e in zip(base, extra)]
+        raised = [product(a, tiles_ref[t]) for a, t in zip(left, tile)]
+        return slot, tile, [jnp.exp2(a) for a in raised]
+
+    def add_up(g, tile, power):
+        total = [jnp.sum(a.reshape(BLK // 8, 8, TILE), axis=0) for a in power]
         for k in range(G):
-            left_ref[g * G + k] = left[k]
-        raised = [product(a, tiles_ref[t]) for a, t in zip(left, tile)]
-        total = [jnp.sum(jnp.exp2(a).reshape(BLK // 8, 8, TILE), axis=0) for a in raised]
+            into = jnp.where(g * G + k < count, tile[k], tiles)
+            sums_ref[into] += total[k]
+
+    def first_kept(g, carry):
+        slot, tile, power = powers(g)
         for k in range(G):
-            sums_ref[into[k]] += total[k]
-        return carry
-
-    lax.fori_loop(0, groups, body, 0)
+            kept_ref[g * G + k] = power[k]
+        add_up(g, tile, power)
+        return carry
+
+    def first_rest(g, carry):
+        slot, tile, power = powers(g)
+        add_up(g, tile, power)
+        return carry
+
+    lax.fori_loop(0, limit, first_kept, 0)
+    lax.fori_loop(limit, groups, first_rest, 0)
     total = jnp.sum(sums_ref[0:tiles], axis=1)
-    pot_ref[...] = jnp.log2(lanes_of(mass_ref)) - jnp.log2(total)
-
-
-def middle_kernel(list_ref, size_ref, recv_ref, rows_ref, tiles_ref, mass_ref, part_ref, left_ref, sums_ref, peak_ref, pot_ref):
-    groups = size_ref[0]
-    column_pass(list_ref, groups, recv_ref, rows_ref, tiles_ref, mass_ref, left_ref, sums_ref, peak_ref, pot_ref)
-
-    def body(g, carry):
-        slot = [list_ref[0, g * G + k] for k in range(G)]
-        tile = [list_ref[1, g * G + k] for k in range(G)]
-        raised = [product(left_ref[g * G + k], tiles_ref[tile[k]]) for k in range(G)]
-        power = [jnp.exp2(a + pot_ref[pl.ds(t, 1), :]) for a, t in zip(raised, tile)]
-        total = [jnp.sum(fold_lanes(a).T, axis=0, keepdims=True) for a in power]
+    weights(lanes_of(mass_ref) / total, weight_ref)
+
+    def second_kept(g, carry):
         for k in range(G):
-            part_ref[pl.ds(slot[k], 1), :] = total[k]
-        return carry
-
-    lax.fori_loop(0, groups, body, 0)
-
-
-def last_kernel(list_ref, size_ref, recv_ref, rows_ref, tiles_ref, mass_ref, sample_ref, part_ref, left_ref, sums_ref, peak_ref, pot_ref):
-    groups = size_ref[0]
-    column_pass(list_ref, groups, recv_ref, rows_ref, tiles_ref, mass_ref, left_ref, sums_ref, peak_ref, pot_ref)
-    pieces = 2
-
-    def body(h, carry):
-        for j in range(G // pieces):
-            at = [h * G + j * pieces + k for k in range(pieces)]
-            slot = [list_ref[0, i] for i in at]
-            tile = [list_ref[1, i] for i in at]
-            raised = [product(left_ref[i], tiles_ref[t]) for i, t in zip(at, tile)]
-            power = [jnp.exp2(a + pot_ref[pl.ds(t, 1), :]) for a, t in zip(raised, tile)]
-            for k in range(pieces):
-                where = pl.ds(pl.multiple_of(tile[k] * TILE, TILE), TILE)
-                for d in range(3):
-                    place = sample_ref[d : d + 1, where] - 0.5
-                    part_ref[pl.ds(slot[k] * ROWS + d, 1), :] = jnp.sum(
-                        fold_lanes(power[k] * place).T, axis=0, keepdims=True
-                    )
-                part_ref[pl.ds(slot[k] * ROWS + 3, 1), :] = jnp.sum(
-                    fold_lanes(power[k]).T, axis=0, keepdims=True
-                )
-        return carry
-
-    lax.fori_loop(0, groups, body, 0)
+            store(list_ref[0, g * G + k], list_ref[1, g * G + k], kept_ref[g * G + k], weight_ref)
+        return carry
+
+    def second_rest(g, carry):
+        slot, tile, power = powers(g)
+        for k in range(G):
+            store(slot[k], tile[k], power[k], weight_ref)
+        return carry
+
+    lax.fori_loop(0, limit, second_kept, 0)
+    lax.fori_loop(limit, groups, second_rest, 0)
+
+
+def middle_kernel(
+    capacity, list_ref, size_ref, recv_ref, rows_ref, tiles_ref, mass_ref, part_ref, *scratch
+):
+    def weights(value, weight_ref):
+        weight_ref[...] = value
+
+    def store(slot, tile, power, weight_ref):
+        power = power * weight_ref[pl.ds(tile, 1), :]
+        part_ref[pl.ds(slot, 1), :] = jnp.sum(fold_lanes(power).T, axis=0, keepdims=True)
+
+    iterate(
+        capacity,
+        weights,
+        store,
+        list_ref,
+        size_ref,
+        recv_ref,
+        rows_ref,
+        tiles_ref,
+        mass_ref,
+        *scratch,
+    )
+
+
+def last_kernel(
+    capacity,
+    list_ref,
+    size_ref,
+    recv_ref,
+    rows_ref,
+    tiles_ref,
+    mass_ref,
+    sample_ref,
+    part_ref,
+    *scratch,
+):
+    *scratch, value_ref = scratch
+    row = lax.broadcasted_iota(jnp.int32, (8, TILE), 0)
+
+    def weights(value, weight_ref):
+        value_ref[...] = value
+
+        def body(t, carry):
+            where = pl.ds(pl.multiple_of(t * TILE, TILE), TILE)
+            place = jnp.ones((8, TILE), f32)
+            for d in range(3):
+                part = jnp.broadcast_to(sample_ref[d : d + 1, where], (8, TILE)) - 0.5
+                place = jnp.where((row == d) | (row == d + 4), part, place)
+            high, middle, low = split3(place * value_ref[pl.ds(t, 1), :])
+            upper = jnp.where(row < 4, high, middle)
+            lower = jnp.where(row < 4, low, 0.0)
+            weight_ref[t] = jnp.concatenate([upper, lower], 0).astype(bf16)
+            return carry
+
+        lax.fori_loop(0, value_ref.shape[0], body, 0, unroll=4)
+
+    def store(slot, tile, power, weight_ref):
+        left = weight_ref[tile]
+        high = power.astype(bf16)
+        low = (power - high.astype(f32)).astype(bf16)
+        dims = (((1,), (1,)), ((), ()))
+        out = lax.dot_general(left, high, dims, preferred_element_type=f32)
+        out = out + lax.dot_general(left, low, dims, preferred_element_type=f32)
+        out = out[0:8] + out[8:16]
+        part_ref[pl.ds(pl.multiple_of(slot * ROWS, ROWS), ROWS), :] = out[0:4] + out[4:8]
+
+    iterate(
+        capacity,
+        weights,
+        store,
+        list_ref,
+        size_ref,
+        recv_ref,
+        rows_ref,
+        tiles_ref,
+        mass_ref,
+        *scratch,
+    )
 
 
 def local(
@@ -330,7 +435,7 @@
         (VMEM, SMEM),
         [pltpu.SMEM((devices,), jnp.int32)],
         10**6,
-        (route_owner, route_tile, live_count, positions),
+        (route_owner.T, route_tile.T, live_count, positions),
     )
     recv = exchange(send)
     split_tiles = call(
@@ -345,16 +450,20 @@
     mass_rows = masses.reshape(blocks, BLK)
     sample_rows = sample_mass.reshape(tiles * CHUNKS, BLK)
     pot_rows = start_potential.reshape(tiles * CHUNKS, BLK)
-    asked = recv.reshape(slots, ROWS, BLK)[:, 3, 0].astype(jnp.int32)
-
     part, listed, size = call(
-        row_first_kernel,
-        (struct((slots, BLK), f32), struct((3, slots + 2 * G), jnp.int32), struct((1,), jnp.int32)),
-        [SMEM, VMEM, VMEM, VMEM],
+        functools.partial(row_first_kernel, capacity),
+        (struct((slots, BLK), f32), struct((3, slots + 2 * G), jnp.int32), struct((2,), jnp.int32)),
+        [VMEM, VMEM, VMEM],
         (VMEM, SMEM, SMEM),
-        [pltpu.VMEM((tiles, TILE), f32), pltpu.VMEM((tiles, BLK), f32)],
+        [
+            pltpu.VMEM((tiles, TILE), f32),
+            pltpu.VMEM((tiles, BLK), f32),
+            pltpu.VMEM((devices, BLK), jnp.int32),
+            pltpu.SMEM((devices, BLK), jnp.int32),
+            pltpu.SemaphoreType.DMA,
+        ],
         10**9,
-        (asked, recv, split_tiles, pot_rows),
+        (recv, split_tiles, pot_rows),
     )
     part = exchange(part)
     row_scratch = [pltpu.VMEM((K, blocks, BLK), f32)]
@@ -370,17 +479,17 @@
     )
     rows = exchange(send)
     scratch = [
-        pltpu.VMEM((slots + G, BLK, DEPTH), bf16),
+        pltpu.VMEM((min(KEPT, slots), BLK, TILE), f32),
         pltpu.VMEM((tiles + 1, 8, TILE), f32),
-        pltpu.VMEM((tiles + 8, BLK), f32),
-        pltpu.VMEM((tiles, TILE), f32),
+        pltpu.VMEM((tiles, BLK), f32),
     ]
+    values = pltpu.VMEM((tiles, TILE), f32)
     part = call(
-        middle_kernel,
+        functools.partial(middle_kernel, capacity),
         struct((slots, BLK), f32),
         [SMEM, SMEM] + [VMEM] * 4,
         VMEM,
-        scratch,
+        scratch + [values],
         10**9,
         (listed, size, recv, rows, split_tiles, sample_rows),
     )
@@ -396,11 +505,11 @@
     )
     rows = exchange(send)
     part = call(
-        last_kernel,
+        functools.partial(last_kernel, capacity),
         struct((slots * ROWS, BLK), f32),
         [SMEM, SMEM] + [VMEM] * 5,
         VMEM,
-        scratch,
+        scratch + [pltpu.VMEM((tiles, 16, TILE), bf16), values],
         10**9,
         (listed, size, recv, rows, split_tiles, sample_rows, samples),
     )

time: 201 us -> 173 us (0.86)
  blocking collectives: 113 us -> 93.3 us
  other arithmetic: 5.19 us -> 0 us
  local copies, waits for them, and re-layouts: 2.74 us -> 0 us
    all_to_all x5, blocking collectives: 113 us -> 93.3 us  [exchange(): lax.all_to_all(values.reshape(devices, rows, BLK), 'dev', split_axis=0, c...]
    convert_element_type x1 -> x0, other arithmetic: 5.19 us -> none  [local(): asked = recv.reshape(slots, ROWS, BLK)[:, 3, 0].astype(jnp.int32)]
    unnamed x4 -> x0, local copies, waits for them, and re-layouts: 2.74 us -> none
where the time goes in v2:
time: 173 us; the launch traced here: 172 us
  blocking collectives  93.3 us (54%)
  Pallas kernels  57.9 us (33%)
  waiting for transfers between devices  12.2 us (7%)
  starting transfers between devices  7.46 us (4%)
    all_to_all x5, blocking collectives, exchange(): lax.all_to_all(values.reshape(devices, rows, BLK), 'dev', split_axis=0, c...  93.3 us
    pallas_call x8, Pallas kernels, call(): pl.pallas_call(kernel, out_shape=out_shape, in_specs=in_specs, out_specs=...  57.9 us
    all_to_all x1, waiting for transfers between devices, exchange(): lax.all_to_all(values.reshape(devices, rows, BLK), 'dev', split_axis=0, c...  12.2 us
    all_to_all x1, starting transfers between devices, exchange(): lax.all_to_all(values.reshape(devices, rows, BLK), 'dev', split_axis=0, c...  7.46 us
  transfers between devices with their start and end apart: 1, of which 1 were waited for; matrix products, arithmetic and copies ran while one was open for 0% of the time, Pallas kernels for 2%

profile of v2, /device:TPU:0, one launch (start us, length us, event | category | flops | bytes accessed | tf_op | source)
XLA Modules:
  0.0 171.5 jit_solution(4520214099936072579)
XLA Ops:
  0.6 2.5 %shard_map.104 = (f32[1024,128]{1,0:T(8,128)}, s32[128]{0:T(128)}) custom-call(s32[4,32]{1,0:T(4,128)} %bitcast.32, s32[4,32]{1,0:T(4,128)} %bitcast.33, s32[32]{0:T(128)} %live_ref.7, f32[3,4096]{1,0:T(4,128)} %pos_ref.3), custom_call_target="tpu_custom_call" | custom-call | flops 1000000 | bytes 50304 | tf_op jit(solution)/shard_map/pallas_call | solution.py:34
  3.1 7.5 %all-to-all-start = ((f32[32,32,128]{2,1,0:T(8,128)}), f32[32,32,128]{2,1,0:T(8,128)}, u32[]{:S(2)}, u32[]{:S(2)}) async-start(f32[32,32,128]{2,1,0:T(8,128)} %bitcast.21), calls=%async_computation | async-start | bytes 1048576 | tf_op jit(solution)/shard_map/all_to_all | solution.py:426
  10.6 3.4 %shard_map.105.tiles_ref = bf16[64,32,512]{2,1,0:T(8,128)(2,1)} custom-call(f32[3,32768]{1,0:T(4,128)} %sample_ref.3), custom_call_target="tpu_custom_call" | custom-call | flops 10000000 | bytes 393216 | tf_op jit(solution)/shard_map/pallas_call | solution.py:34
  14.0 12.2 %all-to-all-done = f32[32,32,128]{2,1,0:T(8,128)} async-done(((f32[32,32,128]{2,1,0:T(8,128)}), f32[32,32,128]{2,1,0:T(8,128)}, u32[]{:S(2)}, u32[]{:S(2)}) %all-to-all-start) | async-done | bytes 524320 | tf_op jit(solution)/shard_map/all_to_all | solution.py:426
  26.2 12.6 %shard_map.106 = (f32[256,128]{1,0:T(8,128)}, s32[3,288]{1,0:T(4,128)}, s32[2]{0:T(128)}) custom-call(f32[1024,128]{1,0:T(8,128)} %bitcast.3.recv_ref, bf16[64,32,512]{2,1,0:T(8,128)(2,1)} %shard_map.105.tiles_ref, f32[256,128]{1,0:T(8,128)} %bitcast.34), custom_call_target="tpu_custom_call" | custom-call | flops 1000000000 | bytes 2752512 | tf_op jit(solution)/shard_map/pallas_call | solution.py:34
  38.9 17.3 %all_to_all.30 = f32[32,8,128]{2,1,0:T(8,128)} all-to-all(f32[32,8,128]{2,1,0:T(8,128)} %bitcast.26), channel_id=1, replica_groups=mesh['dev'=32] {'dev'}, dimensions={0} | all-to-all | bytes 262144 | tf_op jit(solution)/shard_map/all_to_all | solution.py:426
  56.1 1.8 %shard_map.107 = (f32[256,128]{1,0:T(8,128)}, f32[32,128]{1,0:T(8,128)}) custom-call(s32[128]{0:T(128)} %get-tuple-element.10.slot_ref, s32[32]{0:T(128)} %live_ref.7, f32[256,128]{1,0:T(8,128)} %bitcast.22, f32[32,128]{1,0:T(8,128)} %bitcast.30), custom_call_target="tpu_custom_call" | custom-call | flops 1000000 | bytes 148096 | tf_op jit(solution)/shard_map/pallas_call | solution.py:34
  58.0 11.5 %all_to_all.31 = f32[32,8,128]{2,1,0:T(8,128)} all-to-all(f32[32,8,128]{2,1,0:T(8,128)} %bitcast.27), channel_id=1, replica_groups=mesh['dev'=32] {'dev'}, dimensions={0} | all-to-all | bytes 262144 | tf_op jit(solution)/shard_map/all_to_all | solution.py:426
  69.4 12.9 %shard_map.108 = f32[256,128]{1,0:T(8,128)} custom-call(s32[3,288]{1,0:T(4,128)} %get-tuple-element.12.list_ref, s32[2]{0:T(128)} %get-tuple-element.13.size_ref, f32[1024,128]{1,0:T(8,128)} %bitcast.3.recv_ref, f32[256,128]{1,0:T(8,128)} %bitcast.28, bf16[64,32,512]{2,1,0:T(8,128)(2,1)} %shard_map.105.tiles_ref, f32[256,128]{1,0:T(8,128)} %bitcast.23), custom_call_target="tpu_custom_call" | custom-call | flops 1000000000 | bytes 2887048 | tf_op jit(solution)/shard_map/pallas_call | solution.py:34
  82.3 19.7 %all_to_all.32 = f32[32,8,128]{2,1,0:T(8,128)} all-to-all(f32[32,8,128]{2,1,0:T(8,128)} %bitcast.29), channel_id=1, replica_groups=mesh['dev'=32] {'dev'}, dimensions={0} | all-to-all | bytes 262144 | tf_op jit(solution)/shard_map/all_to_all | solution.py:426
  102.1 1.8 %shard_map.109 = (f32[256,128]{1,0:T(8,128)}, f32[32,128]{1,0:T(8,128)}) custom-call(s32[128]{0:T(128)} %get-tuple-element.10.slot_ref, s32[32]{0:T(128)} %live_ref.7, f32[256,128]{1,0:T(8,128)} %bitcast.20, f32[32,128]{1,0:T(8,128)} %bitcast.31, f32[32,128]{1,0:T(8,128)} %get-tuple-element.16.old_ref), custom_call_target="tpu_custom_call" | custom-call | flops 1000000 | bytes 164480 | tf_op jit(solution)/shard_map/pallas_call | solution.py:34
  103.9 11.5 %all_to_all.33 = f32[32,8,128]{2,1,0:T(8,128)} all-to-all(f32[32,8,128]{2,1,0:T(8,128)} %bitcast.25), channel_id=1, replica_groups=mesh['dev'=32] {'dev'}, dimensions={0} | all-to-all | bytes 262144 | tf_op jit(solution)/shard_map/all_to_all | solution.py:426
  115.4 20.8 %shard_map.110 = f32[1024,128]{1,0:T(8,128)} custom-call(s32[3,288]{1,0:T(4,128)} %get-tuple-element.12.list_ref, s32[2]{0:T(128)} %get-tuple-element.13.size_ref, f32[1024,128]{1,0:T(8,128)} %bitcast.3.recv_ref, f32[256,128]{1,0:T(8,128)} %bitcast.19, bf16[64,32,512]{2,1,0:T(8,128)(2,1)} %shard_map.105.tiles_ref, f32[256,128]{1,0:T(8,128)} %bitcast.24, ...), custom_call_target="tpu_custom_call" | custom-call | flops 1000000000 | bytes 3280264 | tf_op jit(solution)/shard_map/pallas_call | solution.py:34
  136.1 33.4 %all_to_all.34 = f32[32,32,128]{2,1,0:T(8,128)} all-to-all(f32[32,32,128]{2,1,0:T(8,128)} %bitcast.17), channel_id=1, replica_groups=mesh['dev'=32] {'dev'}, dimensions={0} | all-to-all | bytes 1048576 | tf_op jit(solution)/shard_map/all_to_all | solution.py:426
  169.6 2.0 %shard_map.111 = (f32[3,4096]{1,0:T(4,128)}, f32[3,4096]{1,0:T(4,128)}) custom-call(s32[128]{0:T(128)} %get-tuple-element.10.slot_ref, s32[32]{0:T(128)} %live_ref.7, f32[1024,128]{1,0:T(8,128)} %bitcast.18, f32[3,4096]{1,0:T(4,128)} %pos_ref.3, f32[3,4096]{1,0:T(4,128)} %vel_ref.1), custom_call_target="tpu_custom_call" | custom-call | flops 1000000 | bytes 623232 | tf_op jit(solution)/shard_map/pallas_call | solution.py:34
Async XLA Ops:
  3.1 23.1 %all-to-all-start = ((f32[32,32,128]{2,1,0:T(8,128)}), f32[32,32,128]{2,1,0:T(8,128)}, u32[]{:S(2)}, u32[]{:S(2)}) async-start(f32[32,32,128]{2,1,0:T(8,128)} %bitcast.21), calls=%async_computation | async-start | bytes 1048576 | tf_op jit(solution)/shard_map/all_to_all | solution.py:426

commit v3 on v2

--- a/solution.py
+++ b/solution.py
@@ -26,6 +26,7 @@
 f32 = jnp.float32
 bf16 = jnp.bfloat16
 VMEM = pl.BlockSpec(memory_space=pltpu.VMEM)
+ANY = pl.BlockSpec(memory_space=pl.ANY)
 SMEM = pl.BlockSpec(memory_space=pltpu.SMEM)
 
 
@@ -165,7 +166,7 @@
     second = jnp.where(one, 1.0, jnp.where(row == 3, middle, high))
     third = jnp.where(one, 1.0, jnp.where(row < 3, middle, low))
     zero = jnp.zeros_like(first)
-    return jnp.concatenate([first, second, third, zero], 0).T.astype(bf16)
+    return jnp.concatenate([first, second, third, zero], 0).astype(bf16).T
 
 
 def fold_lanes(value):
@@ -179,26 +180,42 @@
     return jnp.dot(left, right, preferred_element_type=f32)
 
 
+def unpack(list_ref, index, capacity):
+    code = list_ref[index]
+    slot = lax.shift_right_logical(code, 16)
+    device = lax.div(slot, capacity)
+    return slot, code & 0xFFFF, slot + device * (capacity * (ROWS - 1))
+
+
+def listed(list_ref, g, capacity):
+    slots = [unpack(list_ref, g * G + k, capacity) for k in range(G)]
+    return [list(item) for item in zip(*slots)]
+
+
 def row_first_kernel(
     capacity,
     recv_ref,
-    tiles_ref,
+    tiles_any,
     pot_ref,
     part_ref,
     list_ref,
     size_ref,
+    tiles_ref,
     beta_ref,
     top_ref,
+    left_ref,
     asked_ref,
     tile_ref,
-    sem,
+    sems,
 ):
+    load = pltpu.make_async_copy(tiles_any, tiles_ref, sems.at[0])
+    load.start()
     devices = asked_ref.shape[0]
     lane = lax.broadcasted_iota(jnp.int32, (devices, capacity, BLK), 2)
     rank = lax.broadcasted_iota(jnp.int32, (devices, capacity, BLK), 1)
     asked = recv_ref[...].reshape(devices, ROWS * capacity, BLK)[:, 3 * capacity :, :]
     asked_ref[...] = jnp.sum(jnp.where(lane == rank, asked, 0.0), axis=1).astype(jnp.int32)
-    copy = pltpu.make_async_copy(asked_ref, tile_ref, sem)
+    copy = pltpu.make_async_copy(asked_ref, tile_ref, sems.at[1])
     copy.start()
 
     pot = lanes_of(pot_ref) * SCALE
@@ -211,32 +228,36 @@
     def compact(device, count):
         for k in range(capacity):
             tile = tile_ref[device, k]
-            list_ref[0, count] = device * capacity + k
-            list_ref[1, count] = tile
-            list_ref[2, count] = device * (capacity * ROWS) + k
+            list_ref[count] = ((device * capacity + k) << 16) + jnp.maximum(tile, 0)
             count = count + jnp.where(tile >= 0, 1, 0)
         return count
 
     count = lax.fori_loop(0, devices, compact, 0)
-    size_ref[0] = (count + G - 1) // G
+    groups = (count + G - 1) // G
+    size_ref[0] = groups
     size_ref[1] = count
     for k in range(G):
-        for i in range(3):
-            list_ref[i, count + k] = list_ref[i, 0]
+        list_ref[count + k] = list_ref[0]
+
+    def prepare(g):
+        slot, tile, base = listed(list_ref, g, capacity)
+        for k in range(G):
+            left_ref[k] = particle_rows(recv_ref, (base[k], capacity), ROW_SHIFT, row)
+
+    prepare(0)
+    load.wait()
 
     def body(g, carry):
-        slot = [list_ref[0, g * G + k] for k in range(G)]
-        tile = [list_ref[1, g * G + k] for k in range(G)]
-        base = [list_ref[2, g * G + k] for k in range(G)]
-        left = [particle_rows(recv_ref, (i, capacity), ROW_SHIFT, row) for i in base]
-        raised = [product(a, tiles_ref[t]) for a, t in zip(left, tile)]
+        slot, tile, base = listed(list_ref, g, capacity)
+        raised = [product(left_ref[k], tiles_ref[tile[k]]) for k in range(G)]
         power = [jnp.exp2(a + beta_ref[pl.ds(t, 1), :]) for a, t in zip(raised, tile)]
+        prepare(jnp.minimum(g + 1, groups - 1))
         total = [jnp.sum(fold_lanes(a).T, axis=0, keepdims=True) for a in power]
         for k in range(G):
             part_ref[pl.ds(slot[k], 1), :] = jnp.log2(total[k]) + top_ref[pl.ds(tile[k], 1), :]
         return carry
 
-    lax.fori_loop(0, size_ref[0], body, 0)
+    lax.fori_loop(0, groups, body, 0)
 
 
 def iterate(
@@ -245,76 +266,81 @@
     store,
     list_ref,
     size_ref,
+    recv_any,
+    rows_ref,
+    tiles_any,
+    mass_ref,
     recv_ref,
-    rows_ref,
     tiles_ref,
-    mass_ref,
     kept_ref,
+    left_ref,
     sums_ref,
     peak_ref,
+    sems,
     weight_ref,
 ):
+    load_recv = pltpu.make_async_copy(recv_any, recv_ref, sems.at[0])
+    load_recv.start()
+    load_tiles = pltpu.make_async_copy(tiles_any, tiles_ref, sems.at[1])
+    load_tiles.start()
     tiles = tiles_ref.shape[0]
     groups, count = size_ref[0], size_ref[1]
     limit = jnp.minimum(groups, KEPT // G)
     row = lax.broadcasted_iota(jnp.int32, (8, BLK), 0)
     peak_ref[...] = jnp.full(peak_ref.shape, NEGATIVE, f32)
+    sums_ref[...] = jnp.zeros(sums_ref.shape, f32)
 
     def find(g, carry):
-        for k in range(G):
-            at = pl.ds(list_ref[1, g * G + k], 1)
-            peak_ref[at, :] = jnp.maximum(
-                peak_ref[at, :], rows_ref[pl.ds(list_ref[0, g * G + k], 1), :]
-            )
+        slot, tile, base = listed(list_ref, g, capacity)
+        for k in range(G):
+            at = pl.ds(tile[k], 1)
+            peak_ref[at, :] = jnp.maximum(peak_ref[at, :], rows_ref[pl.ds(slot[k], 1), :])
         return carry
 
     lax.fori_loop(0, groups, find, 0)
     peak = jnp.max(peak_ref[...], axis=1, keepdims=True)
     peak_ref[...] = jnp.broadcast_to(COL_SHIFT - peak, peak_ref.shape)
-    sums_ref[...] = jnp.zeros(sums_ref.shape, f32)
-
-    def powers(g):
-        slot = [list_ref[0, g * G + k] for k in range(G)]
-        tile = [list_ref[1, g * G + k] for k in range(G)]
-        base = [list_ref[2, g * G + k] for k in range(G)]
-        extra = [
-            jnp.broadcast_to(rows_ref[pl.ds(s, 1), :] + peak_ref[pl.ds(t, 1), :], (8, BLK))
-            for s, t in zip(slot, tile)
-        ]
-        left = [particle_rows(recv_ref, (i, capacity), e, row) for i, e in zip(base, extra)]
-        raised = [product(a, tiles_ref[t]) for a, t in zip(left, tile)]
-        return slot, tile, [jnp.exp2(a) for a in raised]
-
-    def add_up(g, tile, power):
-        total = [jnp.sum(a.reshape(BLK // 8, 8, TILE), axis=0) for a in power]
-        for k in range(G):
+
+    def prepare(g):
+        slot, tile, base = listed(list_ref, g, capacity)
+        for k in range(G):
+            extra = rows_ref[pl.ds(slot[k], 1), :] + peak_ref[pl.ds(tile[k], 1), :]
+            extra = jnp.broadcast_to(extra, (8, BLK))
+            left_ref[k] = particle_rows(recv_ref, (base[k], capacity), extra, row)
+
+    def powers(tile):
+        raised = [product(left_ref[k], tiles_ref[tile[k]]) for k in range(G)]
+        return [jnp.exp2(a) for a in raised]
+
+    def first(keep, g, carry):
+        slot, tile, base = listed(list_ref, g, capacity)
+        power = powers(tile)
+        prepare(jnp.minimum(g + 1, groups - 1))
+        for k in range(G):
+            if keep:
+                kept_ref[g * G + k] = power[k]
             into = jnp.where(g * G + k < count, tile[k], tiles)
-            sums_ref[into] += total[k]
-
-    def first_kept(g, carry):
-        slot, tile, power = powers(g)
-        for k in range(G):
-            kept_ref[g * G + k] = power[k]
-        add_up(g, tile, power)
-        return carry
-
-    def first_rest(g, carry):
-        slot, tile, power = powers(g)
-        add_up(g, tile, power)
-        return carry
-
-    lax.fori_loop(0, limit, first_kept, 0)
-    lax.fori_loop(limit, groups, first_rest, 0)
+            sums_ref[into] += jnp.sum(power[k].reshape(BLK // 8, 8, TILE), axis=0)
+        return carry
+
+    load_recv.wait()
+    prepare(0)
+    load_tiles.wait()
+    lax.fori_loop(0, limit, functools.partial(first, True), 0)
+    lax.fori_loop(limit, groups, functools.partial(first, False), 0)
     total = jnp.sum(sums_ref[0:tiles], axis=1)
     weights(lanes_of(mass_ref) / total, weight_ref)
 
     def second_kept(g, carry):
-        for k in range(G):
-            store(list_ref[0, g * G + k], list_ref[1, g * G + k], kept_ref[g * G + k], weight_ref)
+        slot, tile, base = listed(list_ref, g, capacity)
+        for k in range(G):
+            store(slot[k], tile[k], kept_ref[g * G + k], weight_ref)
         return carry
 
     def second_rest(g, carry):
-        slot, tile, power = powers(g)
+        slot, tile, base = listed(list_ref, g, capacity)
+        prepare(g)
+        power = powers(tile)
         for k in range(G):
             store(slot[k], tile[k], power[k], weight_ref)
         return carry
@@ -450,17 +476,19 @@
     mass_rows = masses.reshape(blocks, BLK)
     sample_rows = sample_mass.reshape(tiles * CHUNKS, BLK)
     pot_rows = start_potential.reshape(tiles * CHUNKS, BLK)
-    part, listed, size = call(
+    part, order, size = call(
         functools.partial(row_first_kernel, capacity),
-        (struct((slots, BLK), f32), struct((3, slots + 2 * G), jnp.int32), struct((2,), jnp.int32)),
-        [VMEM, VMEM, VMEM],
+        (struct((slots, BLK), f32), struct((slots + 2 * G,), jnp.int32), struct((2,), jnp.int32)),
+        [VMEM, ANY, VMEM],
         (VMEM, SMEM, SMEM),
         [
+            pltpu.VMEM((tiles, DEPTH, TILE), bf16),
             pltpu.VMEM((tiles, TILE), f32),
             pltpu.VMEM((tiles, BLK), f32),
+            pltpu.VMEM((G, BLK, DEPTH), bf16),
             pltpu.VMEM((devices, BLK), jnp.int32),
             pltpu.SMEM((devices, BLK), jnp.int32),
-            pltpu.SemaphoreType.DMA,
+            pltpu.SemaphoreType.DMA((2,)),
         ],
         10**9,
         (recv, split_tiles, pot_rows),
@@ -479,19 +507,23 @@
     )
     rows = exchange(send)
     scratch = [
+        pltpu.VMEM((slots * ROWS, BLK), f32),
+        pltpu.VMEM((tiles, DEPTH, TILE), bf16),
         pltpu.VMEM((min(KEPT, slots), BLK, TILE), f32),
+        pltpu.VMEM((G, BLK, DEPTH), bf16),
         pltpu.VMEM((tiles + 1, 8, TILE), f32),
         pltpu.VMEM((tiles, BLK), f32),
+        pltpu.SemaphoreType.DMA((2,)),
     ]
     values = pltpu.VMEM((tiles, TILE), f32)
     part = call(
         functools.partial(middle_kernel, capacity),
         struct((slots, BLK), f32),
-        [SMEM, SMEM] + [VMEM] * 4,
+        [SMEM, SMEM, ANY, VMEM, ANY, VMEM],
         VMEM,
         scratch + [values],
         10**9,
-        (listed, size, recv, rows, split_tiles, sample_rows),
+        (order, size, recv, rows, split_tiles, sample_rows),
     )
     part = exchange(part)
     send, row = call(
@@ -507,11 +539,11 @@
     part = call(
         functools.partial(last_kernel, capacity),
         struct((slots * ROWS, BLK), f32),
-        [SMEM, SMEM] + [VMEM] * 5,
+        [SMEM, SMEM, ANY, VMEM, ANY, VMEM, VMEM],
         VMEM,
         scratch + [pltpu.VMEM((tiles, 16, TILE), bf16), values],
         10**9,
-        (listed, size, recv, rows, split_tiles, sample_rows, samples),
+        (order, size, recv, rows, split_tiles, sample_rows, samples),
     )
     part = exchange(part)
     return call(

time: 173 us -> 164 us (0.948); the launches traced: 172 us -> 166 us
  Pallas kernels: 57.9 us -> 39.5 us
  blocking collectives: 93.3 us -> 106 us
    pallas_call x8, Pallas kernels: 57.9 us -> 39.5 us  [call(): pl.pallas_call(kernel, out_shape=out_shape, in_specs=in_specs, out_specs=...]
    all_to_all x5, blocking collectives: 93.3 us -> 106 us  [exchange(): lax.all_to_all(values.reshape(devices, rows, BLK), 'dev', split_axis=0, c...]
where the time goes in v3:
time: 164 us; the launch traced here: 166 us
  blocking collectives  106 us (65%)
  Pallas kernels  39.5 us (24%)
  waiting for transfers between devices  12.2 us (7%)
  starting transfers between devices  7.46 us (5%)
    all_to_all x5, blocking collectives, exchange(): lax.all_to_all(values.reshape(devices, rows, BLK), 'dev', split_axis=0, c...  106 us
    pallas_call x8, Pallas kernels, call(): pl.pallas_call(kernel, out_shape=out_shape, in_specs=in_specs, out_specs=...  39.5 us
    all_to_all x1, waiting for transfers between devices, exchange(): lax.all_to_all(values.reshape(devices, rows, BLK), 'dev', split_axis=0, c...  12.2 us
    all_to_all x1, starting transfers between devices, exchange(): lax.all_to_all(values.reshape(devices, rows, BLK), 'dev', split_axis=0, c...  7.46 us
  transfers between devices with their start and end apart: 1, of which 1 were waited for; matrix products, arithmetic and copies ran while one was open for 0% of the time, Pallas kernels for 2%

profile of v3, /device:TPU:0, one launch (start us, length us, event | category | flops | bytes accessed | tf_op | source)
XLA Modules:
  0.0 166.1 jit_solution(11052638364732061086)
XLA Ops:
  0.6 2.5 %shard_map.104 = (f32[1024,128]{1,0:T(8,128)}, s32[128]{0:T(128)}) custom-call(s32[4,32]{1,0:T(4,128)} %bitcast.32, s32[4,32]{1,0:T(4,128)} %bitcast.33, s32[32]{0:T(128)} %live_ref.7, f32[3,4096]{1,0:T(4,128)} %pos_ref.3), custom_call_target="tpu_custom_call" | custom-call | flops 1000000 | bytes 50304 | tf_op jit(solution)/shard_map/pallas_call | solution.py:35
  3.1 7.5 %all-to-all-start = ((f32[32,32,128]{2,1,0:T(8,128)}), f32[32,32,128]{2,1,0:T(8,128)}, u32[]{:S(2)}, u32[]{:S(2)}) async-start(f32[32,32,128]{2,1,0:T(8,128)} %bitcast.20), calls=%async_computation | async-start | bytes 1048576 | tf_op jit(solution)/shard_map/all_to_all | solution.py:452
  10.6 3.4 %shard_map.105.tiles_any.tiles_ref = bf16[64,32,512]{2,1,0:T(8,128)(2,1)} custom-call(f32[3,32768]{1,0:T(4,128)} %sample_ref.3), custom_call_target="tpu_custom_call" | custom-call | flops 10000000 | bytes 393216 | tf_op jit(solution)/shard_map/pallas_call | solution.py:35
  14.0 12.2 %all-to-all-done = f32[32,32,128]{2,1,0:T(8,128)} async-done(((f32[32,32,128]{2,1,0:T(8,128)}), f32[32,32,128]{2,1,0:T(8,128)}, u32[]{:S(2)}, u32[]{:S(2)}) %all-to-all-start) | async-done | bytes 524320 | tf_op jit(solution)/shard_map/all_to_all | solution.py:452
  26.2 7.5 %shard_map.106 = (f32[256,128]{1,0:T(8,128)}, s32[288]{0:T(512)}, s32[2]{0:T(128)}) custom-call(f32[1024,128]{1,0:T(8,128)} %bitcast.3.recv_ref, bf16[64,32,512]{2,1,0:T(8,128)(2,1)} %shard_map.105.tiles_any.tiles_ref, f32[256,128]{1,0:T(8,128)} %bitcast.34), custom_call_target="tpu_custom_call" | custom-call | flops 1000000000 | bytes 2752512 | tf_op jit(solution)/shard_map/pallas_call | solution.py:35
  33.7 20.6 %all_to_all.30 = f32[32,8,128]{2,1,0:T(8,128)} all-to-all(f32[32,8,128]{2,1,0:T(8,128)} %bitcast.24), channel_id=1, replica_groups=mesh['dev'=32] {'dev'}, dimensions={0} | all-to-all | bytes 262144 | tf_op jit(solution)/shard_map/all_to_all | solution.py:452
  54.3 1.8 %shard_map.107 = (f32[256,128]{1,0:T(8,128)}, f32[32,128]{1,0:T(8,128)}) custom-call(s32[128]{0:T(128)} %get-tuple-element.10.slot_ref, s32[32]{0:T(128)} %live_ref.7, f32[256,128]{1,0:T(8,128)} %bitcast.21, f32[32,128]{1,0:T(8,128)} %bitcast.30), custom_call_target="tpu_custom_call" | custom-call | flops 1000000 | bytes 148096 | tf_op jit(solution)/shard_map/pallas_call | solution.py:35
  56.2 11.5 %all_to_all.31 = f32[32,8,128]{2,1,0:T(8,128)} all-to-all(f32[32,8,128]{2,1,0:T(8,128)} %bitcast.25), channel_id=1, replica_groups=mesh['dev'=32] {'dev'}, dimensions={0} | all-to-all | bytes 262144 | tf_op jit(solution)/shard_map/all_to_all | solution.py:452
  67.6 8.0 %shard_map.108 = f32[256,128]{1,0:T(8,128)} custom-call(s32[288]{0:T(512)} %get-tuple-element.12.list_ref, s32[2]{0:T(128)} %get-tuple-element.13.size_ref, f32[1024,128]{1,0:T(8,128)} %bitcast.3.recv_ref, f32[256,128]{1,0:T(8,128)} %bitcast.26, bf16[64,32,512]{2,1,0:T(8,128)(2,1)} %shard_map.105.tiles_any.tiles_ref, f32[256,128]{1,0:T(8,128)} %bitcast.28), custom_call_target="tpu_custom_call" | custom-call | flops 1000000000 | bytes 2884744 | tf_op jit(solution)/shard_map/pallas_call | solution.py:35
  75.6 22.7 %all_to_all.32 = f32[32,8,128]{2,1,0:T(8,128)} all-to-all(f32[32,8,128]{2,1,0:T(8,128)} %bitcast.27), channel_id=1, replica_groups=mesh['dev'=32] {'dev'}, dimensions={0} | all-to-all | bytes 262144 | tf_op jit(solution)/shard_map/all_to_all | solution.py:452
  98.3 1.8 %shard_map.109 = (f32[256,128]{1,0:T(8,128)}, f32[32,128]{1,0:T(8,128)}) custom-call(s32[128]{0:T(128)} %get-tuple-element.10.slot_ref, s32[32]{0:T(128)} %live_ref.7, f32[256,128]{1,0:T(8,128)} %bitcast.19, f32[32,128]{1,0:T(8,128)} %bitcast.31, f32[32,128]{1,0:T(8,128)} %get-tuple-element.16.old_ref), custom_call_target="tpu_custom_call" | custom-call | flops 1000000 | bytes 164480 | tf_op jit(solution)/shard_map/pallas_call | solution.py:35
  100.2 11.5 %all_to_all.33 = f32[32,8,128]{2,1,0:T(8,128)} all-to-all(f32[32,8,128]{2,1,0:T(8,128)} %bitcast.23), channel_id=1, replica_groups=mesh['dev'=32] {'dev'}, dimensions={0} | all-to-all | bytes 262144 | tf_op jit(solution)/shard_map/all_to_all | solution.py:452
  111.6 12.5 %shard_map.110 = f32[1024,128]{1,0:T(8,128)} custom-call(s32[288]{0:T(512)} %get-tuple-element.12.list_ref, s32[2]{0:T(128)} %get-tuple-element.13.size_ref, f32[1024,128]{1,0:T(8,128)} %bitcast.3.recv_ref, f32[256,128]{1,0:T(8,128)} %bitcast.22, bf16[64,32,512]{2,1,0:T(8,128)(2,1)} %shard_map.105.tiles_any.tiles_ref, f32[256,128]{1,0:T(8,128)} %bitcast.29, ...), custom_call_target="tpu_custom_call" | custom-call | flops 1000000000 | bytes 3277960 | tf_op jit(solution)/shard_map/pallas_call | solution.py:35
  124.1 40.0 %all_to_all.34 = f32[32,32,128]{2,1,0:T(8,128)} all-to-all(f32[32,32,128]{2,1,0:T(8,128)} %bitcast.18), channel_id=1, replica_groups=mesh['dev'=32] {'dev'}, dimensions={0} | all-to-all | bytes 1048576 | tf_op jit(solution)/shard_map/all_to_all | solution.py:452
  164.1 2.0 %shard_map.111 = (f32[3,4096]{1,0:T(4,128)}, f32[3,4096]{1,0:T(4,128)}) custom-call(s32[128]{0:T(128)} %get-tuple-element.10.slot_ref, s32[32]{0:T(128)} %live_ref.7, f32[1024,128]{1,0:T(8,128)} %bitcast.17, f32[3,4096]{1,0:T(4,128)} %pos_ref.3, f32[3,4096]{1,0:T(4,128)} %vel_ref.1), custom_call_target="tpu_custom_call" | custom-call | flops 1000000 | bytes 623232 | tf_op jit(solution)/shard_map/pallas_call | solution.py:35
Async XLA Ops:
  3.1 23.1 %all-to-all-start = ((f32[32,32,128]{2,1,0:T(8,128)}), f32[32,32,128]{2,1,0:T(8,128)}, u32[]{:S(2)}, u32[]{:S(2)}) async-start(f32[32,32,128]{2,1,0:T(8,128)} %bitcast.20), calls=%async_computation | async-start | bytes 1048576 | tf_op jit(solution)/shard_map/all_to_all | solution.py:452

commit v4 on v3

--- a/solution.py
+++ b/solution.py
@@ -30,7 +30,7 @@
 SMEM = pl.BlockSpec(memory_space=pltpu.SMEM)
 
 
-def call(kernel, out_shape, in_specs, out_specs, scratch, flops, args):
+def call(kernel, out_shape, in_specs, out_specs, scratch, flops, args, limit=67_000_000):
     size = sum(a.size * a.dtype.itemsize for a in args)
     return pl.pallas_call(
         kernel,
@@ -38,7 +38,7 @@
         in_specs=in_specs,
         out_specs=out_specs,
         scratch_shapes=scratch,
-        compiler_params=pltpu.CompilerParams(vmem_limit_bytes=67_000_000),
+        compiler_params=pltpu.CompilerParams(vmem_limit_bytes=limit),
         cost_estimate=pl.CostEstimate(flops=flops, bytes_accessed=size, transcendentals=0),
     )(*args)
 
@@ -462,6 +462,7 @@
         [pltpu.SMEM((devices,), jnp.int32)],
         10**6,
         (route_owner.T, route_tile.T, live_count, positions),
+        4 * 2**20,
     )
     recv = exchange(send)
     split_tiles = call(
@@ -472,6 +473,7 @@
         [],
         10**7,
         (samples,),
+        8 * 2**20,
     )
     mass_rows = masses.reshape(blocks, BLK)
     sample_rows = sample_mass.reshape(tiles * CHUNKS, BLK)
@@ -492,6 +494,7 @@
         ],
         10**9,
         (recv, split_tiles, pot_rows),
+        16 * 2**20,
     )
     part = exchange(part)
     row_scratch = [pltpu.VMEM((K, blocks, BLK), f32)]
@@ -504,6 +507,7 @@
         row_scratch,
         10**6,
         (slot, live_count, part, mass_rows),
+        4 * 2**20,
     )
     rows = exchange(send)
     scratch = [
@@ -534,6 +538,7 @@
         row_scratch,
         10**6,
         (slot, live_count, part, mass_rows, row),
+        4 * 2**20,
     )
     rows = exchange(send)
     part = call(
@@ -554,6 +559,7 @@
         [],
         10**6,
         (slot, live_count, part, positions, velocities),
+        4 * 2**20,
     )
 
 

time: 164 us -> 163 us (level)
  blocking collectives: 106 us -> 91.7 us
  Pallas kernels: 39.5 us -> 45.6 us
  local copies, waits for them, and re-layouts: 0 us -> 5.6 us
    all_to_all x5, blocking collectives: 106 us -> 91.7 us  [exchange(): lax.all_to_all(values.reshape(devices, rows, BLK), 'dev', split_axis=0, c...]
    pallas_call x8, Pallas kernels: 39.5 us -> 45.6 us  [call(): pl.pallas_call(kernel, out_shape=out_shape, in_specs=in_specs, out_specs=...]
    unnamed x0 -> x28, local copies, waits for them, and re-layouts: none -> 5.6 us
  transfers between devices with their start and end apart: 1 -> 1, of which waited for: 1 -> 1; matrix products, arithmetic and copies ran while one was open for 0% -> 0% of each run, Pallas kernels for 2% -> 1%
where the time goes in v4:
time: 163 us; the launch traced here: 165 us
  blocking collectives  91.7 us (56%)
  Pallas kernels  45.6 us (28%)
  waiting for transfers between devices  13.5 us (8%)
  starting transfers between devices  7.33 us (4%)
  local copies, waits for them, and re-layouts  5.6 us (3%)
    all_to_all x5, blocking collectives, exchange(): lax.all_to_all(values.reshape(devices, rows, BLK), 'dev', split_axis=0, c...  91.7 us
    pallas_call x8, Pallas kernels, call(): pl.pallas_call(kernel, out_shape=out_shape, in_specs=in_specs, out_specs=...  45.6 us
    all_to_all x1, waiting for transfers between devices, exchange(): lax.all_to_all(values.reshape(devices, rows, BLK), 'dev', split_axis=0, c...  13.5 us
    all_to_all x1, starting transfers between devices, exchange(): lax.all_to_all(values.reshape(devices, rows, BLK), 'dev', split_axis=0, c...  7.33 us
    unnamed x28, local copies, waits for them, and re-layouts  5.6 us
  transfers between devices with their start and end apart: 1, of which 1 were waited for; matrix products, arithmetic and copies ran while one was open for 0% of the time, Pallas kernels for 1%

profile of v4, /device:TPU:0, one launch (start us, length us, event | category | flops | bytes accessed | tf_op | source)
XLA Modules:
  0.0 164.6 jit_solution(10565971832967587143)
XLA Ops:
  0.6 0.0 copy-start.3
  0.6 0.8 copy-done.3
  1.5 0.7 copy-done.7
  2.1 0.7 copy-done.10
  2.8 0.7 copy-done.11
  3.5 2.3 %shard_map.104 = (f32[1024,128]{1,0:T(8,128)}, s32[128]{0:T(128)S(1)}) custom-call(s32[4,32]{1,0:T(4,128)S(1)} %bitcast.28, s32[4,32]{1,0:T(4,128)S(1)} %bitcast.29, s32[32]{0:T(128)S(1)} %copy-done.7, f32[3,4096]{1,0:T(4,128)S(1)} %copy-done.3), custom_call_target="tpu_custom_call" | custom-call | flops 1000000 | bytes 50304 | tf_op jit(solution)/shard_map/pallas_call | solution.py:35
  5.8 7.3 %all-to-all-start = ((f32[32,32,128]{2,1,0:T(8,128)}), f32[32,32,128]{2,1,0:T(8,128)S(1)}, u32[]{:S(2)}, u32[]{:S(2)}) async-start(f32[32,32,128]{2,1,0:T(8,128)} %bitcast.2), calls=%async_computation | async-start | bytes 1048576 | tf_op jit(solution)/shard_map/all_to_all | solution.py:452
  13.1 0.0 copy-start.1
  13.1 1.0 copy-done.1
  14.1 1.0 shard_map.105.tiles_any.tiles_ref
  15.2 0.0 copy-start
  15.2 0.0 copy-start.6
  15.2 0.0 copy-start.8
  15.2 13.5 %all-to-all-done = f32[32,32,128]{2,1,0:T(8,128)S(1)} async-done(((f32[32,32,128]{2,1,0:T(8,128)}), f32[32,32,128]{2,1,0:T(8,128)S(1)}, u32[]{:S(2)}, u32[]{:S(2)}) %all-to-all-start) | async-done | bytes 524320 | tf_op jit(solution)/shard_map/all_to_all | solution.py:452
  28.7 0.0 copy-done.13
  28.7 9.3 %shard_map.106 = (f32[256,128]{1,0:T(8,128)S(1)}, s32[288]{0:T(512)S(1)}, s32[2]{0:T(128)S(1)}) custom-call(f32[1024,128]{1,0:T(8,128)S(1)} %bitcast.18, bf16[64,32,512]{2,1,0:T(8,128)(2,1)S(1)} %shard_map.105.tiles_any.tiles_ref, f32[256,128]{1,0:T(8,128)S(1)} %bitcast.30), custom_call_target="tpu_custom_call" | custom-call | flops 1000000000 | bytes 2752512 | tf_op jit(solution)/shard_map/pallas_call | solution.py:35
  38.0 0.0 copy-start.12
  38.0 0.0 copy-start.9
  38.0 16.7 %all_to_all.30 = f32[32,8,128]{2,1,0:T(8,128)S(1)} all-to-all(f32[32,8,128]{2,1,0:T(8,128)S(1)} %bitcast.24), channel_id=1, replica_groups=mesh['dev'=32] {'dev'}, dimensions={0} | all-to-all | bytes 262144 | tf_op jit(solution)/shard_map/all_to_all | solution.py:452
  54.8 0.0 copy-done.12
  54.8 0.8 shard_map.107
  55.6 10.6 %all_to_all.31 = f32[32,8,128]{2,1,0:T(8,128)} all-to-all(f32[32,8,128]{2,1,0:T(8,128)S(1)} %bitcast.25), channel_id=1, replica_groups=mesh['dev'=32] {'dev'}, dimensions={0} | all-to-all | bytes 262144 | tf_op jit(solution)/shard_map/all_to_all | solution.py:452
  66.2 0.0 copy-done
  66.2 11.2 %shard_map.108 = f32[256,128]{1,0:T(8,128)} custom-call(s32[288]{0:T(512)} %copy-done.9, s32[2]{0:T(128)} %copy-done.12, f32[1024,128]{1,0:T(8,128)} %bitcast.19, f32[256,128]{1,0:T(8,128)} %bitcast.33, bf16[64,32,512]{2,1,0:T(8,128)(2,1)} %copy-done, f32[256,128]{1,0:T(8,128)} %bitcast.35), custom_call_target="tpu_custom_call" | custom-call | flops 1000000000 | bytes 2884744 | tf_op jit(solution)/shard_map/pallas_call | solution.py:35
  77.4 19.6 %all_to_all.32 = f32[32,8,128]{2,1,0:T(8,128)S(1)} all-to-all(f32[32,8,128]{2,1,0:T(8,128)} %bitcast.34), channel_id=1, replica_groups=mesh['dev'=32] {'dev'}, dimensions={0} | all-to-all | bytes 262144 | tf_op jit(solution)/shard_map/all_to_all | solution.py:452
  97.0 1.4 shard_map.109
  98.4 10.6 %all_to_all.33 = f32[32,8,128]{2,1,0:T(8,128)} all-to-all(f32[32,8,128]{2,1,0:T(8,128)S(1)} %bitcast.23), channel_id=1, replica_groups=mesh['dev'=32] {'dev'}, dimensions={0} | all-to-all | bytes 262144 | tf_op jit(solution)/shard_map/all_to_all | solution.py:452
  109.0 18.3 %shard_map.110 = f32[1024,128]{1,0:T(8,128)} custom-call(s32[288]{0:T(512)} %copy-done.9, s32[2]{0:T(128)} %copy-done.12, f32[1024,128]{1,0:T(8,128)} %bitcast.20, f32[256,128]{1,0:T(8,128)} %bitcast.32, bf16[64,32,512]{2,1,0:T(8,128)(2,1)} %copy-done, f32[256,128]{1,0:T(8,128)} %bitcast.36, f32[3,32768]{1,0:T(4,128)} %sample_ref.3), custom_call_target="tpu_custom_call" | custom-call | flops 1000000000 | bytes 3277960 | tf_op jit(solution)/shard_map/pallas_call | solution.py:35
  127.2 34.2 %all_to_all.34 = f32[32,32,128]{2,1,0:T(8,128)S(1)} all-to-all(f32[32,32,128]{2,1,0:T(8,128)} %bitcast.31), channel_id=1, replica_groups=mesh['dev'=32] {'dev'}, dimensions={0} | all-to-all | bytes 1048576 | tf_op jit(solution)/shard_map/all_to_all | solution.py:452
  161.5 0.8 copy-done.4
  162.3 0.8 copy-done.5
  163.2 1.4 shard_map.111
  (11 shorter events, 0.0 us)
Async XLA Ops:
  0.6 0.8 copy-start.3
  1.5 0.7 copy-start.7
  2.1 0.7 copy-start.10
  2.8 0.7 copy-start.11
  3.5 25.2 %copy-start.13 = (f32[32768]{0:T(1024)S(1)}, f32[32768]{0:T(1024)}, u32[]{:S(2)}) copy-start(f32[32768]{0:T(1024)} %param.14) | copy-start | bytes 393220
  5.8 23.0 %all-to-all-start = ((f32[32,32,128]{2,1,0:T(8,128)}), f32[32,32,128]{2,1,0:T(8,128)S(1)}, u32[]{:S(2)}, u32[]{:S(2)}) async-start(f32[32,32,128]{2,1,0:T(8,128)} %bitcast.2), calls=%async_computation | async-start | bytes 1048576 | tf_op jit(solution)/shard_map/all_to_all | solution.py:452
  13.1 1.0 copy-start.1
  15.2 51.0 %copy-start = (bf16[64,32,512]{2,1,0:T(8,128)(2,1)}, bf16[64,32,512]{2,1,0:T(8,128)(2,1)S(1)}, u32[]{:S(2)}) copy-start(bf16[64,32,512]{2,1,0:T(8,128)(2,1)S(1)} %shard_map.105.tiles_any.tiles_ref) | copy-start | bytes 6291460
  15.2 39.6 %copy-start.6 = (f32[4096]{0:T(1024)S(1)}, f32[4096]{0:T(1024)}, u32[]{:S(2)}) copy-start(f32[4096]{0:T(1024)} %param.11) | copy-start | bytes 49156
  15.2 39.6 %copy-start.8 = (s32[32]{0:T(128)S(1)}, s32[32]{0:T(128)}, u32[]{:S(2)}) copy-start(s32[32]{0:T(128)} %live_ref.7) | copy-start | bytes 388
  28.7 37.5 %copy-start.2 = (f32[32,32,128]{2,1,0:T(8,128)}, f32[32,32,128]{2,1,0:T(8,128)S(1)}, u32[]{:S(2)}) copy-start(f32[32,32,128]{2,1,0:T(8,128)S(1)} %all-to-all-done) | copy-start | bytes 1572868
  38.0 16.8 %copy-start.12 = (s32[2]{0:T(128)}, s32[2]{0:T(128)S(1)}, u32[]{:S(2)}) copy-start(s32[2]{0:T(128)S(1)} %get-tuple-element.13.size_ref) | copy-start | bytes 28
  38.0 28.2 %copy-start.9 = (s32[288]{0:T(512)}, s32[288]{0:T(512)S(1)}, u32[]{:S(2)}) copy-start(s32[288]{0:T(512)S(1)} %get-tuple-element.12.list_ref) | copy-start | bytes 3460
  161.5 0.8 copy-start.4
  162.3 0.8 copy-start.5

commit v5 on v4

--- a/solution.py
+++ b/solution.py
@@ -19,18 +19,20 @@
 ROW_SHIFT = 115.0
 COL_SHIFT = 110.0
 G = 16
-KEPT = 208
+KEPT_MIDDLE = 176
+KEPT_LAST = 160
 ROWS = 4
 DEPTH = 32
 
+LARGE = 50 * 2**20
 f32 = jnp.float32
 bf16 = jnp.bfloat16
 VMEM = pl.BlockSpec(memory_space=pltpu.VMEM)
-ANY = pl.BlockSpec(memory_space=pl.ANY)
+HBM = pl.BlockSpec(memory_space=pltpu.HBM)
 SMEM = pl.BlockSpec(memory_space=pltpu.SMEM)
 
 
-def call(kernel, out_shape, in_specs, out_specs, scratch, flops, args, limit=67_000_000):
+def call(kernel, out_shape, in_specs, out_specs, scratch, flops, args, limit=LARGE):
     size = sum(a.size * a.dtype.itemsize for a in args)
     return pl.pallas_call(
         kernel,
@@ -106,7 +108,17 @@
     home_scatter(slot_ref, row_ref, send_ref)
 
 
-def home_last_kernel(slot_ref, live_ref, recv_ref, pos_ref, vel_ref, new_pos_ref, new_vel_ref):
+def home_last_kernel(
+    slot_ref, live_ref, recv_ref, pos_hbm, vel_hbm, new_pos_ref, new_vel_ref, pos_ref, vel_ref, sems
+):
+    loads = [
+        pltpu.make_async_copy(pos_hbm, pos_ref, sems.at[0]),
+        pltpu.make_async_copy(vel_hbm, vel_ref, sems.at[1]),
+    ]
+    for load in loads:
+        load.start()
+    for load in loads:
+        load.wait()
     blocks = live_ref.shape[0]
     for b in range(blocks):
         live = live_ref[b]
@@ -195,27 +207,24 @@
 def row_first_kernel(
     capacity,
     recv_ref,
-    tiles_any,
+    tiles_ref,
     pot_ref,
     part_ref,
     list_ref,
     size_ref,
-    tiles_ref,
     beta_ref,
     top_ref,
     left_ref,
     asked_ref,
     tile_ref,
-    sems,
+    sem,
 ):
-    load = pltpu.make_async_copy(tiles_any, tiles_ref, sems.at[0])
-    load.start()
     devices = asked_ref.shape[0]
     lane = lax.broadcasted_iota(jnp.int32, (devices, capacity, BLK), 2)
     rank = lax.broadcasted_iota(jnp.int32, (devices, capacity, BLK), 1)
     asked = recv_ref[...].reshape(devices, ROWS * capacity, BLK)[:, 3 * capacity :, :]
     asked_ref[...] = jnp.sum(jnp.where(lane == rank, asked, 0.0), axis=1).astype(jnp.int32)
-    copy = pltpu.make_async_copy(asked_ref, tile_ref, sems.at[1])
+    copy = pltpu.make_async_copy(asked_ref, tile_ref, sem)
     copy.start()
 
     pot = lanes_of(pot_ref) * SCALE
@@ -245,7 +254,6 @@
             left_ref[k] = particle_rows(recv_ref, (base[k], capacity), ROW_SHIFT, row)
 
     prepare(0)
-    load.wait()
 
     def body(g, carry):
         slot, tile, base = listed(list_ref, g, capacity)
@@ -266,26 +274,19 @@
     store,
     list_ref,
     size_ref,
-    recv_any,
+    recv_ref,
     rows_ref,
-    tiles_any,
+    tiles_ref,
     mass_ref,
-    recv_ref,
-    tiles_ref,
     kept_ref,
     left_ref,
     sums_ref,
     peak_ref,
-    sems,
     weight_ref,
 ):
-    load_recv = pltpu.make_async_copy(recv_any, recv_ref, sems.at[0])
-    load_recv.start()
-    load_tiles = pltpu.make_async_copy(tiles_any, tiles_ref, sems.at[1])
-    load_tiles.start()
     tiles = tiles_ref.shape[0]
     groups, count = size_ref[0], size_ref[1]
-    limit = jnp.minimum(groups, KEPT // G)
+    limit = jnp.minimum(groups, kept_ref.shape[0] // G)
     row = lax.broadcasted_iota(jnp.int32, (8, BLK), 0)
     peak_ref[...] = jnp.full(peak_ref.shape, NEGATIVE, f32)
     sums_ref[...] = jnp.zeros(sums_ref.shape, f32)
@@ -323,9 +324,7 @@
             sums_ref[into] += jnp.sum(power[k].reshape(BLK // 8, 8, TILE), axis=0)
         return carry
 
-    load_recv.wait()
     prepare(0)
-    load_tiles.wait()
     lax.fori_loop(0, limit, functools.partial(first, True), 0)
     lax.fori_loop(limit, groups, functools.partial(first, False), 0)
     total = jnp.sum(sums_ref[0:tiles], axis=1)
@@ -340,9 +339,9 @@
     def second_rest(g, carry):
         slot, tile, base = listed(list_ref, g, capacity)
         prepare(g)
-        power = powers(tile)
-        for k in range(G):
-            store(slot[k], tile[k], power[k], weight_ref)
+        for k in range(G):
+            power = jnp.exp2(product(left_ref[k], tiles_ref[tile[k]]))
+            store(slot[k], tile[k], power, weight_ref)
         return carry
 
     lax.fori_loop(0, limit, second_kept, 0)
@@ -462,7 +461,7 @@
         [pltpu.SMEM((devices,), jnp.int32)],
         10**6,
         (route_owner.T, route_tile.T, live_count, positions),
-        4 * 2**20,
+        67_000_000,
     )
     recv = exchange(send)
     split_tiles = call(
@@ -481,16 +480,15 @@
     part, order, size = call(
         functools.partial(row_first_kernel, capacity),
         (struct((slots, BLK), f32), struct((slots + 2 * G,), jnp.int32), struct((2,), jnp.int32)),
-        [VMEM, ANY, VMEM],
+        [VMEM, VMEM, VMEM],
         (VMEM, SMEM, SMEM),
         [
-            pltpu.VMEM((tiles, DEPTH, TILE), bf16),
             pltpu.VMEM((tiles, TILE), f32),
             pltpu.VMEM((tiles, BLK), f32),
             pltpu.VMEM((G, BLK, DEPTH), bf16),
             pltpu.VMEM((devices, BLK), jnp.int32),
             pltpu.SMEM((devices, BLK), jnp.int32),
-            pltpu.SemaphoreType.DMA((2,)),
+            pltpu.SemaphoreType.DMA,
         ],
         10**9,
         (recv, split_tiles, pot_rows),
@@ -510,22 +508,19 @@
         4 * 2**20,
     )
     rows = exchange(send)
+    keep = [pltpu.VMEM((min(k, slots), BLK, TILE), f32) for k in (KEPT_MIDDLE, KEPT_LAST)]
     scratch = [
-        pltpu.VMEM((slots * ROWS, BLK), f32),
-        pltpu.VMEM((tiles, DEPTH, TILE), bf16),
-        pltpu.VMEM((min(KEPT, slots), BLK, TILE), f32),
         pltpu.VMEM((G, BLK, DEPTH), bf16),
         pltpu.VMEM((tiles + 1, 8, TILE), f32),
         pltpu.VMEM((tiles, BLK), f32),
-        pltpu.SemaphoreType.DMA((2,)),
     ]
     values = pltpu.VMEM((tiles, TILE), f32)
     part = call(
         functools.partial(middle_kernel, capacity),
         struct((slots, BLK), f32),
-        [SMEM, SMEM, ANY, VMEM, ANY, VMEM],
+        [SMEM, SMEM] + [VMEM] * 4,
         VMEM,
-        scratch + [values],
+        keep[:1] + scratch + [values],
         10**9,
         (order, size, recv, rows, split_tiles, sample_rows),
     )
@@ -544,9 +539,9 @@
     part = call(
         functools.partial(last_kernel, capacity),
         struct((slots * ROWS, BLK), f32),
-        [SMEM, SMEM, ANY, VMEM, ANY, VMEM, VMEM],
+        [SMEM, SMEM] + [VMEM] * 5,
         VMEM,
-        scratch + [pltpu.VMEM((tiles, 16, TILE), bf16), values],
+        keep[1:] + scratch + [pltpu.VMEM((tiles, 16, TILE), bf16), values],
         10**9,
         (order, size, recv, rows, split_tiles, sample_rows, samples),
     )
@@ -554,9 +549,13 @@
     return call(
         home_last_kernel,
         (struct(positions.shape, f32), struct(positions.shape, f32)),
-        [SMEM, SMEM, VMEM, VMEM, VMEM],
+        [SMEM, SMEM, VMEM, HBM, HBM],
         (VMEM, VMEM),
-        [],
+        [
+            pltpu.VMEM(positions.shape, f32),
+            pltpu.VMEM(positions.shape, f32),
+            pltpu.SemaphoreType.DMA((2,)),
+        ],
         10**6,
         (slot, live_count, part, positions, velocities),
         4 * 2**20,

time: 163 us -> 158 us (0.969)
  local copies, waits for them, and re-layouts: 5.6 us -> 1.08 us
  Pallas kernels: 45.6 us -> 49.7 us
  blocking collectives: 91.7 us -> 88.7 us
    unnamed x28 -> x18, local copies, waits for them, and re-layouts: 5.6 us -> 1.08 us
    pallas_call x8, Pallas kernels: 45.6 us -> 49.7 us  [call(): pl.pallas_call(kernel, out_shape=out_shape, in_specs=in_specs, out_specs=...]
    all_to_all x5, blocking collectives: 91.7 us -> 88.7 us  [exchange(): lax.all_to_all(values.reshape(devices, rows, BLK), 'dev', split_axis=0, c...]
where the time goes in v5:
time: 158 us; the launch traced here: 161 us
  blocking collectives  88.7 us (56%)
  Pallas kernels  49.7 us (31%)
  waiting for transfers between devices  13.5 us (9%)
  starting transfers between devices  7.33 us (5%)
    all_to_all x5, blocking collectives, exchange(): lax.all_to_all(values.reshape(devices, rows, BLK), 'dev', split_axis=0, c...  88.7 us
    pallas_call x8, Pallas kernels, call(): pl.pallas_call(kernel, out_shape=out_shape, in_specs=in_specs, out_specs=...  49.7 us
    all_to_all x1, waiting for transfers between devices, exchange(): lax.all_to_all(values.reshape(devices, rows, BLK), 'dev', split_axis=0, c...  13.5 us
    all_to_all x1, starting transfers between devices, exchange(): lax.all_to_all(values.reshape(devices, rows, BLK), 'dev', split_axis=0, c...  7.33 us
  transfers between devices with their start and end apart: 1, of which 1 were waited for; matrix products, arithmetic and copies ran while one was open for 0% of the time, Pallas kernels for 1%

profile of v5, /device:TPU:0, one launch (start us, length us, event | category | flops | bytes accessed | tf_op | source)
XLA Modules:
  0.0 161.1 jit_solution(4722728084871004207)
XLA Ops:
  0.6 2.5 %shard_map.104 = (f32[1024,128]{1,0:T(8,128)}, s32[128]{0:T(128)}) custom-call(s32[4,32]{1,0:T(4,128)} %bitcast.36, s32[4,32]{1,0:T(4,128)} %bitcast.37, s32[32]{0:T(128)} %live_ref.7, f32[3,4096]{1,0:T(4,128)} %pos_hbm.1), custom_call_target="tpu_custom_call" | custom-call | flops 1000000 | bytes 50304 | tf_op jit(solution)/shard_map/pallas_call | solution.py:37
  3.1 0.0 copy-start.8
  3.1 7.3 %all-to-all-start = ((f32[32,32,128]{2,1,0:T(8,128)}), f32[32,32,128]{2,1,0:T(8,128)S(1)}, u32[]{:S(2)}, u32[]{:S(2)}) async-start(f32[32,32,128]{2,1,0:T(8,128)} %bitcast.35), calls=%async_computation | async-start | bytes 1048576 | tf_op jit(solution)/shard_map/all_to_all | solution.py:451
  10.5 0.0 copy-start
  10.5 1.0 copy-done
  11.5 1.0 shard_map.105.tiles_ref
  12.5 0.0 copy-start.5
  12.6 0.0 copy-start.6
  12.6 0.0 copy-start.7
  12.6 13.5 %all-to-all-done = f32[32,32,128]{2,1,0:T(8,128)S(1)} async-done(((f32[32,32,128]{2,1,0:T(8,128)}), f32[32,32,128]{2,1,0:T(8,128)S(1)}, u32[]{:S(2)}, u32[]{:S(2)}) %all-to-all-start) | async-done | bytes 524320 | tf_op jit(solution)/shard_map/all_to_all | solution.py:451
  26.1 0.0 copy-done.8
  26.1 0.0 copy-start.3
  26.1 10.9 %shard_map.106 = (f32[256,128]{1,0:T(8,128)S(1)}, s32[288]{0:T(512)S(1)}, s32[2]{0:T(128)S(1)}) custom-call(f32[1024,128]{1,0:T(8,128)S(1)} %bitcast.18, bf16[64,32,512]{2,1,0:T(8,128)(2,1)S(1)} %shard_map.105.tiles_ref, f32[256,128]{1,0:T(8,128)S(1)} %bitcast.34), custom_call_target="tpu_custom_call" | custom-call | flops 1000000000 | bytes 2752512 | tf_op jit(solution)/shard_map/pallas_call | solution.py:37
  37.0 15.0 %all_to_all.30 = f32[32,8,128]{2,1,0:T(8,128)S(1)} all-to-all(f32[32,8,128]{2,1,0:T(8,128)S(1)} %bitcast.26), channel_id=1, replica_groups=mesh['dev'=32] {'dev'}, dimensions={0} | all-to-all | bytes 262144 | tf_op jit(solution)/shard_map/all_to_all | solution.py:451
  52.1 0.0 copy-done.5
  52.1 0.0 copy-done.6
  52.1 0.0 copy-done.7
  52.1 0.8 shard_map.107
  52.9 10.0 %all_to_all.31 = f32[32,8,128]{2,1,0:T(8,128)S(1)} all-to-all(f32[32,8,128]{2,1,0:T(8,128)S(1)} %bitcast.27), channel_id=1, replica_groups=mesh['dev'=32] {'dev'}, dimensions={0} | all-to-all | bytes 262144 | tf_op jit(solution)/shard_map/all_to_all | solution.py:451
  62.9 0.0 copy-done.3
  62.9 0.0 copy-start.1
  62.9 11.4 %shard_map.108 = f32[256,128]{1,0:T(8,128)S(1)} custom-call(s32[288]{0:T(512)S(1)} %get-tuple-element.12.list_ref, s32[2]{0:T(128)S(1)} %get-tuple-element.13.size_ref, f32[1024,128]{1,0:T(8,128)S(1)} %bitcast.19, f32[256,128]{1,0:T(8,128)S(1)} %bitcast.28, bf16[64,32,512]{2,1,0:T(8,128)(2,1)S(1)} %shard_map.105.tiles_ref, f32[256,128]{1,0:T(8,128)S(1)} %bitcast.30), custom_call_target="tpu_custom_call" | custom-call | flops 1000000000 | bytes 2884744 | tf_op jit(solution)/shard_map/pallas_call | solution.py:37
  74.3 18.4 %all_to_all.32 = f32[32,8,128]{2,1,0:T(8,128)S(1)} all-to-all(f32[32,8,128]{2,1,0:T(8,128)S(1)} %bitcast.29), channel_id=1, replica_groups=mesh['dev'=32] {'dev'}, dimensions={0} | all-to-all | bytes 262144 | tf_op jit(solution)/shard_map/all_to_all | solution.py:451
  92.7 1.4 shard_map.109
  94.1 10.0 %all_to_all.33 = f32[32,8,128]{2,1,0:T(8,128)S(1)} all-to-all(f32[32,8,128]{2,1,0:T(8,128)S(1)} %bitcast.25), channel_id=1, replica_groups=mesh['dev'=32] {'dev'}, dimensions={0} | all-to-all | bytes 262144 | tf_op jit(solution)/shard_map/all_to_all | solution.py:451
  104.0 0.0 copy-done.1
  104.0 0.0 copy-start.2
  104.1 20.0 %shard_map.110 = f32[1024,128]{1,0:T(8,128)S(1)} custom-call(s32[288]{0:T(512)S(1)} %get-tuple-element.12.list_ref, s32[2]{0:T(128)S(1)} %get-tuple-element.13.size_ref, f32[1024,128]{1,0:T(8,128)S(1)} %bitcast.20, f32[256,128]{1,0:T(8,128)S(1)} %bitcast.24, bf16[64,32,512]{2,1,0:T(8,128)(2,1)S(1)} %shard_map.105.tiles_ref, f32[256,128]{1,0:T(8,128)S(1)} %bitcast.31, ...), custom_call_target="tpu_custom_call" | custom-call | flops 1000000000 | bytes 3277960 | tf_op jit(solution)/shard_map/pallas_call | solution.py:37
  124.0 35.4 %all_to_all.34 = f32[32,32,128]{2,1,0:T(8,128)S(1)} all-to-all(f32[32,32,128]{2,1,0:T(8,128)S(1)} %bitcast.21), channel_id=1, replica_groups=mesh['dev'=32] {'dev'}, dimensions={0} | all-to-all | bytes 1048576 | tf_op jit(solution)/shard_map/all_to_all | solution.py:451
  159.4 0.0 copy-done.2
  159.4 0.0 copy-done.4
  159.4 1.6 %shard_map.111 = (f32[3,4096]{1,0:T(4,128)}, f32[3,4096]{1,0:T(4,128)}) custom-call(s32[128]{0:T(128)S(1)} %copy-done.7, s32[32]{0:T(128)S(1)} %copy-done.6, f32[1024,128]{1,0:T(8,128)S(1)} %bitcast.17, f32[3,4096]{1,0:T(4,128)S(1)} %copy-done.2, f32[3,4096]{1,0:T(4,128)S(1)} %copy-done.4), custom_call_target="tpu_custom_call" | custom-call | flops 1000000 | bytes 623232 | tf_op jit(solution)/shard_map/pallas_call | solution.py:37
  (1 shorter events, 0.0 us)
Async XLA Ops:
  3.1 23.0 %copy-start.8 = (f32[32768]{0:T(1024)S(1)}, f32[32768]{0:T(1024)}, u32[]{:S(2)}) copy-start(f32[32768]{0:T(1024)} %param.14) | copy-start | bytes 393220
  3.1 23.0 %all-to-all-start = ((f32[32,32,128]{2,1,0:T(8,128)}), f32[32,32,128]{2,1,0:T(8,128)S(1)}, u32[]{:S(2)}, u32[]{:S(2)}) async-start(f32[32,32,128]{2,1,0:T(8,128)} %bitcast.35), calls=%async_computation | async-start | bytes 1048576 | tf_op jit(solution)/shard_map/all_to_all | solution.py:451
  10.5 1.0 copy-start
  12.5 39.5 %copy-start.5 = (f32[4096]{0:T(1024)S(1)}, f32[4096]{0:T(1024)}, u32[]{:S(2)}) copy-start(f32[4096]{0:T(1024)} %param.11) | copy-start | bytes 49156
  12.6 39.5 %copy-start.6 = (s32[32]{0:T(128)S(1)}, s32[32]{0:T(128)}, u32[]{:S(2)}) copy-start(s32[32]{0:T(128)} %live_ref.7) | copy-start | bytes 388
  12.6 39.5 %copy-start.7 = (s32[128]{0:T(128)S(1)}, s32[128]{0:T(128)}, u32[]{:S(2)}) copy-start(s32[128]{0:T(128)} %get-tuple-element.10.slot_ref) | copy-start | bytes 1540
  26.1 36.8 %copy-start.3 = (f32[32768]{0:T(1024)S(1)}, f32[32768]{0:T(1024)}, u32[]{:S(2)}) copy-start(f32[32768]{0:T(1024)} %param.13) | copy-start | bytes 393220
  62.9 41.2 %copy-start.1 = (f32[3,32768]{1,0:T(4,128)S(1)}, f32[3,32768]{1,0:T(4,128)}, u32[]{:S(2)}) copy-start(f32[3,32768]{1,0:T(4,128)} %sample_ref.3) | copy-start | bytes 1179652
  104.0 55.4 %copy-start.2 = (f32[3,4096]{1,0:T(4,128)S(1)}, f32[3,4096]{1,0:T(4,128)}, u32[]{:S(2)}) copy-start(f32[3,4096]{1,0:T(4,128)} %pos_hbm.1) | copy-start | bytes 147460
  104.0 55.4 %copy-start.4 = (f32[3,4096]{1,0:T(4,128)S(1)}, f32[3,4096]{1,0:T(4,128)}, u32[]{:S(2)}) copy-start(f32[3,4096]{1,0:T(4,128)} %vel_hbm.1) | copy-start | bytes 147460

commit v6 on v5

--- a/solution.py
+++ b/solution.py
@@ -19,12 +19,12 @@
 ROW_SHIFT = 115.0
 COL_SHIFT = 110.0
 G = 16
-KEPT_MIDDLE = 176
-KEPT_LAST = 160
+KEPT = 144
+HALVES = 2
 ROWS = 4
 DEPTH = 32
 
-LARGE = 50 * 2**20
+LARGE = 44 * 2**20
 f32 = jnp.float32
 bf16 = jnp.bfloat16
 VMEM = pl.BlockSpec(memory_space=pltpu.VMEM)
@@ -199,8 +199,12 @@
     return slot, code & 0xFFFF, slot + device * (capacity * (ROWS - 1))
 
 
-def listed(list_ref, g, capacity):
-    slots = [unpack(list_ref, g * G + k, capacity) for k in range(G)]
+def part_start(h, slots):
+    return h * (slots + 2 * G)
+
+
+def listed(list_ref, start, capacity):
+    slots = [unpack(list_ref, start + k, capacity) for k in range(G)]
     return [list(item) for item in zip(*slots)]
 
 
@@ -234,38 +238,55 @@
     row = lax.broadcasted_iota(jnp.int32, (8, BLK), 0)
     copy.wait()
 
-    def compact(device, count):
+    slots = devices * capacity
+    half = tiles_ref.shape[0] // HALVES
+
+    def compact(device, counts):
         for k in range(capacity):
             tile = tile_ref[device, k]
-            list_ref[count] = ((device * capacity + k) << 16) + jnp.maximum(tile, 0)
-            count = count + jnp.where(tile >= 0, 1, 0)
-        return count
-
-    count = lax.fori_loop(0, devices, compact, 0)
-    groups = (count + G - 1) // G
-    size_ref[0] = groups
-    size_ref[1] = count
-    for k in range(G):
-        list_ref[count + k] = list_ref[0]
-
-    def prepare(g):
-        slot, tile, base = listed(list_ref, g, capacity)
+            upper = tile >= half
+            place = jnp.where(upper, part_start(1, slots) + counts[1], counts[0])
+            list_ref[place] = ((device * capacity + k) << 16) + jnp.maximum(tile, 0)
+            low = jnp.where((tile >= 0) & (tile < half), 1, 0)
+            counts = (counts[0] + low, counts[1] + jnp.where(upper, 1, 0))
+        return counts
+
+    zero = jnp.int32(0)
+    counts = lax.fori_loop(0, devices, compact, (zero, zero))
+    for h in range(HALVES):
+        size_ref[h] = counts[h]
+        start = part_start(h, slots)
+        list_ref[start + counts[h]] = 0
         for k in range(G):
-            left_ref[k] = particle_rows(recv_ref, (base[k], capacity), ROW_SHIFT, row)
-
-    prepare(0)
-
-    def body(g, carry):
-        slot, tile, base = listed(list_ref, g, capacity)
-        raised = [product(left_ref[k], tiles_ref[tile[k]]) for k in range(G)]
-        power = [jnp.exp2(a + beta_ref[pl.ds(t, 1), :]) for a, t in zip(raised, tile)]
-        prepare(jnp.minimum(g + 1, groups - 1))
-        total = [jnp.sum(fold_lanes(a).T, axis=0, keepdims=True) for a in power]
-        for k in range(G):
-            part_ref[pl.ds(slot[k], 1), :] = jnp.log2(total[k]) + top_ref[pl.ds(tile[k], 1), :]
-        return carry
-
-    lax.fori_loop(0, groups, body, 0)
+            list_ref[start + counts[h] + k] = list_ref[start]
+
+    def run(h):
+        start = part_start(h, slots)
+        groups = (counts[h] + G - 1) // G
+
+        def prepare(g):
+            slot, tile, base = listed(list_ref, start + g * G, capacity)
+            for k in range(G):
+                left_ref[k] = particle_rows(recv_ref, (base[k], capacity), ROW_SHIFT, row)
+
+        prepare(0)
+
+        def body(g, carry):
+            slot, tile, base = listed(list_ref, start + g * G, capacity)
+            raised = [product(left_ref[k], tiles_ref[tile[k]]) for k in range(G)]
+            power = [jnp.exp2(a + beta_ref[pl.ds(t, 1), :]) for a, t in zip(raised, tile)]
+            prepare(jnp.minimum(g + 1, groups - 1))
+            total = [jnp.sum(fold_lanes(a).T, axis=0, keepdims=True) for a in power]
+            for k in range(G):
+                part_ref[pl.ds(slot[k], 1), :] = (
+                    jnp.log2(total[k]) + top_ref[pl.ds(tile[k], 1), :]
+                )
+            return carry
+
+        lax.fori_loop(0, groups, body, 0)
+
+    for h in range(HALVES):
+        run(h)
 
 
 def iterate(
@@ -285,74 +306,85 @@
     weight_ref,
 ):
     tiles = tiles_ref.shape[0]
-    groups, count = size_ref[0], size_ref[1]
-    limit = jnp.minimum(groups, kept_ref.shape[0] // G)
+    slots = rows_ref.shape[0]
+    half = tiles // HALVES
     row = lax.broadcasted_iota(jnp.int32, (8, BLK), 0)
     peak_ref[...] = jnp.full(peak_ref.shape, NEGATIVE, f32)
     sums_ref[...] = jnp.zeros(sums_ref.shape, f32)
-
-    def find(g, carry):
-        slot, tile, base = listed(list_ref, g, capacity)
-        for k in range(G):
-            at = pl.ds(tile[k], 1)
-            peak_ref[at, :] = jnp.maximum(peak_ref[at, :], rows_ref[pl.ds(slot[k], 1), :])
-        return carry
-
-    lax.fori_loop(0, groups, find, 0)
+    mass = lanes_of(mass_ref)
+
+    for h in range(HALVES):
+
+        def find(g, carry, start=part_start(h, slots)):
+            slot, tile, base = listed(list_ref, start + g * G, capacity)
+            for k in range(G):
+                at = pl.ds(tile[k], 1)
+                peak_ref[at, :] = jnp.maximum(peak_ref[at, :], rows_ref[pl.ds(slot[k], 1), :])
+            return carry
+
+        lax.fori_loop(0, (size_ref[h] + G - 1) // G, find, 0)
     peak = jnp.max(peak_ref[...], axis=1, keepdims=True)
     peak_ref[...] = jnp.broadcast_to(COL_SHIFT - peak, peak_ref.shape)
 
-    def prepare(g):
-        slot, tile, base = listed(list_ref, g, capacity)
-        for k in range(G):
-            extra = rows_ref[pl.ds(slot[k], 1), :] + peak_ref[pl.ds(tile[k], 1), :]
-            extra = jnp.broadcast_to(extra, (8, BLK))
-            left_ref[k] = particle_rows(recv_ref, (base[k], capacity), extra, row)
-
-    def powers(tile):
-        raised = [product(left_ref[k], tiles_ref[tile[k]]) for k in range(G)]
-        return [jnp.exp2(a) for a in raised]
-
-    def first(keep, g, carry):
-        slot, tile, base = listed(list_ref, g, capacity)
-        power = powers(tile)
-        prepare(jnp.minimum(g + 1, groups - 1))
-        for k in range(G):
-            if keep:
-                kept_ref[g * G + k] = power[k]
-            into = jnp.where(g * G + k < count, tile[k], tiles)
-            sums_ref[into] += jnp.sum(power[k].reshape(BLK // 8, 8, TILE), axis=0)
-        return carry
-
-    prepare(0)
-    lax.fori_loop(0, limit, functools.partial(first, True), 0)
-    lax.fori_loop(limit, groups, functools.partial(first, False), 0)
-    total = jnp.sum(sums_ref[0:tiles], axis=1)
-    weights(lanes_of(mass_ref) / total, weight_ref)
-
-    def second_kept(g, carry):
-        slot, tile, base = listed(list_ref, g, capacity)
-        for k in range(G):
-            store(slot[k], tile[k], kept_ref[g * G + k], weight_ref)
-        return carry
-
-    def second_rest(g, carry):
-        slot, tile, base = listed(list_ref, g, capacity)
-        prepare(g)
-        for k in range(G):
-            power = jnp.exp2(product(left_ref[k], tiles_ref[tile[k]]))
-            store(slot[k], tile[k], power, weight_ref)
-        return carry
-
-    lax.fori_loop(0, limit, second_kept, 0)
-    lax.fori_loop(limit, groups, second_rest, 0)
+    def part(h):
+        start = part_start(h, slots)
+        count = size_ref[h]
+        groups = (count + G - 1) // G
+        limit = jnp.minimum(groups, kept_ref.shape[0] // G)
+
+        def prepare(g):
+            slot, tile, base = listed(list_ref, start + g * G, capacity)
+            for k in range(G):
+                extra = rows_ref[pl.ds(slot[k], 1), :] + peak_ref[pl.ds(tile[k], 1), :]
+                extra = jnp.broadcast_to(extra, (8, BLK))
+                left_ref[k] = particle_rows(recv_ref, (base[k], capacity), extra, row)
+
+        def power(k, tile):
+            return jnp.exp2(product(left_ref[k], tiles_ref[tile[k]]))
+
+        def first(keep, g, carry):
+            slot, tile, base = listed(list_ref, start + g * G, capacity)
+            raised = [power(k, tile) for k in range(G)]
+            prepare(jnp.minimum(g + 1, groups - 1))
+            for k in range(G):
+                if keep:
+                    kept_ref[g * G + k] = raised[k]
+                into = jnp.where(g * G + k < count, tile[k], tiles)
+                sums_ref[into] += jnp.sum(raised[k].reshape(BLK // 8, 8, TILE), axis=0)
+            return carry
+
+        prepare(0)
+        lax.fori_loop(0, limit, functools.partial(first, True), 0)
+        lax.fori_loop(limit, groups, functools.partial(first, False), 0)
+        here = slice(h * half, (h + 1) * half)
+        total = jnp.sum(sums_ref[here], axis=1)
+        weights(h * half, mass[here] / total, weight_ref)
+
+        def second_kept(g, carry):
+            slot, tile, base = listed(list_ref, start + g * G, capacity)
+            for k in range(G):
+                store(slot[k], tile[k], kept_ref[g * G + k], weight_ref)
+            return carry
+
+        def second_rest(g, carry):
+            slot, tile, base = listed(list_ref, start + g * G, capacity)
+            prepare(g)
+            for k in range(G):
+                store(slot[k], tile[k], power(k, tile), weight_ref)
+            return carry
+
+        lax.fori_loop(0, limit, second_kept, 0)
+        lax.fori_loop(limit, groups, second_rest, 0)
+
+    for h in range(HALVES):
+        part(h)
 
 
 def middle_kernel(
     capacity, list_ref, size_ref, recv_ref, rows_ref, tiles_ref, mass_ref, part_ref, *scratch
 ):
-    def weights(value, weight_ref):
-        weight_ref[...] = value
+    def weights(start, value, weight_ref):
+        weight_ref[start : start + value.shape[0], :] = value
 
     def store(slot, tile, power, weight_ref):
         power = power * weight_ref[pl.ds(tile, 1), :]
@@ -387,8 +419,8 @@
     *scratch, value_ref = scratch
     row = lax.broadcasted_iota(jnp.int32, (8, TILE), 0)
 
-    def weights(value, weight_ref):
-        value_ref[...] = value
+    def weights(start, value, weight_ref):
+        value_ref[start : start + value.shape[0], :] = value
 
         def body(t, carry):
             where = pl.ds(pl.multiple_of(t * TILE, TILE), TILE)
@@ -402,7 +434,7 @@
             weight_ref[t] = jnp.concatenate([upper, lower], 0).astype(bf16)
             return carry
 
-        lax.fori_loop(0, value_ref.shape[0], body, 0, unroll=4)
+        lax.fori_loop(start, start + value.shape[0], body, 0, unroll=4)
 
     def store(slot, tile, power, weight_ref):
         left = weight_ref[tile]
@@ -479,7 +511,7 @@
     pot_rows = start_potential.reshape(tiles * CHUNKS, BLK)
     part, order, size = call(
         functools.partial(row_first_kernel, capacity),
-        (struct((slots, BLK), f32), struct((slots + 2 * G,), jnp.int32), struct((2,), jnp.int32)),
+        (struct((slots, BLK), f32), struct((HALVES * (slots + 2 * G),), jnp.int32), struct((HALVES,), jnp.int32)),
         [VMEM, VMEM, VMEM],
         (VMEM, SMEM, SMEM),
         [
@@ -508,8 +540,8 @@
         4 * 2**20,
     )
     rows = exchange(send)
-    keep = [pltpu.VMEM((min(k, slots), BLK, TILE), f32) for k in (KEPT_MIDDLE, KEPT_LAST)]
     scratch = [
+        pltpu.VMEM((min(KEPT, slots), BLK, TILE), f32),
         pltpu.VMEM((G, BLK, DEPTH), bf16),
         pltpu.VMEM((tiles + 1, 8, TILE), f32),
         pltpu.VMEM((tiles, BLK), f32),
@@ -520,7 +552,7 @@
         struct((slots, BLK), f32),
         [SMEM, SMEM] + [VMEM] * 4,
         VMEM,
-        keep[:1] + scratch + [values],
+        scratch + [values],
         10**9,
         (order, size, recv, rows, split_tiles, sample_rows),
     )
@@ -541,7 +573,7 @@
         struct((slots * ROWS, BLK), f32),
         [SMEM, SMEM] + [VMEM] * 5,
         VMEM,
-        keep[1:] + scratch + [pltpu.VMEM((tiles, 16, TILE), bf16), values],
+        scratch + [pltpu.VMEM((tiles, 16, TILE), bf16), values],
         10**9,
         (order, size, recv, rows, split_tiles, sample_rows, samples),
     )

time: 158 us -> 155 us (0.981); the launches traced: 161 us -> 154 us
  Pallas kernels: 49.7 us -> 35 us
  blocking collectives: 88.7 us -> 96.6 us
    pallas_call x8, Pallas kernels: 49.7 us -> 35 us  [call(): pl.pallas_call(kernel, out_shape=out_shape, in_specs=in_specs, out_specs=...]
    all_to_all x5, blocking collectives: 88.7 us -> 96.6 us  [exchange(): lax.all_to_all(values.reshape(devices, rows, BLK), 'dev', split_axis=0, c...]
where the time goes in v6:
time: 155 us; the launch traced here: 154 us
  blocking collectives  96.6 us (62%)
  Pallas kernels  35 us (23%)
  waiting for transfers between devices  13.5 us (9%)
  starting transfers between devices  7.33 us (5%)
    all_to_all x5, blocking collectives, exchange(): lax.all_to_all(values.reshape(devices, rows, BLK), 'dev', split_axis=0, c...  96.6 us
    pallas_call x8, Pallas kernels, call(): pl.pallas_call(kernel, out_shape=out_shape, in_specs=in_specs, out_specs=...  35 us
    all_to_all x1, waiting for transfers between devices, exchange(): lax.all_to_all(values.reshape(devices, rows, BLK), 'dev', split_axis=0, c...  13.5 us
    all_to_all x1, starting transfers between devices, exchange(): lax.all_to_all(values.reshape(devices, rows, BLK), 'dev', split_axis=0, c...  7.33 us
  transfers between devices with their start and end apart: 1, of which 1 were waited for; matrix products, arithmetic and copies ran while one was open for 0% of the time, Pallas kernels for 1%

profile of v6, /device:TPU:0, one launch (start us, length us, event | category | flops | bytes accessed | tf_op | source)
XLA Modules:
  0.0 154.5 jit_solution(5195784834096756993)
XLA Ops:
  0.6 2.5 %shard_map.104 = (f32[1024,128]{1,0:T(8,128)}, s32[128]{0:T(128)}) custom-call(s32[4,32]{1,0:T(4,128)} %bitcast.36, s32[4,32]{1,0:T(4,128)} %bitcast.37, s32[32]{0:T(128)} %live_ref.7, f32[3,4096]{1,0:T(4,128)} %pos_hbm.1), custom_call_target="tpu_custom_call" | custom-call | flops 1000000 | bytes 50304 | tf_op jit(solution)/shard_map/pallas_call | solution.py:37
  3.1 0.0 copy-start.8
  3.1 7.3 %all-to-all-start = ((f32[32,32,128]{2,1,0:T(8,128)}), f32[32,32,128]{2,1,0:T(8,128)S(1)}, u32[]{:S(2)}, u32[]{:S(2)}) async-start(f32[32,32,128]{2,1,0:T(8,128)} %bitcast.35), calls=%async_computation | async-start | bytes 1048576 | tf_op jit(solution)/shard_map/all_to_all | solution.py:483
  10.5 0.0 copy-start
  10.5 1.0 copy-done
  11.5 1.0 shard_map.105.tiles_ref
  12.5 0.0 copy-start.5
  12.6 0.0 copy-start.6
  12.6 0.0 copy-start.7
  12.6 13.5 %all-to-all-done = f32[32,32,128]{2,1,0:T(8,128)S(1)} async-done(((f32[32,32,128]{2,1,0:T(8,128)}), f32[32,32,128]{2,1,0:T(8,128)S(1)}, u32[]{:S(2)}, u32[]{:S(2)}) %all-to-all-start) | async-done | bytes 524320 | tf_op jit(solution)/shard_map/all_to_all | solution.py:483
  26.1 0.0 copy-done.8
  26.1 0.0 copy-start.3
  26.1 8.1 %shard_map.106 = (f32[256,128]{1,0:T(8,128)S(1)}, s32[576]{0:T(1024)S(1)}, s32[2]{0:T(128)S(1)}) custom-call(f32[1024,128]{1,0:T(8,128)S(1)} %bitcast.17, bf16[64,32,512]{2,1,0:T(8,128)(2,1)S(1)} %shard_map.105.tiles_ref, f32[256,128]{1,0:T(8,128)S(1)} %bitcast.34), custom_call_target="tpu_custom_call" | custom-call | flops 1000000000 | bytes 2752512 | tf_op jit(solution)/shard_map/pallas_call | solution.py:37
  34.2 18.4 %all_to_all.30 = f32[32,8,128]{2,1,0:T(8,128)S(1)} all-to-all(f32[32,8,128]{2,1,0:T(8,128)S(1)} %bitcast.28), channel_id=1, replica_groups=mesh['dev'=32] {'dev'}, dimensions={0} | all-to-all | bytes 262144 | tf_op jit(solution)/shard_map/all_to_all | solution.py:483
  52.7 0.0 copy-done.5
  52.7 0.0 copy-done.6
  52.7 0.0 copy-done.7
  52.7 0.8 shard_map.107
  53.5 10.0 %all_to_all.31 = f32[32,8,128]{2,1,0:T(8,128)S(1)} all-to-all(f32[32,8,128]{2,1,0:T(8,128)S(1)} %bitcast.29), channel_id=1, replica_groups=mesh['dev'=32] {'dev'}, dimensions={0} | all-to-all | bytes 262144 | tf_op jit(solution)/shard_map/all_to_all | solution.py:483
  63.5 0.0 copy-done.3
  63.5 0.0 copy-start.1
  63.5 7.2 %shard_map.108 = f32[256,128]{1,0:T(8,128)S(1)} custom-call(s32[576]{0:T(1024)S(1)} %get-tuple-element.12.list_ref, s32[2]{0:T(128)S(1)} %get-tuple-element.13.size_ref, f32[1024,128]{1,0:T(8,128)S(1)} %bitcast.18, f32[256,128]{1,0:T(8,128)S(1)} %bitcast.30, bf16[64,32,512]{2,1,0:T(8,128)(2,1)S(1)} %shard_map.105.tiles_ref, f32[256,128]{1,0:T(8,128)S(1)} %bitcast.25), custom_call_target="tpu_custom_call" | custom-call | flops 1000000000 | bytes 2885896 | tf_op jit(solution)/shard_map/pallas_call | solution.py:37
  70.6 21.1 %all_to_all.32 = f32[32,8,128]{2,1,0:T(8,128)S(1)} all-to-all(f32[32,8,128]{2,1,0:T(8,128)S(1)} %bitcast.31), channel_id=1, replica_groups=mesh['dev'=32] {'dev'}, dimensions={0} | all-to-all | bytes 262144 | tf_op jit(solution)/shard_map/all_to_all | solution.py:483
  91.7 1.4 shard_map.109
  93.1 10.0 %all_to_all.33 = f32[32,8,128]{2,1,0:T(8,128)S(1)} all-to-all(f32[32,8,128]{2,1,0:T(8,128)S(1)} %bitcast.27), channel_id=1, replica_groups=mesh['dev'=32] {'dev'}, dimensions={0} | all-to-all | bytes 262144 | tf_op jit(solution)/shard_map/all_to_all | solution.py:483
  103.1 0.0 copy-done.1
  103.1 0.0 copy-start.2
  103.1 12.4 %shard_map.110 = f32[1024,128]{1,0:T(8,128)S(1)} custom-call(s32[576]{0:T(1024)S(1)} %get-tuple-element.12.list_ref, s32[2]{0:T(128)S(1)} %get-tuple-element.13.size_ref, f32[1024,128]{1,0:T(8,128)S(1)} %bitcast.19, f32[256,128]{1,0:T(8,128)S(1)} %bitcast.22, bf16[64,32,512]{2,1,0:T(8,128)(2,1)S(1)} %shard_map.105.tiles_ref, f32[256,128]{1,0:T(8,128)S(1)} %bitcast.26, ...), custom_call_target="tpu_custom_call" | custom-call | flops 1000000000 | bytes 3279112 | tf_op jit(solution)/shard_map/pallas_call | solution.py:37
  115.5 37.2 %all_to_all.34 = f32[32,32,128]{2,1,0:T(8,128)S(1)} all-to-all(f32[32,32,128]{2,1,0:T(8,128)S(1)} %bitcast.20), channel_id=1, replica_groups=mesh['dev'=32] {'dev'}, dimensions={0} | all-to-all | bytes 1048576 | tf_op jit(solution)/shard_map/all_to_all | solution.py:483
  152.7 0.0 copy-done.2
  152.7 0.0 copy-done.4
  152.7 1.6 %shard_map.111 = (f32[3,4096]{1,0:T(4,128)}, f32[3,4096]{1,0:T(4,128)}) custom-call(s32[128]{0:T(128)S(1)} %copy-done.7, s32[32]{0:T(128)S(1)} %copy-done.6, f32[1024,128]{1,0:T(8,128)S(1)} %bitcast.21, f32[3,4096]{1,0:T(4,128)S(1)} %copy-done.2, f32[3,4096]{1,0:T(4,128)S(1)} %copy-done.4), custom_call_target="tpu_custom_call" | custom-call | flops 1000000 | bytes 623232 | tf_op jit(solution)/shard_map/pallas_call | solution.py:37
  (1 shorter events, 0.0 us)
Async XLA Ops:
  3.1 23.0 %copy-start.8 = (f32[32768]{0:T(1024)S(1)}, f32[32768]{0:T(1024)}, u32[]{:S(2)}) copy-start(f32[32768]{0:T(1024)} %param.14) | copy-start | bytes 393220
  3.1 23.0 %all-to-all-start = ((f32[32,32,128]{2,1,0:T(8,128)}), f32[32,32,128]{2,1,0:T(8,128)S(1)}, u32[]{:S(2)}, u32[]{:S(2)}) async-start(f32[32,32,128]{2,1,0:T(8,128)} %bitcast.35), calls=%async_computation | async-start | bytes 1048576 | tf_op jit(solution)/shard_map/all_to_all | solution.py:483
  10.5 1.0 copy-start
  12.5 40.1 %copy-start.5 = (f32[4096]{0:T(1024)S(1)}, f32[4096]{0:T(1024)}, u32[]{:S(2)}) copy-start(f32[4096]{0:T(1024)} %param.11) | copy-start | bytes 49156
  12.6 40.1 %copy-start.6 = (s32[32]{0:T(128)S(1)}, s32[32]{0:T(128)}, u32[]{:S(2)}) copy-start(s32[32]{0:T(128)} %live_ref.7) | copy-start | bytes 388
  12.6 40.1 %copy-start.7 = (s32[128]{0:T(128)S(1)}, s32[128]{0:T(128)}, u32[]{:S(2)}) copy-start(s32[128]{0:T(128)} %get-tuple-element.10.slot_ref) | copy-start | bytes 1540
  26.1 37.3 %copy-start.3 = (f32[32768]{0:T(1024)S(1)}, f32[32768]{0:T(1024)}, u32[]{:S(2)}) copy-start(f32[32768]{0:T(1024)} %param.13) | copy-start | bytes 393220
  63.5 39.6 %copy-start.1 = (f32[3,32768]{1,0:T(4,128)S(1)}, f32[3,32768]{1,0:T(4,128)}, u32[]{:S(2)}) copy-start(f32[3,32768]{1,0:T(4,128)} %sample_ref.3) | copy-start | bytes 1179652
  103.1 49.6 %copy-start.2 = (f32[3,4096]{1,0:T(4,128)S(1)}, f32[3,4096]{1,0:T(4,128)}, u32[]{:S(2)}) copy-start(f32[3,4096]{1,0:T(4,128)} %pos_hbm.1) | copy-start | bytes 147460
  103.1 49.6 %copy-start.4 = (f32[3,4096]{1,0:T(4,128)S(1)}, f32[3,4096]{1,0:T(4,128)}, u32[]{:S(2)}) copy-start(f32[3,4096]{1,0:T(4,128)} %vel_hbm.1) | copy-start | bytes 147460

commit v7 on v6

--- a/solution.py
+++ b/solution.py
@@ -28,7 +28,6 @@
 f32 = jnp.float32
 bf16 = jnp.bfloat16
 VMEM = pl.BlockSpec(memory_space=pltpu.VMEM)
-HBM = pl.BlockSpec(memory_space=pltpu.HBM)
 SMEM = pl.BlockSpec(memory_space=pltpu.SMEM)
 
 
@@ -108,17 +107,7 @@
     home_scatter(slot_ref, row_ref, send_ref)
 
 
-def home_last_kernel(
-    slot_ref, live_ref, recv_ref, pos_hbm, vel_hbm, new_pos_ref, new_vel_ref, pos_ref, vel_ref, sems
-):
-    loads = [
-        pltpu.make_async_copy(pos_hbm, pos_ref, sems.at[0]),
-        pltpu.make_async_copy(vel_hbm, vel_ref, sems.at[1]),
-    ]
-    for load in loads:
-        load.start()
-    for load in loads:
-        load.wait()
+def home_last_kernel(slot_ref, live_ref, recv_ref, pos_ref, vel_ref, new_pos_ref, new_vel_ref):
     blocks = live_ref.shape[0]
     for b in range(blocks):
         live = live_ref[b]
@@ -221,6 +210,7 @@
     left_ref,
     asked_ref,
     tile_ref,
+    all_ref,
     sem,
 ):
     devices = asked_ref.shape[0]
@@ -245,8 +235,10 @@
         for k in range(capacity):
             tile = tile_ref[device, k]
             upper = tile >= half
+            code = ((device * capacity + k) << 16) + jnp.maximum(tile, 0)
+            all_ref[counts[0] + counts[1]] = code
             place = jnp.where(upper, part_start(1, slots) + counts[1], counts[0])
-            list_ref[place] = ((device * capacity + k) << 16) + jnp.maximum(tile, 0)
+            list_ref[place] = code
             low = jnp.where((tile >= 0) & (tile < half), 1, 0)
             counts = (counts[0] + low, counts[1] + jnp.where(upper, 1, 0))
         return counts
@@ -260,33 +252,30 @@
         for k in range(G):
             list_ref[start + counts[h] + k] = list_ref[start]
 
-    def run(h):
-        start = part_start(h, slots)
-        groups = (counts[h] + G - 1) // G
-
-        def prepare(g):
-            slot, tile, base = listed(list_ref, start + g * G, capacity)
-            for k in range(G):
-                left_ref[k] = particle_rows(recv_ref, (base[k], capacity), ROW_SHIFT, row)
-
-        prepare(0)
-
-        def body(g, carry):
-            slot, tile, base = listed(list_ref, start + g * G, capacity)
-            raised = [product(left_ref[k], tiles_ref[tile[k]]) for k in range(G)]
-            power = [jnp.exp2(a + beta_ref[pl.ds(t, 1), :]) for a, t in zip(raised, tile)]
-            prepare(jnp.minimum(g + 1, groups - 1))
-            total = [jnp.sum(fold_lanes(a).T, axis=0, keepdims=True) for a in power]
-            for k in range(G):
-                part_ref[pl.ds(slot[k], 1), :] = (
-                    jnp.log2(total[k]) + top_ref[pl.ds(tile[k], 1), :]
-                )
-            return carry
-
-        lax.fori_loop(0, groups, body, 0)
-
-    for h in range(HALVES):
-        run(h)
+    count = counts[0] + counts[1]
+    groups = (count + G - 1) // G
+    all_ref[count] = 0
+    for k in range(G):
+        all_ref[count + k] = all_ref[0]
+
+    def prepare(g):
+        slot, tile, base = listed(all_ref, g * G, capacity)
+        for k in range(G):
+            left_ref[k] = particle_rows(recv_ref, (base[k], capacity), ROW_SHIFT, row)
+
+    prepare(0)
+
+    def body(g, carry):
+        slot, tile, base = listed(all_ref, g * G, capacity)
+        raised = [product(left_ref[k], tiles_ref[tile[k]]) for k in range(G)]
+        power = [jnp.exp2(a + beta_ref[pl.ds(t, 1), :]) for a, t in zip(raised, tile)]
+        prepare(jnp.minimum(g + 1, groups - 1))
+        total = [jnp.sum(fold_lanes(a).T, axis=0, keepdims=True) for a in power]
+        for k in range(G):
+            part_ref[pl.ds(slot[k], 1), :] = jnp.log2(total[k]) + top_ref[pl.ds(tile[k], 1), :]
+        return carry
+
+    lax.fori_loop(0, groups, body, 0)
 
 
 def iterate(
@@ -520,6 +509,7 @@
             pltpu.VMEM((G, BLK, DEPTH), bf16),
             pltpu.VMEM((devices, BLK), jnp.int32),
             pltpu.SMEM((devices, BLK), jnp.int32),
+            pltpu.SMEM((slots + 2 * G,), jnp.int32),
             pltpu.SemaphoreType.DMA,
         ],
         10**9,
@@ -528,10 +518,9 @@
     )
     part = exchange(part)
     row_scratch = [pltpu.VMEM((K, blocks, BLK), f32)]
-    row_out = (struct((slots, BLK), f32), struct((blocks, BLK), f32))
     send, row = call(
         home_first_kernel,
-        row_out,
+        (struct((slots, BLK), f32), struct((blocks, BLK), f32)),
         [SMEM, SMEM, VMEM, VMEM],
         (VMEM, VMEM),
         row_scratch,
@@ -557,12 +546,12 @@
         (order, size, recv, rows, split_tiles, sample_rows),
     )
     part = exchange(part)
-    send, row = call(
+    send = call(
         home_next_kernel,
-        row_out,
+        struct((slots, BLK), f32),
         [SMEM, SMEM, VMEM, VMEM, VMEM],
-        (VMEM, VMEM),
-        row_scratch,
+        VMEM,
+        [pltpu.VMEM((blocks, BLK), f32)] + row_scratch,
         10**6,
         (slot, live_count, part, mass_rows, row),
         4 * 2**20,
@@ -581,13 +570,9 @@
     return call(
         home_last_kernel,
         (struct(positions.shape, f32), struct(positions.shape, f32)),
-        [SMEM, SMEM, VMEM, HBM, HBM],
+        [SMEM, SMEM, VMEM, VMEM, VMEM],
         (VMEM, VMEM),
-        [
-            pltpu.VMEM(positions.shape, f32),
-            pltpu.VMEM(positions.shape, f32),
-            pltpu.SemaphoreType.DMA((2,)),
-        ],
+        [],
         10**6,
         (slot, live_count, part, positions, velocities),
         4 * 2**20,

time: 155 us -> 154 us (level)
  Pallas kernels: 35 us -> 33.4 us
    pallas_call x8, Pallas kernels: 35 us -> 33.4 us  [call(): pl.pallas_call(kernel, out_shape=out_shape, in_specs=in_specs, out_specs=...]
where the time goes in v7:
time: 154 us; the launch traced here: 153 us
  blocking collectives  97.3 us (63%)
  Pallas kernels  33.4 us (22%)
  waiting for transfers between devices  13.5 us (9%)
  starting transfers between devices  7.33 us (5%)
    all_to_all x5, blocking collectives, exchange(): lax.all_to_all(values.reshape(devices, rows, BLK), 'dev', split_axis=0, c...  97.3 us
    pallas_call x8, Pallas kernels, call(): pl.pallas_call(kernel, out_shape=out_shape, in_specs=in_specs, out_specs=...  33.4 us
    all_to_all x1, waiting for transfers between devices, exchange(): lax.all_to_all(values.reshape(devices, rows, BLK), 'dev', split_axis=0, c...  13.5 us
    all_to_all x1, starting transfers between devices, exchange(): lax.all_to_all(values.reshape(devices, rows, BLK), 'dev', split_axis=0, c...  7.33 us
  transfers between devices with their start and end apart: 1, of which 1 were waited for; matrix products, arithmetic and copies ran while one was open for 0% of the time, Pallas kernels for 1%

profile of v7, /device:TPU:0, one launch (start us, length us, event | category | flops | bytes accessed | tf_op | source)
XLA Modules:
  0.0 153.3 jit_solution(6977838963582211468)
XLA Ops:
  0.6 2.5 %shard_map.104 = (f32[1024,128]{1,0:T(8,128)}, s32[128]{0:T(128)}) custom-call(s32[4,32]{1,0:T(4,128)} %bitcast.36, s32[4,32]{1,0:T(4,128)} %bitcast.37, s32[32]{0:T(128)} %live_ref.7, f32[3,4096]{1,0:T(4,128)} %pos_ref.3), custom_call_target="tpu_custom_call" | custom-call | flops 1000000 | bytes 50304 | tf_op jit(solution)/shard_map/pallas_call | solution.py:36
  3.1 0.0 copy-start.8
  3.2 7.3 %all-to-all-start = ((f32[32,32,128]{2,1,0:T(8,128)}), f32[32,32,128]{2,1,0:T(8,128)S(1)}, u32[]{:S(2)}, u32[]{:S(2)}) async-start(f32[32,32,128]{2,1,0:T(8,128)} %bitcast.35), calls=%async_computation | async-start | bytes 1048576 | tf_op jit(solution)/shard_map/all_to_all | solution.py:472
  10.5 0.0 copy-start
  10.5 1.0 copy-done
  11.5 1.0 shard_map.105.tiles_ref
  12.5 0.0 copy-start.5
  12.6 0.0 copy-start.6
  12.6 0.0 copy-start.7
  12.6 13.5 %all-to-all-done = f32[32,32,128]{2,1,0:T(8,128)S(1)} async-done(((f32[32,32,128]{2,1,0:T(8,128)}), f32[32,32,128]{2,1,0:T(8,128)S(1)}, u32[]{:S(2)}, u32[]{:S(2)}) %all-to-all-start) | async-done | bytes 524320 | tf_op jit(solution)/shard_map/all_to_all | solution.py:472
  26.1 0.0 copy-done.8
  26.1 0.0 copy-start.3
  26.1 7.2 %shard_map.106 = (f32[256,128]{1,0:T(8,128)S(1)}, s32[576]{0:T(1024)S(1)}, s32[2]{0:T(128)S(1)}) custom-call(f32[1024,128]{1,0:T(8,128)S(1)} %bitcast.17, bf16[64,32,512]{2,1,0:T(8,128)(2,1)S(1)} %shard_map.105.tiles_ref, f32[256,128]{1,0:T(8,128)S(1)} %bitcast.34), custom_call_target="tpu_custom_call" | custom-call | flops 1000000000 | bytes 2752512 | tf_op jit(solution)/shard_map/pallas_call | solution.py:36
  33.3 19.4 %all_to_all.30 = f32[32,8,128]{2,1,0:T(8,128)S(1)} all-to-all(f32[32,8,128]{2,1,0:T(8,128)S(1)} %bitcast.28), channel_id=1, replica_groups=mesh['dev'=32] {'dev'}, dimensions={0} | all-to-all | bytes 262144 | tf_op jit(solution)/shard_map/all_to_all | solution.py:472
  52.7 0.0 copy-done.5
  52.7 0.0 copy-done.6
  52.7 0.0 copy-done.7
  52.7 0.8 shard_map.107
  53.5 10.0 %all_to_all.31 = f32[32,8,128]{2,1,0:T(8,128)S(1)} all-to-all(f32[32,8,128]{2,1,0:T(8,128)S(1)} %bitcast.29), channel_id=1, replica_groups=mesh['dev'=32] {'dev'}, dimensions={0} | all-to-all | bytes 262144 | tf_op jit(solution)/shard_map/all_to_all | solution.py:472
  63.5 0.0 copy-done.3
  63.5 0.0 copy-start.1
  63.5 7.2 %shard_map.108 = f32[256,128]{1,0:T(8,128)S(1)} custom-call(s32[576]{0:T(1024)S(1)} %get-tuple-element.11.list_ref, s32[2]{0:T(128)S(1)} %get-tuple-element.12.size_ref, f32[1024,128]{1,0:T(8,128)S(1)} %bitcast.18, f32[256,128]{1,0:T(8,128)S(1)} %bitcast.30, bf16[64,32,512]{2,1,0:T(8,128)(2,1)S(1)} %shard_map.105.tiles_ref, f32[256,128]{1,0:T(8,128)S(1)} %bitcast.26), custom_call_target="tpu_custom_call" | custom-call | flops 1000000000 | bytes 2885896 | tf_op jit(solution)/shard_map/pallas_call | solution.py:36
  70.7 20.9 %all_to_all.32 = f32[32,8,128]{2,1,0:T(8,128)S(1)} all-to-all(f32[32,8,128]{2,1,0:T(8,128)S(1)} %bitcast.31), channel_id=1, replica_groups=mesh['dev'=32] {'dev'}, dimensions={0} | all-to-all | bytes 262144 | tf_op jit(solution)/shard_map/all_to_all | solution.py:472
  91.6 0.8 shard_map.109
  92.4 10.0 %all_to_all.33 = f32[32,8,128]{2,1,0:T(8,128)S(1)} all-to-all(f32[32,8,128]{2,1,0:T(8,128)S(1)} %bitcast.25), channel_id=1, replica_groups=mesh['dev'=32] {'dev'}, dimensions={0} | all-to-all | bytes 262144 | tf_op jit(solution)/shard_map/all_to_all | solution.py:472
  102.3 0.0 copy-done.1
  102.3 0.0 copy-start.2
  102.4 12.4 %shard_map.110 = f32[1024,128]{1,0:T(8,128)S(1)} custom-call(s32[576]{0:T(1024)S(1)} %get-tuple-element.11.list_ref, s32[2]{0:T(128)S(1)} %get-tuple-element.12.size_ref, f32[1024,128]{1,0:T(8,128)S(1)} %bitcast.19, f32[256,128]{1,0:T(8,128)S(1)} %bitcast.22, bf16[64,32,512]{2,1,0:T(8,128)(2,1)S(1)} %shard_map.105.tiles_ref, f32[256,128]{1,0:T(8,128)S(1)} %bitcast.27, ...), custom_call_target="tpu_custom_call" | custom-call | flops 1000000000 | bytes 3279112 | tf_op jit(solution)/shard_map/pallas_call | solution.py:36
  114.8 37.1 %all_to_all.34 = f32[32,32,128]{2,1,0:T(8,128)S(1)} all-to-all(f32[32,32,128]{2,1,0:T(8,128)S(1)} %bitcast.20), channel_id=1, replica_groups=mesh['dev'=32] {'dev'}, dimensions={0} | all-to-all | bytes 1048576 | tf_op jit(solution)/shard_map/all_to_all | solution.py:472
  151.8 0.0 copy-done.2
  151.8 0.0 copy-done.4
  151.8 1.4 shard_map.111
  (1 shorter events, 0.0 us)
Async XLA Ops:
  3.1 23.0 %copy-start.8 = (f32[32768]{0:T(1024)S(1)}, f32[32768]{0:T(1024)}, u32[]{:S(2)}) copy-start(f32[32768]{0:T(1024)} %param.14) | copy-start | bytes 393220
  3.2 23.0 %all-to-all-start = ((f32[32,32,128]{2,1,0:T(8,128)}), f32[32,32,128]{2,1,0:T(8,128)S(1)}, u32[]{:S(2)}, u32[]{:S(2)}) async-start(f32[32,32,128]{2,1,0:T(8,128)} %bitcast.35), calls=%async_computation | async-start | bytes 1048576 | tf_op jit(solution)/shard_map/all_to_all | solution.py:472
  10.5 1.0 copy-start
  12.5 40.1 %copy-start.5 = (f32[4096]{0:T(1024)S(1)}, f32[4096]{0:T(1024)}, u32[]{:S(2)}) copy-start(f32[4096]{0:T(1024)} %param.11) | copy-start | bytes 49156
  12.6 40.1 %copy-start.6 = (s32[32]{0:T(128)S(1)}, s32[32]{0:T(128)}, u32[]{:S(2)}) copy-start(s32[32]{0:T(128)} %live_ref.7) | copy-start | bytes 388
  12.6 40.1 %copy-start.7 = (s32[128]{0:T(128)S(1)}, s32[128]{0:T(128)}, u32[]{:S(2)}) copy-start(s32[128]{0:T(128)} %get-tuple-element.9.slot_ref) | copy-start | bytes 1540
  26.1 37.4 %copy-start.3 = (f32[32768]{0:T(1024)S(1)}, f32[32768]{0:T(1024)}, u32[]{:S(2)}) copy-start(f32[32768]{0:T(1024)} %param.13) | copy-start | bytes 393220
  63.5 38.9 %copy-start.1 = (f32[3,32768]{1,0:T(4,128)S(1)}, f32[3,32768]{1,0:T(4,128)}, u32[]{:S(2)}) copy-start(f32[3,32768]{1,0:T(4,128)} %sample_ref.3) | copy-start | bytes 1179652
  102.3 49.5 %copy-start.2 = (f32[3,4096]{1,0:T(4,128)S(1)}, f32[3,4096]{1,0:T(4,128)}, u32[]{:S(2)}) copy-start(f32[3,4096]{1,0:T(4,128)} %pos_ref.3) | copy-start | bytes 147460
  102.4 49.5 %copy-start.4 = (f32[3,4096]{1,0:T(4,128)S(1)}, f32[3,4096]{1,0:T(4,128)}, u32[]{:S(2)}) copy-start(f32[3,4096]{1,0:T(4,128)} %vel_ref.1) | copy-start | bytes 147460

commit v8 on v7

--- a/solution.py
+++ b/solution.py
@@ -23,6 +23,7 @@
 HALVES = 2
 ROWS = 4
 DEPTH = 32
+PACK = BLK // DEPTH
 
 LARGE = 44 * 2**20
 f32 = jnp.float32
@@ -123,27 +124,40 @@
         new_pos_ref[:, where] = here + TIMESTEP * velocity
 
 
-def sample_kernel(sample_ref, tiles_ref):
-    tiles = tiles_ref.shape[0]
+def sample_rows(sample_ref, t, extra, row):
+    where = pl.ds(pl.multiple_of(t * TILE, TILE), TILE)
+    parts = [jnp.broadcast_to(sample_ref[d : d + 1, where], (8, TILE)) - 0.5 for d in range(3)]
+    square = parts[0] * parts[0] + parts[1] * parts[1] + parts[2] * parts[2]
+    value = (-0.5 * SCALE) * square
+    if extra is not None:
+        value = value + extra
+    for d in range(3):
+        value = jnp.where((row == d) | (row == d + 5), parts[d], value)
+    high, middle, low = split3(value)
+    one = row == 3
+    first = jnp.where(one, 1.0, jnp.where(row > 4, middle, high))
+    second = jnp.where(one, 1.0, jnp.where(row > 4, low, middle))
+    third = jnp.where(one, 1.0, jnp.where(row == 4, low, high))
+    return jnp.concatenate([first, second, third, jnp.zeros_like(first)], 0)
+
+
+def sample_kernel(sample_ref, pot_ref, tiles_ref, turned_ref, top_ref, beta_ref):
     row = lax.broadcasted_iota(jnp.int32, (8, TILE), 0)
-
-    def body(t, carry):
-        where = pl.ds(pl.multiple_of(t * TILE, TILE), TILE)
-        parts = [jnp.broadcast_to(sample_ref[d : d + 1, where], (8, TILE)) - 0.5 for d in range(3)]
-        square = parts[0] * parts[0] + parts[1] * parts[1] + parts[2] * parts[2]
-        value = (-0.5 * SCALE) * square
-        for d in range(3):
-            value = jnp.where((row == d) | (row == d + 5), parts[d], value)
-        high, middle, low = split3(value)
-        one = row == 3
-        first = jnp.where(one, 1.0, jnp.where(row > 4, middle, high))
-        second = jnp.where(one, 1.0, jnp.where(row > 4, low, middle))
-        third = jnp.where(one, 1.0, jnp.where(row == 4, low, high))
-        zero = jnp.zeros_like(first)
-        tiles_ref[t] = jnp.concatenate([first, second, third, zero], 0).astype(bf16)
+    pot = lanes_of(pot_ref) * SCALE
+    top = jnp.max(pot, axis=1, keepdims=True)
+    beta_ref[...] = pot - top
+    top_ref[...] = jnp.broadcast_to(top - ROW_SHIFT, top_ref.shape)
+
+    def body(q, carry):
+        sides = []
+        for i in range(PACK):
+            t = q * PACK + i
+            tiles_ref[t] = sample_rows(sample_ref, t, None, row).astype(bf16)
+            sides.append(sample_rows(sample_ref, t, beta_ref[pl.ds(t, 1), :], row))
+        turned_ref[q] = jnp.concatenate(sides, 0).astype(bf16).T
         return carry
 
-    lax.fori_loop(0, tiles, body, 0, unroll=4)
+    lax.fori_loop(0, turned_ref.shape[0], body, 0)
 
 
 def lanes_of(ref):
@@ -167,7 +181,7 @@
     second = jnp.where(one, 1.0, jnp.where(row == 3, middle, high))
     third = jnp.where(one, 1.0, jnp.where(row < 3, middle, low))
     zero = jnp.zeros_like(first)
-    return jnp.concatenate([first, second, third, zero], 0).astype(bf16).T
+    return jnp.concatenate([first, second, third, zero], 0).astype(bf16)
 
 
 def fold_lanes(value):
@@ -200,14 +214,12 @@
 def row_first_kernel(
     capacity,
     recv_ref,
-    tiles_ref,
-    pot_ref,
+    turned_ref,
+    top_ref,
     part_ref,
     list_ref,
     size_ref,
-    beta_ref,
-    top_ref,
-    left_ref,
+    right_ref,
     asked_ref,
     tile_ref,
     all_ref,
@@ -221,15 +233,11 @@
     copy = pltpu.make_async_copy(asked_ref, tile_ref, sem)
     copy.start()
 
-    pot = lanes_of(pot_ref) * SCALE
-    top = jnp.max(pot, axis=1, keepdims=True)
-    beta_ref[...] = pot - top
-    top_ref[...] = jnp.broadcast_to(top - ROW_SHIFT, top_ref.shape)
     row = lax.broadcasted_iota(jnp.int32, (8, BLK), 0)
     copy.wait()
 
     slots = devices * capacity
-    half = tiles_ref.shape[0] // HALVES
+    half = top_ref.shape[0] // HALVES
 
     def compact(device, counts):
         for k in range(capacity):
@@ -261,18 +269,20 @@
     def prepare(g):
         slot, tile, base = listed(all_ref, g * G, capacity)
         for k in range(G):
-            left_ref[k] = particle_rows(recv_ref, (base[k], capacity), ROW_SHIFT, row)
+            side = particle_rows(recv_ref, (base[k], capacity), ROW_SHIFT, row)
+            at = tile[k] % PACK
+            sides = [jnp.where(at == i, side, jnp.zeros_like(side)) for i in range(PACK)]
+            right_ref[k] = jnp.concatenate(sides, 0)
 
     prepare(0)
 
     def body(g, carry):
         slot, tile, base = listed(all_ref, g * G, capacity)
-        raised = [product(left_ref[k], tiles_ref[tile[k]]) for k in range(G)]
-        power = [jnp.exp2(a + beta_ref[pl.ds(t, 1), :]) for a, t in zip(raised, tile)]
+        power = [jnp.exp2(product(turned_ref[tile[k] // PACK], right_ref[k])) for k in range(G)]
         prepare(jnp.minimum(g + 1, groups - 1))
-        total = [jnp.sum(fold_lanes(a).T, axis=0, keepdims=True) for a in power]
         for k in range(G):
-            part_ref[pl.ds(slot[k], 1), :] = jnp.log2(total[k]) + top_ref[pl.ds(tile[k], 1), :]
+            total = jnp.sum(jnp.sum(power[k].reshape(TILE // 8, 8, BLK), axis=0), axis=0)
+            part_ref[pl.ds(slot[k], 1), :] = jnp.log2(total[None]) + top_ref[pl.ds(tile[k], 1), :]
         return carry
 
     lax.fori_loop(0, groups, body, 0)
@@ -326,7 +336,7 @@
             for k in range(G):
                 extra = rows_ref[pl.ds(slot[k], 1), :] + peak_ref[pl.ds(tile[k], 1), :]
                 extra = jnp.broadcast_to(extra, (8, BLK))
-                left_ref[k] = particle_rows(recv_ref, (base[k], capacity), extra, row)
+                left_ref[k] = particle_rows(recv_ref, (base[k], capacity), extra, row).T
 
         def power(k, tile):
             return jnp.exp2(product(left_ref[k], tiles_ref[tile[k]]))
@@ -485,36 +495,38 @@
         67_000_000,
     )
     recv = exchange(send)
-    split_tiles = call(
+    pot_rows = start_potential.reshape(tiles * CHUNKS, BLK)
+    split_tiles, turned, top = call(
         sample_kernel,
-        struct((tiles, DEPTH, TILE), bf16),
-        [VMEM],
-        VMEM,
-        [],
+        (
+            struct((tiles, DEPTH, TILE), bf16),
+            struct((tiles // PACK, TILE, BLK), bf16),
+            struct((tiles, BLK), f32),
+        ),
+        [VMEM, VMEM],
+        (VMEM, VMEM, VMEM),
+        [pltpu.VMEM((tiles, TILE), f32)],
         10**7,
-        (samples,),
-        8 * 2**20,
+        (samples, pot_rows),
+        10 * 2**20,
     )
     mass_rows = masses.reshape(blocks, BLK)
-    sample_rows = sample_mass.reshape(tiles * CHUNKS, BLK)
-    pot_rows = start_potential.reshape(tiles * CHUNKS, BLK)
+    weight_rows = sample_mass.reshape(tiles * CHUNKS, BLK)
     part, order, size = call(
         functools.partial(row_first_kernel, capacity),
         (struct((slots, BLK), f32), struct((HALVES * (slots + 2 * G),), jnp.int32), struct((HALVES,), jnp.int32)),
         [VMEM, VMEM, VMEM],
         (VMEM, SMEM, SMEM),
         [
-            pltpu.VMEM((tiles, TILE), f32),
-            pltpu.VMEM((tiles, BLK), f32),
-            pltpu.VMEM((G, BLK, DEPTH), bf16),
+            pltpu.VMEM((G, BLK, BLK), bf16),
             pltpu.VMEM((devices, BLK), jnp.int32),
             pltpu.SMEM((devices, BLK), jnp.int32),
             pltpu.SMEM((slots + 2 * G,), jnp.int32),
             pltpu.SemaphoreType.DMA,
         ],
         10**9,
-        (recv, split_tiles, pot_rows),
-        16 * 2**20,
+        (recv, turned, top),
+        8 * 2**20,
     )
     part = exchange(part)
     row_scratch = [pltpu.VMEM((K, blocks, BLK), f32)]
@@ -543,7 +555,7 @@
         VMEM,
         scratch + [values],
         10**9,
-        (order, size, recv, rows, split_tiles, sample_rows),
+        (order, size, recv, rows, split_tiles, weight_rows),
     )
     part = exchange(part)
     send = call(
@@ -564,7 +576,7 @@
         VMEM,
         scratch + [pltpu.VMEM((tiles, 16, TILE), bf16), values],
         10**9,
-        (order, size, recv, rows, split_tiles, sample_rows, samples),
+        (order, size, recv, rows, split_tiles, weight_rows, samples),
     )
     part = exchange(part)
     return call(

time: 154 us -> 152 us (0.987); the launches traced: 153 us -> 149 us
  waiting for transfers between devices: 13.5 us -> 9.56 us
  local copies, waits for them, and re-layouts: 1.08 us -> 4.88 us
  Pallas kernels: 33.4 us -> 31.2 us
  blocking collectives: 97.3 us -> 95.4 us
    all_to_all x1, waiting for transfers between devices: 13.5 us -> 9.56 us  [exchange(): lax.all_to_all(values.reshape(devices, rows, BLK), 'dev', split_axis=0, c...]
    unnamed x18 -> x22, local copies, waits for them, and re-layouts: 1.08 us -> 4.88 us
    pallas_call x8, Pallas kernels: 33.4 us -> 31.2 us  [call(): pl.pallas_call(kernel, out_shape=out_shape, in_specs=in_specs, out_specs=...]
    all_to_all x5, blocking collectives: 97.3 us -> 95.4 us  [exchange(): lax.all_to_all(values.reshape(devices, rows, BLK), 'dev', split_axis=0, c...]
  transfers between devices with their start and end apart: 1 -> 1, of which waited for: 1 -> 1; matrix products, arithmetic and copies ran while one was open for 0% -> 0% of each run, Pallas kernels for 1% -> 2%
where the time goes in v8:
time: 152 us; the launch traced here: 149 us
  blocking collectives  95.4 us (63%)
  Pallas kernels  31.2 us (21%)
  waiting for transfers between devices  9.56 us (6%)
  starting transfers between devices  7.33 us (5%)
  local copies, waits for them, and re-layouts  4.88 us (3%)
    all_to_all x5, blocking collectives, exchange(): lax.all_to_all(values.reshape(devices, rows, BLK), 'dev', split_axis=0, c...  95.4 us
    pallas_call x8, Pallas kernels, call(): pl.pallas_call(kernel, out_shape=out_shape, in_specs=in_specs, out_specs=...  31.2 us
    all_to_all x1, waiting for transfers between devices, exchange(): lax.all_to_all(values.reshape(devices, rows, BLK), 'dev', split_axis=0, c...  9.56 us
    all_to_all x1, starting transfers between devices, exchange(): lax.all_to_all(values.reshape(devices, rows, BLK), 'dev', split_axis=0, c...  7.33 us
    unnamed x22, local copies, waits for them, and re-layouts  4.88 us
  transfers between devices with their start and end apart: 1, of which 1 were waited for; matrix products, arithmetic and copies ran while one was open for 0% of the time, Pallas kernels for 2%

profile of v8, /device:TPU:0, one launch (start us, length us, event | category | flops | bytes accessed | tf_op | source)
XLA Modules:
  0.0 149.1 jit_solution(14761211593457997008)
XLA Ops:
  0.6 2.5 %shard_map.104 = (f32[1024,128]{1,0:T(8,128)}, s32[128]{0:T(128)}) custom-call(s32[4,32]{1,0:T(4,128)} %bitcast.36, s32[4,32]{1,0:T(4,128)} %bitcast.37, s32[32]{0:T(128)} %live_ref.7, f32[3,4096]{1,0:T(4,128)} %pos_ref.3), custom_call_target="tpu_custom_call" | custom-call | flops 1000000 | bytes 50304 | tf_op jit(solution)/shard_map/pallas_call | solution.py:37
  3.2 7.3 %all-to-all-start = ((f32[32,32,128]{2,1,0:T(8,128)}), f32[32,32,128]{2,1,0:T(8,128)S(1)}, u32[]{:S(2)}, u32[]{:S(2)}) async-start(f32[32,32,128]{2,1,0:T(8,128)} %bitcast.35), calls=%async_computation | async-start | bytes 1048576 | tf_op jit(solution)/shard_map/all_to_all | solution.py:482
  10.5 0.0 copy-start
  10.5 1.0 copy-done
  11.6 0.9 copy-done.3
  12.5 2.8 %shard_map.105 = (bf16[64,32,512]{2,1,0:T(8,128)(2,1)S(1)}, bf16[16,512,128]{2,1,0:T(8,128)(2,1)S(1)}, f32[64,128]{1,0:T(8,128)S(1)}) custom-call(f32[3,32768]{1,0:T(4,128)S(1)} %copy-done, f32[256,128]{1,0:T(8,128)S(1)} %bitcast.26), custom_call_target="tpu_custom_call" | custom-call | flops 10000000 | bytes 524288 | tf_op jit(solution)/shard_map/pallas_call | solution.py:37
  15.2 0.0 copy-start.9
  15.2 1.3 copy-done.9
  16.5 0.0 copy-start.6
  16.5 0.0 copy-start.7
  16.6 0.0 copy-start.8
  16.6 9.6 %all-to-all-done = f32[32,32,128]{2,1,0:T(8,128)S(1)} async-done(((f32[32,32,128]{2,1,0:T(8,128)}), f32[32,32,128]{2,1,0:T(8,128)S(1)}, u32[]{:S(2)}, u32[]{:S(2)}) %all-to-all-start) | async-done | bytes 524320 | tf_op jit(solution)/shard_map/all_to_all | solution.py:482
  26.1 0.0 copy-start.10
  26.1 1.6 %copy-done.10 = bf16[16,512,128]{2,1,0:T(8,128)(2,1)S(1)} copy-done((bf16[16,512,128]{2,1,0:T(8,128)(2,1)S(1)}, bf16[16,512,128]{2,1,0:T(8,128)(2,1)}, u32[]{:S(2)}) %copy-start.10) | copy-done | bytes 2097176
  27.7 6.5 %shard_map.106 = (f32[256,128]{1,0:T(8,128)S(1)}, s32[576]{0:T(1024)S(1)}, s32[2]{0:T(128)S(1)}) custom-call(f32[1024,128]{1,0:T(8,128)S(1)} %bitcast.17, bf16[16,512,128]{2,1,0:T(8,128)(2,1)S(1)} %copy-done.10, f32[64,128]{1,0:T(8,128)S(1)} %get-tuple-element.15.top_ref), custom_call_target="tpu_custom_call" | custom-call | flops 1000000000 | bytes 2654208 | tf_op jit(solution)/shard_map/pallas_call | solution.py:37
  34.2 17.1 %all_to_all.30 = f32[32,8,128]{2,1,0:T(8,128)S(1)} all-to-all(f32[32,8,128]{2,1,0:T(8,128)S(1)} %bitcast.29), channel_id=1, replica_groups=mesh['dev'=32] {'dev'}, dimensions={0} | all-to-all | bytes 262144 | tf_op jit(solution)/shard_map/all_to_all | solution.py:482
  51.3 0.0 copy-done.6
  51.3 0.0 copy-done.7
  51.3 0.0 copy-done.8
  51.3 0.8 shard_map.107
  52.1 10.0 %all_to_all.31 = f32[32,8,128]{2,1,0:T(8,128)S(1)} all-to-all(f32[32,8,128]{2,1,0:T(8,128)S(1)} %bitcast.30), channel_id=1, replica_groups=mesh['dev'=32] {'dev'}, dimensions={0} | all-to-all | bytes 262144 | tf_op jit(solution)/shard_map/all_to_all | solution.py:482
  62.1 0.0 copy-done.4
  62.1 6.0 %shard_map.108 = f32[256,128]{1,0:T(8,128)S(1)} custom-call(s32[576]{0:T(1024)S(1)} %get-tuple-element.16.list_ref, s32[2]{0:T(128)S(1)} %get-tuple-element.17.size_ref, f32[1024,128]{1,0:T(8,128)S(1)} %bitcast.18, f32[256,128]{1,0:T(8,128)S(1)} %bitcast.31, bf16[64,32,512]{2,1,0:T(8,128)(2,1)S(1)} %get-tuple-element.20.tiles_ref, f32[256,128]{1,0:T(8,128)S(1)} %bitcast.27), custom_call_target="tpu_custom_call" | custom-call | flops 1000000000 | bytes 2885896 | tf_op jit(solution)/shard_map/pallas_call | solution.py:37
  68.1 20.9 %all_to_all.32 = f32[32,8,128]{2,1,0:T(8,128)S(1)} all-to-all(f32[32,8,128]{2,1,0:T(8,128)S(1)} %bitcast.32), channel_id=1, replica_groups=mesh['dev'=32] {'dev'}, dimensions={0} | all-to-all | bytes 262144 | tf_op jit(solution)/shard_map/all_to_all | solution.py:482
  89.1 0.8 shard_map.109
  89.9 10.0 %all_to_all.33 = f32[32,8,128]{2,1,0:T(8,128)S(1)} all-to-all(f32[32,8,128]{2,1,0:T(8,128)S(1)} %bitcast.25), channel_id=1, replica_groups=mesh['dev'=32] {'dev'}, dimensions={0} | all-to-all | bytes 262144 | tf_op jit(solution)/shard_map/all_to_all | solution.py:482
  99.8 0.0 copy-done.1
  99.8 10.4 %shard_map.110 = f32[1024,128]{1,0:T(8,128)S(1)} custom-call(s32[576]{0:T(1024)S(1)} %get-tuple-element.16.list_ref, s32[2]{0:T(128)S(1)} %get-tuple-element.17.size_ref, f32[1024,128]{1,0:T(8,128)S(1)} %bitcast.19, f32[256,128]{1,0:T(8,128)S(1)} %bitcast.22, bf16[64,32,512]{2,1,0:T(8,128)(2,1)S(1)} %get-tuple-element.20.tiles_ref, f32[256,128]{1,0:T(8,128)S(1)} %bitcast.28, ...), custom_call_target="tpu_custom_call" | custom-call | flops 1000000000 | bytes 3279112 | tf_op jit(solution)/shard_map/pallas_call | solution.py:37
  110.2 37.4 %all_to_all.34 = f32[32,32,128]{2,1,0:T(8,128)S(1)} all-to-all(f32[32,32,128]{2,1,0:T(8,128)S(1)} %bitcast.20), channel_id=1, replica_groups=mesh['dev'=32] {'dev'}, dimensions={0} | all-to-all | bytes 1048576 | tf_op jit(solution)/shard_map/all_to_all | solution.py:482
  147.6 0.0 copy-done.2
  147.6 0.0 copy-done.5
  147.7 1.4 shard_map.111
  (5 shorter events, 0.0 us)
Async XLA Ops:
  3.2 23.0 %all-to-all-start = ((f32[32,32,128]{2,1,0:T(8,128)}), f32[32,32,128]{2,1,0:T(8,128)S(1)}, u32[]{:S(2)}, u32[]{:S(2)}) async-start(f32[32,32,128]{2,1,0:T(8,128)} %bitcast.35), calls=%async_computation | async-start | bytes 1048576 | tf_op jit(solution)/shard_map/all_to_all | solution.py:482
  10.5 1.0 copy-start
  11.5 0.9 copy-start.3
  15.2 1.3 copy-start.9
  16.5 34.8 %copy-start.6 = (f32[4096]{0:T(1024)S(1)}, f32[4096]{0:T(1024)}, u32[]{:S(2)}) copy-start(f32[4096]{0:T(1024)} %param.11) | copy-start | bytes 49156
  16.5 34.8 %copy-start.7 = (s32[32]{0:T(128)S(1)}, s32[32]{0:T(128)}, u32[]{:S(2)}) copy-start(s32[32]{0:T(128)} %live_ref.7) | copy-start | bytes 388
  16.6 34.8 %copy-start.8 = (s32[128]{0:T(128)S(1)}, s32[128]{0:T(128)}, u32[]{:S(2)}) copy-start(s32[128]{0:T(128)} %get-tuple-element.12.slot_ref) | copy-start | bytes 1540
  26.1 1.6 %copy-start.10 = (bf16[16,512,128]{2,1,0:T(8,128)(2,1)S(1)}, bf16[16,512,128]{2,1,0:T(8,128)(2,1)}, u32[]{:S(2)}) copy-start(bf16[16,512,128]{2,1,0:T(8,128)(2,1)} %copy-done.9) | copy-start | bytes 6291460
  27.7 34.4 %copy-start.4 = (f32[32768]{0:T(1024)S(1)}, f32[32768]{0:T(1024)}, u32[]{:S(2)}) copy-start(f32[32768]{0:T(1024)} %param.13) | copy-start | bytes 393220
  62.1 37.7 %copy-start.1 = (f32[3,32768]{1,0:T(4,128)S(1)}, f32[3,32768]{1,0:T(4,128)}, u32[]{:S(2)}) copy-start(f32[3,32768]{1,0:T(4,128)} %sample_ref.3) | copy-start | bytes 1179652
  99.8 47.8 %copy-start.2 = (f32[3,4096]{1,0:T(4,128)S(1)}, f32[3,4096]{1,0:T(4,128)}, u32[]{:S(2)}) copy-start(f32[3,4096]{1,0:T(4,128)} %pos_ref.3) | copy-start | bytes 147460
  99.8 47.8 %copy-start.5 = (f32[3,4096]{1,0:T(4,128)S(1)}, f32[3,4096]{1,0:T(4,128)}, u32[]{:S(2)}) copy-start(f32[3,4096]{1,0:T(4,128)} %vel_ref.1) | copy-start | bytes 147460
